TPU v7x, 128 devices: a whole 4x4x4 slice. The times are simulated.
128 devices in a mesh: member: 8 (over z, core), band: 16 (over x, y).
Axes of the slice: x: 4, y: 4, z: 4, core: 2. Of those that a mesh axis runs over, the one named last changes fastest.
Arguments:
- latent: bfloat16 [8, 4096, 1024], P('member', 'band'), may hold values from -6 to 6
- observed: bfloat16 [4096, 128], P('band'), may hold values from -6 to 6
- area_weight: float32 [4096], P('band'), may hold values from 0.3 to 25, as said below
- band_counts: int32 [16], replicated, may hold values from 128 to 256, as said below
- gain_attn: float32 [1024], replicated, may hold values from 0.25 to 1.75
- w_query: bfloat16 [1024, 1024], replicated, may hold values from -0.1875 to 0.1875
- w_key: bfloat16 [1024, 1024], replicated, may hold values from -0.1875 to 0.1875
- w_value: bfloat16 [1024, 1024], replicated, may hold values from -0.1875 to 0.1875
- w_out: bfloat16 [1024, 1024], replicated, may hold values from -1.5 to 1.5
- gain_head: float32 [1024], replicated, may hold values from 0.25 to 1.75
- w_head: bfloat16 [1024, 128], replicated, may hold values from -0.1875 to 0.1875
Outputs:
- grad_latent: bfloat16 [8, 4096, 1024], P('member', 'band')
- grad_head: float32 [1024, 128], P('band')
- ensemble_loss: float32 [], replicated
Inputs may be any that keep to these rules, and one draw needn't show every extreme that they name: Band b holds band_counts[b] live grid points in its first slots; the remaining of its 256 slots are padding. In every draw some band holds exactly 256 and another exactly 128. `area_weight`: positive area weights.
All inputs are finite; a program needn't handle non-finite values.
Results may differ from a plain program's by a relative error of at most 0.019.
Values may be sent and summed in bfloat16 or wider, within the bound.
No kernel may reach another device: no remote copies, remote signals or barrier semaphores. Data moves between devices by JAX's collectives and lax.ppermute only.
A program may use at most 192 MiB of HBM per device.

v0:
```python
import math

import jax
import jax.numpy as jnp
from jax import lax
from jax.sharding import PartitionSpec as P

HEADS = 16
CH = 128
R = 512
HOPS = 4


NORM_EPS = 1e-06
SMOOTH_WIDTH = 0.25
FAIR_ALPHA = 0.95
heads_per_group = 4


def from_behind(value, axis, steps):
    count = lax.axis_size(axis)
    leading, last = (max(0, -steps), min(count, count - steps))
    return lax.ppermute(value, axis, [(source, source + steps) for source in range(leading, last)])


def inverse_rms(values):
    return lax.rsqrt(jnp.mean(values * values, axis=-1, keepdims=True) + NORM_EPS)


def norm_backward(values, gain_vec, inverse, upstream):
    scaled = upstream * gain_vec
    return inverse * scaled - values * inverse**3 * jnp.mean(
        values * scaled, axis=-1, keepdims=True
    )


def times_transposed(left_side, scaling_coefficient):
    return lax.dot_general(
        left_side,
        scaling_coefficient,
        (((left_side.ndim - 1,), (1,)), ((), ())),
        preferred_element_type=jnp.float32,
    )


def window_probs(query_group, key_group, allowed):
    head_size = query_group.shape[-1]
    scores = jnp.einsum(
        "mqgd,mkgd->mgqk", query_group, key_group, preferred_element_type=jnp.float32
    ) * (1.0 / math.sqrt(head_size))
    exponent = jnp.where(allowed[None, None], jnp.exp(scores), 0.0)
    return exponent / jnp.sum(exponent, axis=-1, keepdims=True)


def split_group(array_in, first_col, group_width, head_size):
    part_cols = lax.dynamic_slice_in_dim(array_in, first_col, group_width, 2)
    return part_cols.reshape(array_in.shape[0], array_in.shape[1], heads_per_group, head_size)


def attention_forward(queries, key_rows, value_rows, allowed):
    number_of_realizations, row_count, model_width = queries.shape
    head_size = model_width // HEADS
    group_width = heads_per_group * head_size

    def one_group(group_index, output):
        first_col = (group_index * group_width).astype(jnp.int32)
        query_group = split_group(queries, first_col, group_width, head_size)
        key_group = split_group(key_rows, first_col, group_width, head_size)
        value_group = split_group(value_rows, first_col, group_width, head_size)
        soft_b = window_probs(query_group, key_group, allowed).astype(jnp.bfloat16)
        mixed_group = jnp.einsum(
            "mgqk,mkgd->mqgd", soft_b, value_group, preferred_element_type=jnp.float32
        )
        mixed_group = mixed_group.reshape(number_of_realizations, row_count, group_width).astype(
            jnp.bfloat16
        )
        return lax.dynamic_update_slice_in_dim(output, mixed_group, first_col, 2)

    return lax.fori_loop(
        0, model_width // group_width, one_group, jnp.zeros(queries.shape, jnp.bfloat16)
    )


def attention_backward(queries, key_rows, value_rows, allowed, grad_mixed):
    number_of_realizations, row_count, model_width = queries.shape
    key_count = key_rows.shape[1]
    head_size = model_width // HEADS
    group_width = heads_per_group * head_size
    score_scale = 1.0 / math.sqrt(head_size)

    def one_group(group_index, carried):
        grad_query, grad_key, grad_value = carried
        first_col = (group_index * group_width).astype(jnp.int32)
        query_group = split_group(queries, first_col, group_width, head_size)
        key_group = split_group(key_rows, first_col, group_width, head_size)
        value_group = split_group(value_rows, first_col, group_width, head_size)
        upstream_group = split_group(grad_mixed, first_col, group_width, head_size)
        soft = window_probs(query_group, key_group, allowed)
        soft_b = soft.astype(jnp.bfloat16)
        d_soft = jnp.einsum(
            "mqgd,mkgd->mgqk", upstream_group, value_group, preferred_element_type=jnp.float32
        )
        inner_sum = jnp.sum(soft * d_soft, axis=-1, keepdims=True)
        d_score = (soft * (d_soft - inner_sum) * score_scale).astype(jnp.bfloat16)
        query_part = jnp.einsum(
            "mgqk,mkgd->mqgd", d_score, key_group, preferred_element_type=jnp.float32
        )
        key_part = jnp.einsum(
            "mgqk,mqgd->mkgd", d_score, query_group, preferred_element_type=jnp.float32
        )
        value_part = jnp.einsum(
            "mgqk,mqgd->mkgd", soft_b, upstream_group, preferred_element_type=jnp.float32
        )
        grad_query = lax.dynamic_update_slice_in_dim(
            grad_query,
            query_part.reshape(number_of_realizations, row_count, group_width).astype(jnp.bfloat16),
            first_col,
            2,
        )
        grad_key = lax.dynamic_update_slice_in_dim(
            grad_key,
            key_part.reshape(number_of_realizations, key_count, group_width).astype(jnp.bfloat16),
            first_col,
            2,
        )
        grad_value = lax.dynamic_update_slice_in_dim(
            grad_value,
            value_part.reshape(number_of_realizations, key_count, group_width).astype(jnp.bfloat16),
            first_col,
            2,
        )
        return (grad_query, grad_key, grad_value)

    initial = (
        jnp.zeros(queries.shape, jnp.bfloat16),
        jnp.zeros(key_rows.shape, jnp.bfloat16),
        jnp.zeros(value_rows.shape, jnp.bfloat16),
    )
    return lax.fori_loop(0, model_width // group_width, one_group, initial)


def probabilistic_accuracy(predicted_states, measured_part, scaling_coefficient):
    number_of_realizations = predicted_states.shape[0]
    fair_factor = 1.0 - (1.0 - FAIR_ALPHA) / number_of_realizations
    gap_from_measured = predicted_states - measured_part[None]
    smooth_observed = jnp.sqrt(gap_from_measured * gap_from_measured + SMOOTH_WIDTH * SMOOTH_WIDTH)
    between_realization_gap = predicted_states[:, None] - predicted_states[None, :]
    smooth_pair = jnp.sqrt(
        between_realization_gap * between_realization_gap + SMOOTH_WIDTH * SMOOTH_WIDTH
    )
    off_diagonal = (1.0 - jnp.eye(number_of_realizations, dtype=jnp.float32))[:, :, None, None]
    point_score = jnp.sum(smooth_observed, axis=0) / number_of_realizations - fair_factor / (
        2.0 * number_of_realizations * (number_of_realizations - 1)
    ) * jnp.sum(off_diagonal * smooth_pair, axis=(0, 1))
    total = jnp.sum(scaling_coefficient[:, None] * point_score)
    gradient = scaling_coefficient[None, :, None] * (
        gap_from_measured / smooth_observed / number_of_realizations
        - fair_factor
        / (number_of_realizations * (number_of_realizations - 1.0))
        * jnp.sum(between_realization_gap / smooth_pair, axis=1)
    )
    return (total, gradient)


def project_terms(key_part, value_part, w_key, w_value):
    return (times_transposed(key_part, w_key) + times_transposed(value_part, w_value)).astype(
        jnp.bfloat16
    )


def body(
    latent,
    observed,
    area_weight,
    band_counts,
    gain_attn,
    w_query,
    w_key,
    w_value,
    w_out,
    gain_head,
    w_head,
):
    band_index = lax.axis_index("band")
    band_total = lax.axis_size("band")
    member_total = lax.axis_size("member")
    members, slot_count, model_width = latent.shape
    hops = HOPS
    offsets_list = list(range(-hops, hops + 1))
    slot_iota = jnp.arange(slot_count, dtype=jnp.int32)
    offsets = jnp.cumsum(band_counts) - band_counts

    def band_rows(shift_by):
        other = band_index + shift_by
        inside = (other >= 0) & (other < band_total)
        clipped = jnp.clip(other, 0, band_total - 1)
        return (offsets[clipped] + slot_iota, inside & (slot_iota < band_counts[clipped]))

    own_pos, own_live = band_rows(0)
    key_pos = jnp.concatenate([band_rows(offset)[0] for offset in offsets_list])
    key_live = jnp.concatenate([band_rows(offset)[1] for offset in offsets_list])
    allowed = key_live[None, :] & (jnp.abs(own_pos[:, None] - key_pos[None, :]) <= R)
    latent_f = latent.astype(jnp.float32)
    inverse_one = inverse_rms(latent_f)
    normed = (latent_f * inverse_one * gain_attn).astype(jnp.bfloat16)
    queries = jnp.dot(normed, w_query, preferred_element_type=jnp.float32).astype(jnp.bfloat16)
    own_keys = jnp.dot(normed, w_key, preferred_element_type=jnp.float32).astype(jnp.bfloat16)
    own_values = jnp.dot(normed, w_value, preferred_element_type=jnp.float32).astype(jnp.bfloat16)
    key_parts = []
    value_parts = []
    for offset in offsets_list:
        if offset == 0:
            arrived = (own_keys, own_values)
        else:
            arrived = from_behind((own_keys, own_values), "band", -offset)
        key_parts.append(arrived[0])
        value_parts.append(arrived[1])
    key_rows = jnp.concatenate(key_parts, axis=1)
    value_rows = jnp.concatenate(value_parts, axis=1)
    mixed_out = attention_forward(queries, key_rows, value_rows, allowed)
    hidden = latent_f + jnp.dot(mixed_out, w_out, preferred_element_type=jnp.float32)
    inverse_two = inverse_rms(hidden)
    head_in = (hidden * inverse_two * gain_head).astype(jnp.bfloat16)
    predicted = jnp.dot(head_in, w_head, preferred_element_type=jnp.float32).astype(jnp.bfloat16)
    total_live = jnp.sum(band_counts).astype(jnp.float32) * CH
    point_weight = area_weight * own_live.astype(jnp.float32) / total_live
    grouped = lax.all_to_all(predicted, "member", split_axis=1, concat_axis=0, tiled=True)
    point_share = slot_count // member_total
    first_point = lax.axis_index("member") * point_share
    measured_part = lax.dynamic_slice_in_dim(observed, first_point, point_share, 0).astype(
        jnp.float32
    )
    weight_part = lax.dynamic_slice_in_dim(point_weight, first_point, point_share, 0)
    loss_part, gradient = probabilistic_accuracy(
        grouped.astype(jnp.float32), measured_part, weight_part
    )
    grad_pred = lax.all_to_all(
        gradient.astype(jnp.bfloat16), "member", split_axis=0, concat_axis=1, tiled=True
    )
    ensemble_loss = lax.psum(loss_part, ("member", "band"))
    head_share = lax.psum_scatter(
        lax.dot_general(
            head_in, grad_pred, (((0, 1), (0, 1)), ((), ())), preferred_element_type=jnp.float32
        ).astype(jnp.bfloat16),
        "band",
        scatter_dimension=0,
        tiled=True,
    )
    grad_head = lax.psum(head_share, "member").astype(jnp.float32)
    grad_hidden = norm_backward(hidden, gain_head, inverse_two, times_transposed(grad_pred, w_head))
    grad_mixed = times_transposed(grad_hidden.astype(jnp.bfloat16), w_out).astype(jnp.bfloat16)
    grad_queries, key_terms, value_terms = attention_backward(
        queries, key_rows, value_rows, allowed, grad_mixed
    )
    normed_total = jnp.zeros((members, slot_count, model_width), jnp.float32)
    for piece_index, offset in enumerate(offsets_list):
        key_piece = key_terms[:, piece_index * slot_count : (piece_index + 1) * slot_count]
        value_piece = value_terms[:, piece_index * slot_count : (piece_index + 1) * slot_count]
        if offset == 0:
            received = (key_piece, value_piece)
        else:
            received = from_behind((key_piece, value_piece), "band", offset)
        normed_piece = project_terms(received[0], received[1], w_key, w_value)
        normed_total = normed_total + normed_piece.astype(jnp.float32)
    grad_normed = times_transposed(grad_queries, w_query) + normed_total
    grad_latent = (
        grad_hidden + norm_backward(latent_f, gain_attn, inverse_one, grad_normed)
    ).astype(jnp.bfloat16)
    return (grad_latent, grad_head, ensemble_loss)


def solution(mesh):
    placed = (
        P("member", "band", None),
        P("band", None),
        P("band"),
        P(),
        P(),
        P(),
        P(),
        P(),
        P(),
        P(),
        P(),
    )
    return jax.shard_map(
        body,
        mesh=mesh,
        in_specs=placed,
        out_specs=(P("member", "band", None), P("band", None), P()),
        check_vma=False,
    )
```

profile of v0, /device:TPU:112, one launch (start us, length us, event | category | flops | bytes accessed | tf_op | source)
XLA Modules:
  0.0 862.6 jit_solution(12827514641480962040)
XLA Ops:
  58.5 10.5 %collective-permute-done.8 = bf16[1,256,1024]{2,1,0:T(8,128)(2,1)} collective-permute-done((bf16[1,256,1024]{2,1,0:T(8,128)(2,1)}, bf16[1,256,1024]{2,1,0:T(8,128)(2,1)}, u32[]{:S(2)}, u32[]{:S(2)}) %collective-permute-start.8) | collective-permute-done | bytes 524320 | tf_op jit(solution)/shard_map/ppermute | solution.py:23
  88.0 11.4 %collective-permute-start.1 = (bf16[1,256,1024]{2,1,0:T(8,128)(2,1)S(1)}, bf16[1,256,1024]{2,1,0:T(8,128)(2,1)S(1)}, u32[]{:S(2)}, u32[]{:S(2)}) collective-permute-start(bf16[1,256,1024]{2,1,0:T(8,128)(2,1)S(1)} %copy-done.25), channel_id=1, source_target_pairs={{0,3},{1,4},{2,5},{3,6},{4,7},{5,8},{6,9},{7,10},{8,11},{9,12},{10... | collective-permute-start | bytes 1572872 | tf_op jit(solution)/shard_map/ppermute | solution.py:23
  100.2 6.0 collective-permute-start.2
  107.1 14.1 %collective-permute-done.13 = bf16[1,256,1024]{2,1,0:T(8,128)(2,1)S(1)} collective-permute-done((bf16[1,256,1024]{2,1,0:T(8,128)(2,1)}, bf16[1,256,1024]{2,1,0:T(8,128)(2,1)S(1)}, u32[]{:S(2)}, u32[]{:S(2)}) %collective-permute-start.13) | collective-permute-done | bytes 524320 | tf_op jit(solution)/shard_map/ppermute | solution.py:23
  126.8 6.6 collective-permute-start.4
  147.4 6.7 copy.42
  156.9 24.9 %collective-permute-done.5 = bf16[1,256,1024]{2,1,0:T(8,128)(2,1)S(1)} collective-permute-done((bf16[1,256,1024]{2,1,0:T(8,128)(2,1)S(1)}, bf16[1,256,1024]{2,1,0:T(8,128)(2,1)S(1)}, u32[]{:S(2)}, u32[]{:S(2)}) %collective-permute-start.5) | collective-permute-done | bytes 524320 | tf_op jit(solution)/shard_map/ppermute | solution.py:23
  186.3 6.7 copy.40
  193.2 39.2 %while.32 = (s32[]{:T(128)}, bf16[1,256,1024]{1,2,0:T(8,128)(2,1)S(1)}, bf16[1,2304,1024]{1,2,0:T(8,128)(2,1)}, bf16[1,256,1024]{1,2,0:T(8,128)(2,1)}, bf16[1,23...) while((s32[]{:T(128)}, ...), condition=%wide.region_4.5_spmd.clone, body=%wide.region_2.4_spmd.clone.sunk | while | flops 622918656 | bytes 28529072 | solution.py:79
  261.8 69.6 %psum.15 = f32[]{:T(128)} all-reduce(f32[]{:T(128)} %multiply_reduce_fusion.2), channel_id=1, replica_groups=mesh['member'=8,'band'=16] {'member','band'}, use_global_device_ids=true, to_apply=%region_19.20 | all-reduce | flops 1 | bytes 8 | tf_op jit(solution)/shard_map/psum | solution.py:240
  344.2 257.5 %while.33 = (s32[]{:T(128)}, bf16[1,256,1024]{1,2,0:T(8,128)(2,1)}, bf16[1,2304,1024]{1,2,0:T(8,128)(2,1)}, bf16[1,2304,1024]{1,2,0:T(8,128)(2,1)}, bf16[1,2304,...) while((s32[]{:T(128)}, bf16[1,256,1024]{1,2,0:T(8,128)(2,1)}, ...), condition=%wide.region_12.13_spmd.clone, body=%wide.region_9.12_spmd.clone.sunk | while | flops 1581979136 | bytes 88961552 | solution.py:139
  361.6 19.0 %fusion.217 = bf16[4,64,256]{2,1,0:T(8,128)(2,1)} fusion(bf16[2304,4,64]{0,2,1:T(8,128)(2,1)S(1)} %bitcast.244, f32[4,256,2304]{2,1,0:T(8,128)} %fusion.214, f32[4,256,2304]{2,1,0:T(8,128)} %get-tuple-element.631, f32[4,256]{1,0:T(4,128)} %get-tuple-element.632, pred[256,2304]{1,0:T(8,128)(4,1)} %copy-done.5), kind=kOutput, calls=%fused_computation.30.clone.1 | convolution fusion | flops 328011008 | bytes 20779008 | tf_op jit(solution)/shard_map/while/body/eval_jaxpr/mgqk,mkgd->mqgd/dot_general | solution.py:105
  380.6 19.6 %fusion.219 = bf16[4,64,2304]{2,1,0:T(8,128)(2,1)S(1)} fusion(bf16[256,4,64]{0,2,1:T(8,128)(2,1)S(1)} %bitcast.248, f32[4,256,2304]{2,1,0:T(8,128)} %fusion.214, f32[4,256,2304]{2,1,0:T(8,128)} %get-tuple-element.631, f32[4,256]{1,0:T(4,128)} %get-tuple-element.632, pred[256,2304]{1,0:T(8,128)(4,1)} %copy-done.5), kind=kOutput, calls=%fused_computation.27.clone.1 | convolution fusion | flops 328535296 | bytes 20779008 | tf_op jit(solution)/shard_map/while/body/eval_jaxpr/mgqk,mqgd->mkgd/dot_general | solution.py:108
  400.2 6.4 fusion.218
  425.8 19.0 %fusion.217 = bf16[4,64,256]{2,1,0:T(8,128)(2,1)} fusion(bf16[2304,4,64]{0,2,1:T(8,128)(2,1)S(1)} %bitcast.244, f32[4,256,2304]{2,1,0:T(8,128)} %fusion.214, f32[4,256,2304]{2,1,0:T(8,128)} %get-tuple-element.631, f32[4,256]{1,0:T(4,128)} %get-tuple-element.632, pred[256,2304]{1,0:T(8,128)(4,1)} %copy-done.5), kind=kOutput, calls=%fused_computation.30.clone.1 | convolution fusion | flops 328011008 | bytes 20779008 | tf_op jit(solution)/shard_map/while/body/eval_jaxpr/mgqk,mkgd->mqgd/dot_general | solution.py:105
  444.9 19.6 %fusion.219 = bf16[4,64,2304]{2,1,0:T(8,128)(2,1)S(1)} fusion(bf16[256,4,64]{0,2,1:T(8,128)(2,1)S(1)} %bitcast.248, f32[4,256,2304]{2,1,0:T(8,128)} %fusion.214, f32[4,256,2304]{2,1,0:T(8,128)} %get-tuple-element.631, f32[4,256]{1,0:T(4,128)} %get-tuple-element.632, pred[256,2304]{1,0:T(8,128)(4,1)} %copy-done.5), kind=kOutput, calls=%fused_computation.27.clone.1 | convolution fusion | flops 328535296 | bytes 20779008 | tf_op jit(solution)/shard_map/while/body/eval_jaxpr/mgqk,mqgd->mkgd/dot_general | solution.py:108
  464.5 6.4 fusion.218
  490.1 19.0 %fusion.217 = bf16[4,64,256]{2,1,0:T(8,128)(2,1)} fusion(bf16[2304,4,64]{0,2,1:T(8,128)(2,1)S(1)} %bitcast.244, f32[4,256,2304]{2,1,0:T(8,128)} %fusion.214, f32[4,256,2304]{2,1,0:T(8,128)} %get-tuple-element.631, f32[4,256]{1,0:T(4,128)} %get-tuple-element.632, pred[256,2304]{1,0:T(8,128)(4,1)} %copy-done.5), kind=kOutput, calls=%fused_computation.30.clone.1 | convolution fusion | flops 328011008 | bytes 20779008 | tf_op jit(solution)/shard_map/while/body/eval_jaxpr/mgqk,mkgd->mqgd/dot_general | solution.py:105
  509.1 19.6 %fusion.219 = bf16[4,64,2304]{2,1,0:T(8,128)(2,1)S(1)} fusion(bf16[256,4,64]{0,2,1:T(8,128)(2,1)S(1)} %bitcast.248, f32[4,256,2304]{2,1,0:T(8,128)} %fusion.214, f32[4,256,2304]{2,1,0:T(8,128)} %get-tuple-element.631, f32[4,256]{1,0:T(4,128)} %get-tuple-element.632, pred[256,2304]{1,0:T(8,128)(4,1)} %copy-done.5), kind=kOutput, calls=%fused_computation.27.clone.1 | convolution fusion | flops 328535296 | bytes 20779008 | tf_op jit(solution)/shard_map/while/body/eval_jaxpr/mgqk,mqgd->mkgd/dot_general | solution.py:108
  528.7 6.4 fusion.218
  554.2 19.0 %fusion.217 = bf16[4,64,256]{2,1,0:T(8,128)(2,1)} fusion(bf16[2304,4,64]{0,2,1:T(8,128)(2,1)S(1)} %bitcast.244, f32[4,256,2304]{2,1,0:T(8,128)} %fusion.214, f32[4,256,2304]{2,1,0:T(8,128)} %get-tuple-element.631, f32[4,256]{1,0:T(4,128)} %get-tuple-element.632, pred[256,2304]{1,0:T(8,128)(4,1)} %copy-done.5), kind=kOutput, calls=%fused_computation.30.clone.1 | convolution fusion | flops 328011008 | bytes 20779008 | tf_op jit(solution)/shard_map/while/body/eval_jaxpr/mgqk,mkgd->mqgd/dot_general | solution.py:105
  573.3 19.6 %fusion.219 = bf16[4,64,2304]{2,1,0:T(8,128)(2,1)S(1)} fusion(bf16[256,4,64]{0,2,1:T(8,128)(2,1)S(1)} %bitcast.248, f32[4,256,2304]{2,1,0:T(8,128)} %fusion.214, f32[4,256,2304]{2,1,0:T(8,128)} %get-tuple-element.631, f32[4,256]{1,0:T(4,128)} %get-tuple-element.632, pred[256,2304]{1,0:T(8,128)(4,1)} %copy-done.5), kind=kOutput, calls=%fused_computation.27.clone.1 | convolution fusion | flops 328535296 | bytes 20779008 | tf_op jit(solution)/shard_map/while/body/eval_jaxpr/mgqk,mqgd->mkgd/dot_general | solution.py:108
  592.9 6.4 fusion.218
  632.9 71.4 %reduce-scatter.2.cloned.1.call-done = bf16[64,128]{1,0:T(8,128)(2,1)} async-done(((bf16[1024,128]{1,0:T(8,128)(2,1)}), bf16[64,128]{1,0:T(8,128)(2,1)}) %reduce-scatter.2.cloned.1.call-update) | async-done | bytes 16400 | tf_op jit(solution)/shard_map/reduce_scatter | solution.py:241
  704.3 19.8 %psum.14 = bf16[64,128]{1,0:T(8,128)(2,1)S(1)} all-reduce(bf16[64,128]{1,0:T(8,128)(2,1)} %reduce-scatter.2.cloned.1.call-done), channel_id=1, replica_groups=mesh['member'=8,'band'=16] {'member'}, use_global_device_ids=true, to_apply=%region_15.16 | all-reduce | flops 8192 | bytes 32768 | tf_op jit(solution)/shard_map/psum | solution.py:249
  741.3 18.4 %collective-permute-done.26 = bf16[1,256,1024]{1,2,0:T(8,128)(2,1)S(1)} collective-permute-done((bf16[1,256,1024]{1,2,0:T(8,128)(2,1)}, bf16[1,256,1024]{1,2,0:T(8,128)(2,1)S(1)}, u32[]{:S(2)}, u32[]{:S(2)}) %collective-permute-start.26) | collective-permute-done | bytes 524320 | tf_op jit(solution)/shard_map/ppermute | solution.py:23
  759.7 9.5 %collective-permute-start.24 = (bf16[1,256,1024]{1,2,0:T(8,128)(2,1)S(1)}, bf16[1,256,1024]{1,2,0:T(8,128)(2,1)S(1)}, u32[]{:S(2)}, u32[]{:S(2)}) collective-permute-start(bf16[1,256,1024]{1,2,0:T(8,128)(2,1)S(1)} %copy-done.24), channel_id=1, source_target_pairs={{0,1},{1,2},{2,3},{3,4},{4,5},{5,6},{6,7},{7,8},{8,9},{9,10},{10,1... | collective-permute-start | bytes 1572872 | tf_op jit(solution)/shard_map/ppermute | solution.py:23
  773.2 18.6 %collective-permute-done.24 = bf16[1,256,1024]{1,2,0:T(8,128)(2,1)S(1)} collective-permute-done((bf16[1,256,1024]{1,2,0:T(8,128)(2,1)S(1)}, bf16[1,256,1024]{1,2,0:T(8,128)(2,1)S(1)}, u32[]{:S(2)}, u32[]{:S(2)}) %collective-permute-start.24) | collective-permute-done | bytes 524320 | tf_op jit(solution)/shard_map/ppermute | solution.py:23
  798.0 9.6 %collective-permute-done.22 = bf16[1,256,1024]{1,2,0:T(8,128)(2,1)S(1)} collective-permute-done((bf16[1,256,1024]{1,2,0:T(8,128)(2,1)S(1)}, bf16[1,256,1024]{1,2,0:T(8,128)(2,1)S(1)}, u32[]{:S(2)}, u32[]{:S(2)}) %collective-permute-start.22) | collective-permute-done | bytes 524320 | tf_op jit(solution)/shard_map/ppermute | solution.py:23
  812.6 14.1 %collective-permute-done.20 = bf16[1,256,1024]{1,2,0:T(8,128)(2,1)S(1)} collective-permute-done((bf16[1,256,1024]{1,2,0:T(8,128)(2,1)S(1)}, bf16[1,256,1024]{1,2,0:T(8,128)(2,1)S(1)}, u32[]{:S(2)}, u32[]{:S(2)}) %collective-permute-start.20) | collective-permute-done | bytes 524320 | tf_op jit(solution)/shard_map/ppermute | solution.py:23
  828.8 8.1 collective-permute-start.30
  837.6 10.8 %collective-permute-done.18 = bf16[1,256,1024]{1,2,0:T(8,128)(2,1)S(1)} collective-permute-done((bf16[1,256,1024]{1,2,0:T(8,128)(2,1)S(1)}, bf16[1,256,1024]{1,2,0:T(8,128)(2,1)S(1)}, u32[]{:S(2)}, u32[]{:S(2)}) %collective-permute-start.18) | collective-permute-done | bytes 524320 | tf_op jit(solution)/shard_map/ppermute | solution.py:23
  (314 shorter events, 328.7 us)
Async XLA Ops:
  11.7 115.1 %collective-permute-start.15 = (bf16[1,256,1024]{2,1,0:T(8,128)(2,1)}, bf16[1,256,1024]{2,1,0:T(8,128)(2,1)S(1)}, u32[]{:S(2)}, u32[]{:S(2)}) collective-permute-start(bf16[1,256,1024]{2,1,0:T(8,128)(2,1)} %fusion.73), channel_id=1, source_target_pairs={{4,0},{5,1},{6,2},{7,3},{8,4},{9,5},{10,6},{11,7},{12,8},{13,9},{1... | collective-permute-start | bytes 1572872 | tf_op jit(solution)/shard_map/ppermute | solution.py:23
  13.0 69.9 %collective-permute-start.11 = (bf16[1,256,1024]{2,1,0:T(8,128)(2,1)}, bf16[1,256,1024]{2,1,0:T(8,128)(2,1)}, u32[]{:S(2)}, u32[]{:S(2)}) collective-permute-start(bf16[1,256,1024]{2,1,0:T(8,128)(2,1)} %fusion.73), channel_id=1, source_target_pairs={{0,1},{1,2},{2,3},{3,4},{4,5},{5,6},{6,7},{7,8},{8,9},{9,10},{10,1... | collective-permute-start | bytes 1572872 | tf_op jit(solution)/shard_map/ppermute | solution.py:23
  16.2 62.9 %collective-permute-start.10 = (bf16[1,256,1024]{2,1,0:T(8,128)(2,1)}, bf16[1,256,1024]{2,1,0:T(8,128)(2,1)}, u32[]{:S(2)}, u32[]{:S(2)}) collective-permute-start(bf16[1,256,1024]{2,1,0:T(8,128)(2,1)} %fusion.73), channel_id=1, source_target_pairs={{0,2},{1,3},{2,4},{3,5},{4,6},{5,7},{6,8},{7,9},{8,10},{9,11},{10,... | collective-permute-start | bytes 1572872 | tf_op jit(solution)/shard_map/ppermute | solution.py:23
  20.8 54.5 %collective-permute-start.9 = (bf16[1,256,1024]{2,1,0:T(8,128)(2,1)}, bf16[1,256,1024]{2,1,0:T(8,128)(2,1)}, u32[]{:S(2)}, u32[]{:S(2)}) collective-permute-start(bf16[1,256,1024]{2,1,0:T(8,128)(2,1)} %fusion.73), channel_id=1, source_target_pairs={{0,3},{1,4},{2,5},{3,6},{4,7},{5,8},{6,9},{7,10},{8,11},{9,12},{10... | collective-permute-start | bytes 1572872 | tf_op jit(solution)/shard_map/ppermute | solution.py:23
  25.5 43.5 %collective-permute-start.8 = (bf16[1,256,1024]{2,1,0:T(8,128)(2,1)}, bf16[1,256,1024]{2,1,0:T(8,128)(2,1)}, u32[]{:S(2)}, u32[]{:S(2)}) collective-permute-start(bf16[1,256,1024]{2,1,0:T(8,128)(2,1)} %fusion.73), channel_id=1, source_target_pairs={{0,4},{1,5},{2,6},{3,7},{4,8},{5,9},{6,10},{7,11},{8,12},{9,13},{1... | collective-permute-start | bytes 1572872 | tf_op jit(solution)/shard_map/ppermute | solution.py:23
  75.3 24.9 %collective-permute-start.12 = (bf16[1,256,1024]{2,1,0:T(8,128)(2,1)}, bf16[1,256,1024]{2,1,0:T(8,128)(2,1)S(1)}, u32[]{:S(2)}, u32[]{:S(2)}) collective-permute-start(bf16[1,256,1024]{2,1,0:T(8,128)(2,1)} %fusion.73), channel_id=1, source_target_pairs={{1,0},{2,1},{3,2},{4,3},{5,4},{6,5},{7,6},{8,7},{9,8},{10,9},{11,1... | collective-permute-start | bytes 1572872 | tf_op jit(solution)/shard_map/ppermute | solution.py:23
  79.1 42.1 %collective-permute-start.13 = (bf16[1,256,1024]{2,1,0:T(8,128)(2,1)}, bf16[1,256,1024]{2,1,0:T(8,128)(2,1)S(1)}, u32[]{:S(2)}, u32[]{:S(2)}) collective-permute-start(bf16[1,256,1024]{2,1,0:T(8,128)(2,1)} %fusion.73), channel_id=1, source_target_pairs={{2,0},{3,1},{4,2},{5,3},{6,4},{7,5},{8,6},{9,7},{10,8},{11,9},{12,... | collective-permute-start | bytes 1572872 | tf_op jit(solution)/shard_map/ppermute | solution.py:23
  82.9 41.7 %collective-permute-start.14 = (bf16[1,256,1024]{2,1,0:T(8,128)(2,1)}, bf16[1,256,1024]{2,1,0:T(8,128)(2,1)S(1)}, u32[]{:S(2)}, u32[]{:S(2)}) collective-permute-start(bf16[1,256,1024]{2,1,0:T(8,128)(2,1)} %fusion.73), channel_id=1, source_target_pairs={{3,0},{4,1},{5,2},{6,3},{7,4},{8,5},{9,6},{10,7},{11,8},{12,9},{13... | collective-permute-start | bytes 1572872 | tf_op jit(solution)/shard_map/ppermute | solution.py:23
  88.0 46.3 %collective-permute-start.1 = (bf16[1,256,1024]{2,1,0:T(8,128)(2,1)S(1)}, bf16[1,256,1024]{2,1,0:T(8,128)(2,1)S(1)}, u32[]{:S(2)}, u32[]{:S(2)}) collective-permute-start(bf16[1,256,1024]{2,1,0:T(8,128)(2,1)S(1)} %copy-done.25), channel_id=1, source_target_pairs={{0,3},{1,4},{2,5},{3,6},{4,7},{5,8},{6,9},{7,10},{8,11},{9,12},{10... | collective-permute-start | bytes 1572872 | tf_op jit(solution)/shard_map/ppermute | solution.py:23
  100.2 39.9 %collective-permute-start.2 = (bf16[1,256,1024]{2,1,0:T(8,128)(2,1)S(1)}, bf16[1,256,1024]{2,1,0:T(8,128)(2,1)S(1)}, u32[]{:S(2)}, u32[]{:S(2)}) collective-permute-start(bf16[1,256,1024]{2,1,0:T(8,128)(2,1)S(1)} %copy-done.25), channel_id=1, source_target_pairs={{0,2},{1,3},{2,4},{3,5},{4,6},{5,7},{6,8},{7,9},{8,10},{9,11},{10,... | collective-permute-start | bytes 1572872 | tf_op jit(solution)/shard_map/ppermute | solution.py:23
  121.2 25.4 %collective-permute-start.3 = (bf16[1,256,1024]{2,1,0:T(8,128)(2,1)S(1)}, bf16[1,256,1024]{2,1,0:T(8,128)(2,1)S(1)}, u32[]{:S(2)}, u32[]{:S(2)}) collective-permute-start(bf16[1,256,1024]{2,1,0:T(8,128)(2,1)S(1)} %copy-done.25), channel_id=1, source_target_pairs={{0,1},{1,2},{2,3},{3,4},{4,5},{5,6},{6,7},{7,8},{8,9},{9,10},{10,1... | collective-permute-start | bytes 1572872 | tf_op jit(solution)/shard_map/ppermute | solution.py:23
  124.6 59.8 %collective-permute-start.7 = (bf16[1,256,1024]{2,1,0:T(8,128)(2,1)S(1)}, bf16[1,256,1024]{2,1,0:T(8,128)(2,1)}, u32[]{:S(2)}, u32[]{:S(2)}) collective-permute-start(bf16[1,256,1024]{2,1,0:T(8,128)(2,1)S(1)} %copy-done.25), channel_id=1, source_target_pairs={{4,0},{5,1},{6,2},{7,3},{8,4},{9,5},{10,6},{11,7},{12,8},{13,9},{1... | collective-permute-start | bytes 1572872 | tf_op jit(solution)/shard_map/ppermute | solution.py:23
  126.8 28.2 %collective-permute-start.4 = (bf16[1,256,1024]{2,1,0:T(8,128)(2,1)S(1)}, bf16[1,256,1024]{2,1,0:T(8,128)(2,1)}, u32[]{:S(2)}, u32[]{:S(2)}) collective-permute-start(bf16[1,256,1024]{2,1,0:T(8,128)(2,1)S(1)} %copy-done.25), channel_id=1, source_target_pairs={{1,0},{2,1},{3,2},{4,3},{5,4},{6,5},{7,6},{8,7},{9,8},{10,9},{11,1... | collective-permute-start | bytes 1572872 | tf_op jit(solution)/shard_map/ppermute | solution.py:23
  134.3 47.5 %collective-permute-start.5 = (bf16[1,256,1024]{2,1,0:T(8,128)(2,1)S(1)}, bf16[1,256,1024]{2,1,0:T(8,128)(2,1)S(1)}, u32[]{:S(2)}, u32[]{:S(2)}) collective-permute-start(bf16[1,256,1024]{2,1,0:T(8,128)(2,1)S(1)} %copy-done.25), channel_id=1, source_target_pairs={{2,0},{3,1},{4,2},{5,3},{6,4},{7,5},{8,6},{9,7},{10,8},{11,9},{12,... | collective-permute-start | bytes 1572872 | tf_op jit(solution)/shard_map/ppermute | solution.py:23
  140.1 42.5 %collective-permute-start.6 = (bf16[1,256,1024]{2,1,0:T(8,128)(2,1)S(1)}, bf16[1,256,1024]{2,1,0:T(8,128)(2,1)}, u32[]{:S(2)}, u32[]{:S(2)}) collective-permute-start(bf16[1,256,1024]{2,1,0:T(8,128)(2,1)S(1)} %copy-done.25), channel_id=1, source_target_pairs={{3,0},{4,1},{5,2},{6,3},{7,4},{8,5},{9,6},{10,7},{11,8},{12,9},{13... | collective-permute-start | bytes 1572872 | tf_op jit(solution)/shard_map/ppermute | solution.py:23
  255.0 76.4 %all-to-all-start.1 = ((bf16[8,32,128]{2,1,0:T(8,128)(2,1)}), bf16[8,32,128]{2,1,0:T(8,128)(2,1)S(1)}, u32[]{:S(2)}, u32[]{:S(2)}) async-start(bf16[8,32,128]{2,1,0:T(8,128)(2,1)} %get-tuple-element.463), calls=%async_computation.1 | async-start | bytes 131072 | tf_op jit(solution)/shard_map/all_to_all | solution.py:237
  260.3 443.9 %reduce-scatter.2.cloned.1.call-start = ((), (), s32[]{:S(2)}) async-start(), calls=%async_computation.3 | async-start | bytes 278528 | tf_op jit(solution)/shard_map/reduce_scatter | solution.py:241
  612.3 237.0 %collective-permute-start.17 = (bf16[1,256,1024]{1,2,0:T(8,128)(2,1)}, bf16[1,256,1024]{1,2,0:T(8,128)(2,1)}, u32[]{:S(2)}, u32[]{:S(2)}) collective-permute-start(bf16[1,256,1024]{1,2,0:T(8,128)(2,1)} %get-tuple-element.454), channel_id=1, source_target_pairs={{4,0},{5,1},{6,2},{7,3},{8,4},{9,5},{10,6},{11,7},{12,8},{13,9},{1... | collective-permute-start | bytes 1572872 | tf_op jit(solution)/shard_map/ppermute | solution.py:23
  613.5 111.2 %collective-permute-start.29 = (bf16[1,256,1024]{1,2,0:T(8,128)(2,1)}, bf16[1,256,1024]{1,2,0:T(8,128)(2,1)}, u32[]{:S(2)}, u32[]{:S(2)}) collective-permute-start(bf16[1,256,1024]{1,2,0:T(8,128)(2,1)} %get-tuple-element.455), channel_id=1, source_target_pairs={{0,3},{1,4},{2,5},{3,6},{4,7},{5,8},{6,9},{7,10},{8,11},{9,12},{10... | collective-permute-start | bytes 1572872 | tf_op jit(solution)/shard_map/ppermute | solution.py:23
  619.0 118.4 %collective-permute-start.27 = (bf16[1,256,1024]{1,2,0:T(8,128)(2,1)}, bf16[1,256,1024]{1,2,0:T(8,128)(2,1)}, u32[]{:S(2)}, u32[]{:S(2)}) collective-permute-start(bf16[1,256,1024]{1,2,0:T(8,128)(2,1)} %get-tuple-element.456), channel_id=1, source_target_pairs={{0,2},{1,3},{2,4},{3,5},{4,6},{5,7},{6,8},{7,9},{8,10},{9,11},{10,... | collective-permute-start | bytes 1572872 | tf_op jit(solution)/shard_map/ppermute | solution.py:23
  621.8 148.1 %collective-permute-start.25 = (bf16[1,256,1024]{1,2,0:T(8,128)(2,1)}, bf16[1,256,1024]{1,2,0:T(8,128)(2,1)}, u32[]{:S(2)}, u32[]{:S(2)}) collective-permute-start(bf16[1,256,1024]{1,2,0:T(8,128)(2,1)} %get-tuple-element.457), channel_id=1, source_target_pairs={{0,1},{1,2},{2,3},{3,4},{4,5},{5,6},{6,7},{7,8},{8,9},{9,10},{10,1... | collective-permute-start | bytes 1572872 | tf_op jit(solution)/shard_map/ppermute | solution.py:23
  625.3 104.6 %collective-permute-start.28 = (bf16[1,256,1024]{1,2,0:T(8,128)(2,1)}, bf16[1,256,1024]{1,2,0:T(8,128)(2,1)}, u32[]{:S(2)}, u32[]{:S(2)}) collective-permute-start(bf16[1,256,1024]{1,2,0:T(8,128)(2,1)} %get-tuple-element.447), channel_id=1, source_target_pairs={{0,3},{1,4},{2,5},{3,6},{4,7},{5,8},{6,9},{7,10},{8,11},{9,12},{10... | collective-permute-start | bytes 1572872 | tf_op jit(solution)/shard_map/ppermute | solution.py:23
  724.7 70.1 %collective-permute-start.23 = (bf16[1,256,1024]{1,2,0:T(8,128)(2,1)}, bf16[1,256,1024]{1,2,0:T(8,128)(2,1)S(1)}, u32[]{:S(2)}, u32[]{:S(2)}) collective-permute-start(bf16[1,256,1024]{1,2,0:T(8,128)(2,1)} %get-tuple-element.458), channel_id=1, source_target_pairs={{1,0},{2,1},{3,2},{4,3},{5,4},{6,5},{7,6},{8,7},{9,8},{10,9},{11,1... | collective-permute-start | bytes 1572872 | tf_op jit(solution)/shard_map/ppermute | solution.py:23
  729.9 29.7 %collective-permute-start.26 = (bf16[1,256,1024]{1,2,0:T(8,128)(2,1)}, bf16[1,256,1024]{1,2,0:T(8,128)(2,1)S(1)}, u32[]{:S(2)}, u32[]{:S(2)}) collective-permute-start(bf16[1,256,1024]{1,2,0:T(8,128)(2,1)} %get-tuple-element.448), channel_id=1, source_target_pairs={{0,2},{1,3},{2,4},{3,5},{4,6},{5,7},{6,8},{7,9},{8,10},{9,11},{10,... | collective-permute-start | bytes 1572872 | tf_op jit(solution)/shard_map/ppermute | solution.py:23
  737.4 72.9 %collective-permute-start.21 = (bf16[1,256,1024]{1,2,0:T(8,128)(2,1)S(1)}, bf16[1,256,1024]{1,2,0:T(8,128)(2,1)S(1)}, u32[]{:S(2)}, u32[]{:S(2)}) collective-permute-start(bf16[1,256,1024]{1,2,0:T(8,128)(2,1)S(1)} %copy-done.23), channel_id=1, source_target_pairs={{2,0},{3,1},{4,2},{5,3},{6,4},{7,5},{8,6},{9,7},{10,8},{11,9},{12,... | collective-permute-start | bytes 1572872 | tf_op jit(solution)/shard_map/ppermute | solution.py:23
  759.7 32.2 %collective-permute-start.24 = (bf16[1,256,1024]{1,2,0:T(8,128)(2,1)S(1)}, bf16[1,256,1024]{1,2,0:T(8,128)(2,1)S(1)}, u32[]{:S(2)}, u32[]{:S(2)}) collective-permute-start(bf16[1,256,1024]{1,2,0:T(8,128)(2,1)S(1)} %copy-done.24), channel_id=1, source_target_pairs={{0,1},{1,2},{2,3},{3,4},{4,5},{5,6},{6,7},{7,8},{8,9},{9,10},{10,1... | collective-permute-start | bytes 1572872 | tf_op jit(solution)/shard_map/ppermute | solution.py:23
  769.9 58.8 %collective-permute-start.19 = (bf16[1,256,1024]{1,2,0:T(8,128)(2,1)S(1)}, bf16[1,256,1024]{1,2,0:T(8,128)(2,1)S(1)}, u32[]{:S(2)}, u32[]{:S(2)}) collective-permute-start(bf16[1,256,1024]{1,2,0:T(8,128)(2,1)S(1)} %copy-done.21), channel_id=1, source_target_pairs={{3,0},{4,1},{5,2},{6,3},{7,4},{8,5},{9,6},{10,7},{11,8},{12,9},{13... | collective-permute-start | bytes 1572872 | tf_op jit(solution)/shard_map/ppermute | solution.py:23
  794.9 56.2 %collective-permute-start.31 = (bf16[1,256,1024]{1,2,0:T(8,128)(2,1)S(1)}, bf16[1,256,1024]{1,2,0:T(8,128)(2,1)S(1)}, u32[]{:S(2)}, u32[]{:S(2)}) collective-permute-start(bf16[1,256,1024]{1,2,0:T(8,128)(2,1)S(1)} %copy-done.19), channel_id=1, source_target_pairs={{0,4},{1,5},{2,6},{3,7},{4,8},{5,9},{6,10},{7,11},{8,12},{9,13},{1... | collective-permute-start | bytes 1572872 | tf_op jit(solution)/shard_map/ppermute | solution.py:23
  807.6 19.1 %collective-permute-start.20 = (bf16[1,256,1024]{1,2,0:T(8,128)(2,1)S(1)}, bf16[1,256,1024]{1,2,0:T(8,128)(2,1)S(1)}, u32[]{:S(2)}, u32[]{:S(2)}) collective-permute-start(bf16[1,256,1024]{1,2,0:T(8,128)(2,1)S(1)} %copy-done.20), channel_id=1, source_target_pairs={{2,0},{3,1},{4,2},{5,3},{6,4},{7,5},{8,6},{9,7},{10,8},{11,9},{12,... | collective-permute-start | bytes 1572872 | tf_op jit(solution)/shard_map/ppermute | solution.py:23
  810.4 42.4 %collective-permute-start.16 = (bf16[1,256,1024]{1,2,0:T(8,128)(2,1)S(1)}, bf16[1,256,1024]{1,2,0:T(8,128)(2,1)S(1)}, u32[]{:S(2)}, u32[]{:S(2)}) collective-permute-start(bf16[1,256,1024]{1,2,0:T(8,128)(2,1)S(1)} %copy-done.16), channel_id=1, source_target_pairs={{4,0},{5,1},{6,2},{7,3},{8,4},{9,5},{10,6},{11,7},{12,8},{13,9},{1... | collective-permute-start | bytes 1572872 | tf_op jit(solution)/shard_map/ppermute | solution.py:23
  826.7 21.7 %collective-permute-start.18 = (bf16[1,256,1024]{1,2,0:T(8,128)(2,1)S(1)}, bf16[1,256,1024]{1,2,0:T(8,128)(2,1)S(1)}, u32[]{:S(2)}, u32[]{:S(2)}) collective-permute-start(bf16[1,256,1024]{1,2,0:T(8,128)(2,1)S(1)} %copy-done.18), channel_id=1, source_target_pairs={{3,0},{4,1},{5,2},{6,3},{7,4},{8,5},{9,6},{10,7},{11,8},{12,9},{13... | collective-permute-start | bytes 1572872 | tf_op jit(solution)/shard_map/ppermute | solution.py:23
  828.8 23.1 %collective-permute-start.30 = (bf16[1,256,1024]{1,2,0:T(8,128)(2,1)S(1)}, bf16[1,256,1024]{1,2,0:T(8,128)(2,1)S(1)}, u32[]{:S(2)}, u32[]{:S(2)}) collective-permute-start(bf16[1,256,1024]{1,2,0:T(8,128)(2,1)S(1)} %copy-done.17), channel_id=1, source_target_pairs={{0,4},{1,5},{2,6},{3,7},{4,8},{5,9},{6,10},{7,11},{8,12},{9,13},{1... | collective-permute-start | bytes 1572872 | tf_op jit(solution)/shard_map/ppermute | solution.py:23
  (47 other events, 840.4 us)
Sparse Core Ops, SparseCore 0:
  607.9 96.3 reduce-scatter.1
where the time goes:
time: 871 us; the launch traced here: 863 us
  matrix products  288 us (33%)
  waiting for transfers between devices  203 us (23%)
  starting transfers between devices  123 us (14%)
  local copies, waits for them, and re-layouts  103 us (12%)
  blocking collectives  89.4 us (10%)
  other arithmetic  39.8 us (5%)
  between operations  15.9 us (2%)
    ppermute x32, waiting for transfers between devices, from_behind(): lax.ppermute(value, axis, [(source, source + steps) for source in range(l...  129 us
    ppermute x32, starting transfers between devices, from_behind(): lax.ppermute(value, axis, [(source, source + steps) for source in range(l...  113 us
    dot_general x4, matrix products, one_group(): jnp.einsum('mgqk,mqgd->mkgd', d_score, query_group, preferred_element_typ...  78.6 us
    dot_general x4, matrix products, one_group(): jnp.einsum('mgqk,mkgd->mqgd', d_score, key_group, preferred_element_type=...  76.1 us
    reduce_scatter x1, waiting for transfers between devices, body(): lax.psum_scatter(lax.dot_general(head_in, grad_pred, (((0, 1), (0, 1)), (...  71.4 us
    psum x1, blocking collectives, body(): ensemble_loss = lax.psum(loss_part, ('member', 'band'))  69.6 us
    unnamed x102, local copies, waits for them, and re-layouts  43.2 us
    dot_general x8, matrix products, window_probs(): jnp.einsum('mqgd,mkgd->mgqk', query_group, key_group, preferred_element_t...  33.4 us
  transfers between devices with their start and end apart: 35, of which 13 were waited for; matrix products, arithmetic and copies ran while one was open for 10% of the time, Pallas kernels for 0%

commit v1 on v0

v1 whole, which is shorter than its diff:
```python
import jax
import jax.numpy as jnp
from jax import lax
from jax.experimental import pallas as pl
from jax.experimental.pallas import tpu as pltpu
from jax.sharding import PartitionSpec as P

HEADS = 16
HEAD = 64
CH = 128
R = 512
CAP = 256
MEMBERS = 8
BANDS = 16
EPS = 1e-06
SMOOTH = 0.0625
FAIR = 1.0 - 0.05 / MEMBERS
PAIR_SCALE = FAIR / (MEMBERS * (MEMBERS - 1.0))

WIDTH = 2 * R + CAP + 128
ROWS = BANDS * CAP - CAP + WIDTH
EDGE = 384
CHUNKS = ((0, EDGE, 1), (EDGE, 2 * R, 0), (2 * R, WIDTH, 2))
HEAD_ROWS = 64
SENT_ROWS = 128 + HEAD_ROWS + 16

f32 = jnp.float32
bf16 = jnp.bfloat16


def dot(a, b):
    return lax.dot_general(a, b, (((1,), (0,)), ((), ())), preferred_element_type=f32)


def dot_nt(a, b):
    return lax.dot_general(a, b, (((1,), (1,)), ((), ())), preferred_element_type=f32)


def dot_tn(a, b):
    return lax.dot_general(a, b, (((0,), (0,)), ((), ())), preferred_element_type=f32)


def swap(x):
    return pltpu.roll(x, HEAD, axis=1)


def low_lanes(rows):
    return lax.broadcasted_iota(jnp.int32, (rows, 128), 1) < HEAD


def store_halves(pair, write):
    low = low_lanes(128)
    top, bottom = pair[:128], pair[128:]
    write(0, jnp.where(low, top, swap(bottom)).astype(bf16))
    write(1, jnp.where(low, swap(top), bottom).astype(bf16))


def load_halves(first, second):
    low = low_lanes(128)
    first, second = first.astype(f32), second.astype(f32)
    top = jnp.where(low, first, swap(second))
    bottom = jnp.where(low, swap(first), second)
    return top.astype(bf16), bottom.astype(bf16)


def project_kernel(lat_ref, gain_ref, wq_ref, wk_ref, wv_ref, out_ref):
    x = lat_ref[...].astype(f32)
    inverse = lax.rsqrt(jnp.mean(x * x, axis=-1, keepdims=True) + EPS)
    normed = (x * inverse * gain_ref[...]).astype(bf16)
    low = low_lanes(CAP)
    for quad in range(4):
        cols = slice(quad * 256, quad * 256 + 256)
        q = dot(normed, wq_ref[:, cols]) * 0.125
        k = dot(normed, wk_ref[:, cols])
        v = dot(normed, wv_ref[:, cols])
        for half in range(2):
            head = quad * 4 + half * 2
            part = slice(half * 128, half * 128 + 128)

            def write(i, value):
                out_ref[head + i, 0:128, :] = value

            store_halves(q[:, part], write)
            kp, vp = k[:, part], v[:, part]
            out_ref[head, 128:384, :] = jnp.where(low, kp, swap(vp)).astype(bf16)
            out_ref[head + 1, 128:384, :] = jnp.where(low, swap(kp), vp).astype(bf16)


def query_rows(packed):
    low = low_lanes(128)
    zero = jnp.zeros((128, 128), f32)
    packed = packed.astype(f32)
    return jnp.concatenate(
        [jnp.where(low, packed, zero), jnp.where(low, swap(packed), zero)], 0
    ).astype(bf16)


def upstream_rows(packed):
    low = low_lanes(128)
    zero = jnp.zeros((128, 128), f32)
    packed = packed.astype(f32)
    return jnp.concatenate(
        [jnp.where(low, zero, swap(packed)), jnp.where(low, zero, packed)], 0
    ).astype(bf16)


def exponents(scores, bias, mode, rel):
    e = jnp.exp(scores + jnp.concatenate([bias, bias], 1))
    if mode:
        gap = lax.broadcasted_iota(jnp.int32, e.shape, 0) - lax.broadcasted_iota(
            jnp.int32, e.shape, 1
        )
        e = jnp.where(gap >= rel if mode == 1 else gap <= rel, e, 0.0)
    return e


def forward_kernel(
    counts_ref, x_ref, mixed_ref, exact_ref, inverse_ref, kv_ref, kt_ref, bias_ref, rows_ref, vt_ref
):
    rows_ref[...] = jnp.zeros((ROWS, 128), f32)
    sub = lax.broadcasted_iota(jnp.int32, (1, 8, 128), 1)
    row = lax.broadcasted_iota(jnp.int32, (CAP, 128), 0)

    def place(b, off):
        count = counts_ref[b]
        shift = off & 7
        base = pl.multiple_of(off - shift + R, 8)
        x = jnp.where(row < count, x_ref[b, 128:384, :].astype(f32), 0.0)
        turned = pltpu.roll(x.reshape(32, 8, 128), shift, axis=1)
        before = rows_ref[pl.ds(base, 8), :].reshape(1, 8, 128)
        shifted = jnp.concatenate([before, turned], 0)
        turned = jnp.concatenate([turned, jnp.zeros((1, 8, 128), f32)], 0)
        rows_ref[pl.ds(base, 264), :] = jnp.where(sub < shift, shifted, turned).reshape(264, 128)
        return off + count

    total = lax.fori_loop(0, BANDS, place, jnp.int32(0))
    vt_ref[HEAD:, :] = jnp.ones((16, ROWS), bf16)
    tile_row = lax.broadcasted_iota(jnp.int32, (128, 128), 0)
    for t in range(ROWS // 128):
        span = slice(t * 128, t * 128 + 128)
        tile = rows_ref[span, :]
        kv_ref[span, :] = tile.astype(bf16)
        turned = tile.T
        kt_ref[:, span] = turned[:HEAD].astype(bf16)
        vt_ref[:HEAD, span] = turned[HEAD:].astype(bf16)
        position = tile_row + (t * 128 - R)
        bias_ref[span, :] = jnp.where((position >= 0) & (position < total), 0.0, -1e30)

    def band(b, off):
        rel = off & 127
        start = pl.multiple_of(off - rel, 128)
        q = query_rows(x_ref[b, 0:128, :])
        out = jnp.zeros((HEAD + 16, CAP), f32)
        for first, last, mode in CHUNKS:
            span = pl.ds(pl.multiple_of(start + first, 128), last - first)
            s = dot_nt(kv_ref[span, :], q)
            e = exponents(s, bias_ref[span, :], mode, rel).astype(bf16)
            out = out + dot(vt_ref[:, span], e)
        inverse = 1.0 / out[HEAD : HEAD + 1, :]
        inverse_ref[pl.ds(b, 1), :] = inverse
        out = out[:HEAD] * inverse
        mixed = jnp.concatenate([out[:, :128], out[:, 128:]], 0).T
        exact_ref[b] = mixed
        mixed_ref[b] = mixed.astype(bf16)
        return off + counts_ref[b]

    lax.fori_loop(0, BANDS, band, jnp.int32(0))


def head_kernel(mixed_ref, lat_ref, wo_ref, gain_ref, wh_ref, hidden_ref, pred_ref, rows_ref):
    for pair in range(8):
        top, bottom = load_halves(mixed_ref[2 * pair], mixed_ref[2 * pair + 1])
        rows_ref[:128, pair * 128 : pair * 128 + 128] = top
        rows_ref[128:, pair * 128 : pair * 128 + 128] = bottom
    hidden = lat_ref[...].astype(f32) + dot(rows_ref[...], wo_ref[...])
    hidden_ref[...] = hidden
    inverse = lax.rsqrt(jnp.mean(hidden * hidden, axis=-1, keepdims=True) + EPS)
    head_in = (hidden * inverse * gain_ref[...]).astype(bf16)
    predicted = dot(head_in, wh_ref[...]).astype(bf16)
    for j in range(MEMBERS):
        pred_ref[j] = predicted


def split3(x):
    high = x.astype(bf16)
    rest = x - high.astype(f32)
    middle = rest.astype(bf16)
    low = (rest - middle.astype(f32)).astype(bf16)
    return high, middle, low


def loss_kernel(
    place_ref, counts_ref, pred_ref, obs_ref, area_ref, hidden_ref, gain_ref, wh_ref, wo_ref,
    grad_ref, out_ref,
):
    me, band = place_ref[0], place_ref[1]
    total = lax.fori_loop(0, BANDS, lambda b, t: t + counts_ref[b], jnp.int32(0))
    area = area_ref[...]
    weight = jnp.concatenate(
        [jnp.broadcast_to(area[i : i + 1, :], (128, 128)).T for i in range(2)], 0
    )
    row = lax.broadcasted_iota(jnp.int32, (CAP, CH), 0)
    weight = jnp.where(row < counts_ref[band], weight, 0.0) / (total.astype(f32) * CH)
    mine = pred_ref[me].astype(f32)

    def smooth(gap):
        square = gap * gap + SMOOTH
        inverse = lax.rsqrt(square)
        return square * inverse, gap * inverse

    size, slope = smooth(mine - obs_ref[...].astype(f32))
    pair_size = jnp.zeros((CAP, CH), f32)
    pair_slope = jnp.zeros((CAP, CH), f32)
    for k in range(MEMBERS):
        a, da = smooth(mine - pred_ref[k].astype(f32))
        pair_size = pair_size + jnp.where(me == k, 0.0, 1.0) * a
        pair_slope = pair_slope + da
    loss = jnp.sum(weight * (size / MEMBERS - (0.5 * PAIR_SCALE) * pair_size), axis=0, keepdims=True)
    grad_pred = (weight * (slope / MEMBERS - PAIR_SCALE * pair_slope)).astype(bf16)

    hidden = hidden_ref[...]
    gain = gain_ref[...]
    inverse = lax.rsqrt(jnp.mean(hidden * hidden, axis=-1, keepdims=True) + EPS)
    head_in = (hidden * inverse * gain).astype(bf16)
    grad_head = dot_tn(head_in, grad_pred).astype(bf16)
    scaled = dot_nt(grad_pred, wh_ref[...]) * gain
    grad_hidden = inverse * scaled - hidden * (inverse * inverse * inverse) * jnp.mean(
        hidden * scaled, axis=-1, keepdims=True
    )
    grad_ref[...] = grad_hidden
    grad_mixed = dot_nt(grad_hidden.astype(bf16), wo_ref[...])
    pieces = [jnp.broadcast_to(p, (1, 128)).astype(f32) for p in split3(loss)]
    pieces = jnp.concatenate(pieces + [jnp.zeros((13, 128), f32)], 0).astype(bf16)
    for pair in range(8):

        def write(i, value):
            out_ref[2 * pair + i, 0:128, :] = value

        store_halves(grad_mixed[:, pair * 128 : pair * 128 + 128], write)
    for b in range(BANDS):
        out_ref[b, 128:192, :] = grad_head[b * HEAD_ROWS : (b + 1) * HEAD_ROWS]
        out_ref[b, 192:208, :] = pieces


def share_kernel(sent_ref, out_ref):
    grad = jnp.zeros((HEAD_ROWS, CH), f32)
    loss = jnp.zeros((16, 128), f32)
    for b in range(BANDS):
        grad = grad + sent_ref[b, 128:192, :].astype(f32)
        loss = loss + sent_ref[b, 192:208, :].astype(f32)
    loss = jnp.sum(loss, axis=0, keepdims=True)
    pieces = jnp.concatenate(
        [p.astype(f32) for p in split3(loss)] + [jnp.zeros((13, 128), f32)], 0
    ).astype(bf16)
    grad = grad.astype(bf16)
    for j in range(MEMBERS):
        out_ref[j, :HEAD_ROWS, :] = grad
        out_ref[j, HEAD_ROWS:, :] = pieces


def total_kernel(shared_ref, grad_ref, loss_ref):
    grad = jnp.zeros((HEAD_ROWS, CH), f32)
    loss = jnp.zeros((16, 128), f32)
    for j in range(MEMBERS):
        grad = grad + shared_ref[j, :HEAD_ROWS, :].astype(f32)
        loss = loss + shared_ref[j, HEAD_ROWS:, :].astype(f32)
    grad_ref[...] = grad
    loss_ref[...] = jnp.sum(jnp.sum(loss, axis=0, keepdims=True), axis=1, keepdims=True)


def backward_kernel(
    counts_ref, x_ref, sent_ref, exact_ref, inverse_ref, kv_ref, kt_ref, bias_ref, out_ref, acc_ref
):
    acc_ref[...] = jnp.zeros((ROWS, 128), f32)

    def band(b, off):
        rel = off & 127
        start = pl.multiple_of(off - rel, 128)
        q = query_rows(x_ref[b, 0:128, :])
        upstream = sent_ref[b, 0:128, :]
        g = upstream_rows(upstream)
        both = jnp.concatenate([q, g], 0)
        product = (exact_ref[b] * upstream.astype(f32)).T
        inner = jnp.concatenate(
            [
                jnp.sum(product[:HEAD], axis=0, keepdims=True),
                jnp.sum(product[HEAD:], axis=0, keepdims=True),
            ],
            1,
        )
        inverse = inverse_ref[pl.ds(b, 1), :]
        grad_q = jnp.zeros((HEAD, CAP), f32)
        for first, last, mode in CHUNKS:
            span = pl.ds(pl.multiple_of(start + first, 128), last - first)
            kv = kv_ref[span, :]
            p = exponents(dot_nt(kv, q), bias_ref[span, :], mode, rel) * inverse
            ds = (p * (dot_nt(kv, g) - inner)).astype(bf16)
            acc_ref[span, :] += dot(jnp.concatenate([ds, p.astype(bf16)], 1), both)
            grad_q = grad_q + dot(kt_ref[:, span], ds)
        grad_q = grad_q * 0.125
        out_ref[b, 0:128, :] = jnp.concatenate([grad_q[:, :128], grad_q[:, 128:]], 0).T.astype(bf16)
        return off + counts_ref[b]

    lax.fori_loop(0, BANDS, band, jnp.int32(0))
    sub = lax.broadcasted_iota(jnp.int32, (1, 8, 128), 1)
    row = lax.broadcasted_iota(jnp.int32, (CAP, 128), 0)

    def give(b, off):
        count = counts_ref[b]
        shift = off & 7
        base = pl.multiple_of(off - shift + R, 8)
        x = acc_ref[pl.ds(base, 264), :].reshape(33, 8, 128)
        turned = pltpu.roll(x, (8 - shift) & 7, axis=1)
        x = jnp.where(sub + shift < 8, turned[:32], turned[1:]).reshape(CAP, 128)
        out_ref[b, 128:384, :] = jnp.where(row < count, x, 0.0).astype(bf16)
        return off + count

    lax.fori_loop(0, BANDS, give, jnp.int32(0))


def latent_kernel(
    d_ref, lat_ref, gain_ref, wq_ref, wk_ref, wv_ref, grad_ref, out_ref, dq_ref, dk_ref, dv_ref
):
    low = low_lanes(CAP)
    for pair in range(8):
        cols = slice(pair * 128, pair * 128 + 128)
        top, bottom = load_halves(d_ref[2 * pair, 0:128, :], d_ref[2 * pair + 1, 0:128, :])
        dq_ref[:128, cols] = top
        dq_ref[128:, cols] = bottom
        first = d_ref[2 * pair, 128:384, :].astype(f32)
        second = d_ref[2 * pair + 1, 128:384, :].astype(f32)
        dk_ref[:, cols] = jnp.where(low, first, swap(second)).astype(bf16)
        dv_ref[:, cols] = jnp.where(low, swap(first), second).astype(bf16)
    normed = (
        dot_nt(dq_ref[...], wq_ref[...])
        + dot_nt(dk_ref[...], wk_ref[...])
        + dot_nt(dv_ref[...], wv_ref[...])
    )
    x = lat_ref[...].astype(f32)
    inverse = lax.rsqrt(jnp.mean(x * x, axis=-1, keepdims=True) + EPS)
    scaled = normed * gain_ref[...]
    out_ref[...] = (
        grad_ref[...]
        + inverse * scaled
        - x * (inverse * inverse * inverse) * jnp.mean(x * scaled, axis=-1, keepdims=True)
    ).astype(bf16)


def call(kernel, outs, scalars, arrays, scratch=(), name=None):
    vmem = pl.BlockSpec(memory_space=pltpu.VMEM)
    smem = pl.BlockSpec(memory_space=pltpu.SMEM)
    return pl.pallas_call(
        kernel,
        out_shape=tuple(jax.ShapeDtypeStruct(s, d) for s, d in outs),
        in_specs=[smem] * len(scalars) + [vmem] * len(arrays),
        out_specs=tuple(vmem for _ in outs),
        scratch_shapes=[pltpu.VMEM(s, d) for s, d in scratch],
        name=name,
    )(*scalars, *arrays)


def attend_forward(counts, x):
    return call(
        forward_kernel,
        [
            ((BANDS, 128, 128), bf16),
            ((BANDS, 128, 128), f32),
            ((BANDS, CAP), f32),
            ((ROWS, 128), bf16),
            ((HEAD, ROWS), bf16),
            ((ROWS, 128), f32),
        ],
        [counts],
        [x],
        [((ROWS, 128), f32), ((HEAD + 16, ROWS), bf16)],
        name="attend_forward",
    )


def attend_backward(counts, x, sent, exact, inverse, kv, kt, bias):
    return call(
        backward_kernel,
        [((BANDS, 384, 128), bf16)],
        [counts],
        [x, sent, exact, inverse, kv, kt, bias],
        [((ROWS, 128), f32)],
        name="attend_backward",
    )[0]


def exchange(x, axis):
    return lax.all_to_all(x, axis, split_axis=0, concat_axis=0, tiled=True)


def body(
    latent, observed, area_weight, counts, gain_attn, w_query, w_key, w_value, w_out, gain_head, w_head
):
    members, cap, width = latent.shape
    lat = latent.reshape(cap, width)
    gain_a = gain_attn.reshape(1, width)
    gain_h = gain_head.reshape(1, width)
    area = area_weight.reshape(2, 128)
    place = jnp.stack([lax.axis_index("member"), lax.axis_index("band")]).astype(jnp.int32)
    (sent,) = call(
        project_kernel,
        [((HEADS, 384, 128), bf16)],
        [],
        [lat, gain_a, w_query, w_key, w_value],
        name="project",
    )
    x = exchange(sent, "band")
    mixed, exact, inverse, kv, kt, bias = attend_forward(counts, x)
    mixed = exchange(mixed, "band")
    hidden, predicted = call(
        head_kernel,
        [((cap, width), f32), ((MEMBERS, cap, CH), bf16)],
        [],
        [mixed, lat, w_out, gain_h, w_head],
        [((cap, width), bf16)],
        name="head",
    )
    predicted = exchange(predicted, "member")
    grad_hidden, sent = call(
        loss_kernel,
        [((cap, width), f32), ((BANDS, SENT_ROWS, 128), bf16)],
        [place, counts],
        [predicted, observed, area, hidden, gain_h, w_head, w_out],
        name="loss",
    )
    sent = exchange(sent, "band")
    (shared,) = call(
        share_kernel, [((MEMBERS, HEAD_ROWS + 16, 128), bf16)], [], [sent], name="share"
    )
    shared = exchange(shared, "member")
    grads = attend_backward(counts, x, sent, exact, inverse, kv, kt, bias)
    grads = exchange(grads, "band")
    grad_head, loss = call(
        total_kernel, [((HEAD_ROWS, CH), f32), ((1, 1), f32)], [], [shared], name="total"
    )
    (grad_latent,) = call(
        latent_kernel,
        [((cap, width), bf16)],
        [],
        [grads, lat, gain_a, w_query, w_key, w_value, grad_hidden],
        [((cap, width), bf16)] * 3,
        name="latent",
    )
    return grad_latent.reshape(latent.shape), grad_head, loss.reshape(())


def solution(mesh):
    rows = P("member", "band", None)
    placed = (rows, P("band", None), P("band")) + (P(),) * 8
    return jax.shard_map(
        body,
        mesh=mesh,
        in_specs=placed,
        out_specs=(rows, P("band", None), P()),
        check_vma=False,
    )
```

time: 871 us -> 182 us (0.21)
  the two profiles are of different devices: /device:TPU:112 before, /device:TPU:0 now
where the time goes in v1:
time: 182 us
  Pallas kernels  68.9 us (38%)
  blocking collectives  63.6 us (35%)
  waiting for transfers between devices  33.5 us (18%)
  starting transfers between devices  12.5 us (7%)
  local copies, waits for them, and re-layouts  1.96 us (1%)
    pallas_call x8, Pallas kernels, call(): pl.pallas_call(kernel, out_shape=tuple((jax.ShapeDtypeStruct(s, d) for s,...  68.9 us
    all_to_all x3, blocking collectives, exchange(): return lax.all_to_all(x, axis, split_axis=0, concat_axis=0, tiled=True)  63.6 us
    all_to_all x3, waiting for transfers between devices, exchange(): return lax.all_to_all(x, axis, split_axis=0, concat_axis=0, tiled=True)  33.5 us
    all_to_all x3, starting transfers between devices, exchange(): return lax.all_to_all(x, axis, split_axis=0, concat_axis=0, tiled=True)  12.5 us
  transfers between devices with their start and end apart: 3, of which 2 were waited for; matrix products, arithmetic and copies ran while one was open for 0% of the time, Pallas kernels for 15%

profile of v1, /device:TPU:0, one launch (start us, length us, event | category | flops | bytes accessed | tf_op | source)
XLA Modules:
  0.0 181.8 jit_solution(2834901086650733810)
XLA Ops:
  0.6 6.2 %project.1 = bf16[16,384,128]{2,1,0:T(8,128)(2,1)} custom-call(bf16[256,1024]{1,0:T(8,128)(2,1)} %bitcast.8, f32[1,1024]{1,0:T(1,128)} %bitcast.12, bf16[1024,1024]{1,0:T(8,128)(2,1)} %wq_ref.3, bf16[1024,1024]{1,0:T(8,128)(2,1)} %wk_ref.3, bf16[1024,1024]{1,0:T(8,128)(2,1)} %wv_ref.3), custom_call_target="tpu_custom_call" | custom-call | tf_op jit(solution)/shard_map/project/pallas_call | solution.py:352
  6.8 29.8 %all_to_all.30.x_ref = bf16[16,384,128]{2,1,0:T(8,128)(2,1)} all-to-all(bf16[16,384,128]{2,1,0:T(8,128)(2,1)} %project.1), channel_id=1, replica_groups=mesh['member'=8,'band'=16] {'band'}, dimensions={0} | all-to-all | bytes 3145728 | tf_op jit(solution)/shard_map/all_to_all | solution.py:392
  36.6 17.8 %attend_forward.1 = (bf16[16,128,128]{2,1,0:T(8,128)(2,1)}, f32[16,128,128]{2,1,0:T(8,128)}, f32[16,256]{1,0:T(8,128)}, bf16[5248,128]{1,0:T(8,128)(2,1)}, bf16[...) custom-call(s32[16]{0:T(128)} %counts_ref.5, bf16[16,384,128]{2,1,0:T(8,128)(2,1)} %all_to_all.30.x_ref), custom_call_target="tpu_custom_call" | custom-call | tf_op jit(solution)/shard_map/attend_forward/pallas_call | solution.py:352
  54.4 14.7 %all_to_all.31.mixed_ref = bf16[16,128,128]{2,1,0:T(8,128)(2,1)} all-to-all(bf16[16,128,128]{2,1,0:T(8,128)(2,1)} %get-tuple-element.15), channel_id=1, replica_groups=mesh['member'=8,'band'=16] {'band'}, dimensions={0} | all-to-all | bytes 1048576 | tf_op jit(solution)/shard_map/all_to_all | solution.py:392
  69.1 3.9 %head.1 = (f32[256,1024]{1,0:T(8,128)}, bf16[8,256,128]{2,1,0:T(8,128)(2,1)}) custom-call(bf16[16,128,128]{2,1,0:T(8,128)(2,1)} %all_to_all.31.mixed_ref, bf16[256,1024]{1,0:T(8,128)(2,1)} %bitcast.9, bf16[1024,1024]{1,0:T(8,128)(2,1)} %wo_ref.3, f32[1,1024]{1,0:T(1,128)} %bitcast.14, bf16[1024,128]{1,0:T(8,128)(2,1)} %wh_ref.3), custom_call_target="tpu_custom_call" | custom-call | tf_op jit(solution)/shard_map/head/pallas_call | solution.py:352
  73.0 5.3 %all-to-all-start.2 = ((bf16[8,256,128]{2,1,0:T(8,128)(2,1)}), bf16[8,256,128]{2,1,0:T(8,128)(2,1)S(1)}, u32[]{:S(2)}, u32[]{:S(2)}) async-start(bf16[8,256,128]{2,1,0:T(8,128)(2,1)} %get-tuple-element.16), calls=%async_computation.2 | async-start | bytes 1048576 | tf_op jit(solution)/shard_map/all_to_all | solution.py:392
  78.3 0.6 pad_add_fusion.place_ref
  78.9 9.7 %all-to-all-done.2.pred_ref = bf16[8,256,128]{2,1,0:T(8,128)(2,1)S(1)} async-done(((bf16[8,256,128]{2,1,0:T(8,128)(2,1)}), bf16[8,256,128]{2,1,0:T(8,128)(2,1)S(1)}, u32[]{:S(2)}, u32[]{:S(2)}) %all-to-all-start.2) | async-done | bytes 524320 | tf_op jit(solution)/shard_map/all_to_all | solution.py:392
  88.6 0.0 copy-start.1
  88.6 0.8 copy-done.1
  89.4 4.9 %loss.1 = (f32[256,1024]{1,0:T(8,128)}, bf16[16,208,128]{2,1,0:T(8,128)(2,1)}) custom-call(s32[2]{0:T(128)} %pad_add_fusion.place_ref, s32[16]{0:T(128)} %counts_ref.5, bf16[8,256,128]{2,1,0:T(8,128)(2,1)} %copy-done.1, bf16[256,128]{1,0:T(8,128)(2,1)} %obs_ref.1, f32[2,128]{1,0:T(2,128)} %bitcast.16, f32[256,1024]{1,0:T(8,128)} %get-tuple-element.17.hidden_ref, ...), custom_call_target="tpu_custom_call" | custom-call | tf_op jit(solution)/shard_map/loss/pallas_call | solution.py:352
  94.3 19.1 %all_to_all.32.sent_ref = bf16[16,208,128]{2,1,0:T(8,128)(2,1)} all-to-all(bf16[16,208,128]{2,1,0:T(8,128)(2,1)} %get-tuple-element.18), channel_id=1, replica_groups=mesh['member'=8,'band'=16] {'band'}, dimensions={0} | all-to-all | bytes 1703936 | tf_op jit(solution)/shard_map/all_to_all | solution.py:392
  113.4 1.9 %share.1 = bf16[8,80,128]{2,1,0:T(8,128)(2,1)} custom-call(bf16[16,208,128]{2,1,0:T(8,128)(2,1)} %all_to_all.32.sent_ref), custom_call_target="tpu_custom_call" | custom-call | tf_op jit(solution)/shard_map/share/pallas_call | solution.py:352
  115.2 3.4 %all-to-all-start.5 = ((bf16[8,80,128]{2,1,0:T(8,128)(2,1)}), bf16[8,80,128]{2,1,0:T(8,128)(2,1)S(1)}, u32[]{:S(2)}, u32[]{:S(2)}) async-start(bf16[8,80,128]{2,1,0:T(8,128)(2,1)} %share.1), calls=%async_computation.5 | async-start | bytes 327680 | tf_op jit(solution)/shard_map/all_to_all | solution.py:392
  118.6 26.1 %attend_backward.1 = bf16[16,384,128]{2,1,0:T(8,128)(2,1)} custom-call(s32[16]{0:T(128)} %counts_ref.5, bf16[16,384,128]{2,1,0:T(8,128)(2,1)} %all_to_all.30.x_ref, bf16[16,208,128]{2,1,0:T(8,128)(2,1)} %all_to_all.32.sent_ref, f32[16,128,128]{2,1,0:T(8,128)} %get-tuple-element.19.exact_ref, f32[16,256]{1,0:T(8,128)} %get-tuple-element.20.inverse_ref, ...), custom_call_target="tpu_custom_call" | custom-call | tf_op jit(solution)/shard_map/attend_backward/pallas_call | solution.py:352
  144.8 0.0 all-to-all-done.5.shared_ref
  144.8 0.0 copy-start.2
  144.8 3.8 %all-to-all-start.4 = ((bf16[16,384,128]{2,1,0:T(8,128)(2,1)}), bf16[16,384,128]{2,1,0:T(8,128)(2,1)S(1)}, u32[]{:S(2)}, u32[]{:S(2)}) async-start(bf16[16,384,128]{2,1,0:T(8,128)(2,1)} %attend_backward.1), calls=%async_computation.4 | async-start | bytes 3145728 | tf_op jit(solution)/shard_map/all_to_all | solution.py:392
  148.6 0.0 copy-done.2
  148.6 1.6 total.1
  150.1 23.9 %all-to-all-done.4.d_ref = bf16[16,384,128]{2,1,0:T(8,128)(2,1)S(1)} async-done(((bf16[16,384,128]{2,1,0:T(8,128)(2,1)}), bf16[16,384,128]{2,1,0:T(8,128)(2,1)S(1)}, u32[]{:S(2)}, u32[]{:S(2)}) %all-to-all-start.4) | async-done | bytes 1572896 | tf_op jit(solution)/shard_map/all_to_all | solution.py:392
  174.0 0.0 copy-start
  174.0 1.2 copy-done
  175.2 6.6 %latent.1 = bf16[256,1024]{1,0:T(8,128)(2,1)} custom-call(bf16[16,384,128]{2,1,0:T(8,128)(2,1)} %copy-done, bf16[256,1024]{1,0:T(8,128)(2,1)} %bitcast.10, f32[1,1024]{1,0:T(1,128)} %bitcast.13, bf16[1024,1024]{1,0:T(8,128)(2,1)} %wq_ref.3, bf16[1024,1024]{1,0:T(8,128)(2,1)} %wk_ref.3, bf16[1024,1024]{1,0:T(8,128)(2,1)} %wv_ref.3, ...), custom_call_target="tpu_custom_call" | custom-call | tf_op jit(solution)/shard_map/latent/pallas_call | solution.py:352
Async XLA Ops:
  73.0 15.6 %all-to-all-start.2 = ((bf16[8,256,128]{2,1,0:T(8,128)(2,1)}), bf16[8,256,128]{2,1,0:T(8,128)(2,1)S(1)}, u32[]{:S(2)}, u32[]{:S(2)}) async-start(bf16[8,256,128]{2,1,0:T(8,128)(2,1)} %get-tuple-element.16), calls=%async_computation.2 | async-start | bytes 1048576 | tf_op jit(solution)/shard_map/all_to_all | solution.py:392
  88.6 0.8 copy-start.1
  115.2 29.5 %all-to-all-start.5 = ((bf16[8,80,128]{2,1,0:T(8,128)(2,1)}), bf16[8,80,128]{2,1,0:T(8,128)(2,1)S(1)}, u32[]{:S(2)}, u32[]{:S(2)}) async-start(bf16[8,80,128]{2,1,0:T(8,128)(2,1)} %share.1), calls=%async_computation.5 | async-start | bytes 327680 | tf_op jit(solution)/shard_map/all_to_all | solution.py:392
  144.8 3.8 %copy-start.2 = (bf16[8,80,128]{2,1,0:T(8,128)(2,1)}, bf16[8,80,128]{2,1,0:T(8,128)(2,1)S(1)}, u32[]{:S(2)}) copy-start(bf16[8,80,128]{2,1,0:T(8,128)(2,1)S(1)} %all-to-all-done.5.shared_ref) | copy-start | bytes 491524
  144.8 29.2 %all-to-all-start.4 = ((bf16[16,384,128]{2,1,0:T(8,128)(2,1)}), bf16[16,384,128]{2,1,0:T(8,128)(2,1)S(1)}, u32[]{:S(2)}, u32[]{:S(2)}) async-start(bf16[16,384,128]{2,1,0:T(8,128)(2,1)} %attend_backward.1), calls=%async_computation.4 | async-start | bytes 3145728 | tf_op jit(solution)/shard_map/all_to_all | solution.py:392
  174.0 1.2 copy-start

commit v2 on v1

v2 whole, which is shorter than its diff:
```python
import functools

import jax
import jax.numpy as jnp
from jax import lax
from jax.experimental import pallas as pl
from jax.experimental.pallas import tpu as pltpu
from jax.sharding import PartitionSpec as P

HEADS = 16
HEAD = 64
CH = 128
R = 512
CAP = 256
MEMBERS = 8
BANDS = 16
LOG2E = 1.4426950408889634
EPS = 1e-06
SMOOTH = 0.0625
FAIR = 1.0 - 0.05 / MEMBERS
PAIR_SCALE = FAIR / (MEMBERS * (MEMBERS - 1.0))

HALF = CAP // 2
WIDTH = 2 * R + CAP + 128
COLS = BANDS * CAP - CAP + WIDTH
EDGE = CAP + 128
STEPS = ((0, 512), (512, 512), (1024, 384))
DEAD = -32768.0
ONES, BIAS, AGAIN, DEPTH = 128, 144, 192, 256
TURNED = 144
UNROLL = 2
HEAD_ROWS = 64

f32 = jnp.float32
bf16 = jnp.bfloat16


def dot(a, b):
    return lax.dot_general(a, b, (((1,), (0,)), ((), ())), preferred_element_type=f32)


def dot_nt(a, b):
    return lax.dot_general(a, b, (((1,), (1,)), ((), ())), preferred_element_type=f32)


def dot_tn(a, b):
    return lax.dot_general(a, b, (((0,), (0,)), ((), ())), preferred_element_type=f32)


def swap(x):
    return pltpu.roll(x, HEAD, axis=1)


def lanes(rows):
    return lax.broadcasted_iota(jnp.int32, (rows, 128), 1)


def low_lanes(rows):
    return lanes(rows) < HEAD


def fold(first, second):
    low = low_lanes(64)
    return jnp.where(low, first, swap(second)), jnp.where(low, swap(first), second)


def unfold(packed):
    packed = packed.astype(f32)
    other = swap(packed)
    return jnp.concatenate([packed[:64], other[:64], packed[64:], other[64:]], 0)


def refold(rows):
    low = low_lanes(64)
    return jnp.concatenate(
        [jnp.where(low, rows[i : i + 64], swap(rows[i + 64 : i + 128])) for i in (0, 128)], 0
    )


def split3(x):
    high = x.astype(bf16).astype(f32)
    middle = (x - high).astype(bf16).astype(f32)
    return high, middle, (x - high - middle).astype(bf16).astype(f32)


def inverse_rms(x):
    return lax.rsqrt(jnp.mean(x * x, axis=-1, keepdims=True) + EPS)


def norm_backward(x, inverse, scaled):
    return inverse * scaled - x * (inverse * inverse * inverse) * jnp.mean(
        x * scaled, axis=-1, keepdims=True
    )


def keys_kernel(lat_ref, gain_ref, wk_ref, wv_ref, kv_ref, normed_ref):
    x = lat_ref[...].astype(f32)
    normed_ref[...] = (x * inverse_rms(x) * gain_ref[...]).astype(bf16)
    low = low_lanes(CAP)
    for quad in range(4):
        cols = slice(quad * 256, quad * 256 + 256)
        k = dot(normed_ref[...], wk_ref[:, cols])
        v = dot(normed_ref[...], wv_ref[:, cols])
        for half in range(2):
            head = quad * 4 + half * 2
            part = slice(half * 128, half * 128 + 128)
            kp, vp = k[:, part], v[:, part]
            kv_ref[head] = jnp.where(low, kp, swap(vp)).astype(bf16)
            kv_ref[head + 1] = jnp.where(low, swap(kp), vp).astype(bf16)


def fold_heads(x, refs):
    for i, ref in enumerate(refs):
        for pair in range(HEADS // 2):
            part = x[i * HALF : (i + 1) * HALF, pair * 128 : pair * 128 + 128]
            first, second = fold(part[:64], part[64:])
            ref[2 * pair, 0:64, :] = first.astype(bf16)
            ref[2 * pair + 1, 0:64, :] = second.astype(bf16)


def unfold_heads(refs, rows_ref):
    for i, ref in enumerate(refs):
        for pair in range(HEADS // 2):
            first, second = fold(ref[2 * pair, 0:64, :].astype(f32), ref[2 * pair + 1, 0:64, :].astype(f32))
            cols = slice(pair * 128, pair * 128 + 128)
            rows_ref[i * HALF : i * HALF + 64, cols] = first.astype(bf16)
            rows_ref[i * HALF + 64 : (i + 1) * HALF, cols] = second.astype(bf16)


def parts(ref, n):
    return [ref.at[:, i * 64 : i * 64 + 64, :] for i in range(n)]


def queries_kernel(normed_ref, wq_ref, *q_refs):
    q = dot(normed_ref[...], wq_ref[...]) * 0.125
    fold_heads(q, [part for ref in q_refs for part in parts(ref, 2 // len(q_refs))])


def compact_kernel(counts_ref, kv_ref, kvx_ref, kvt_ref, rows_ref):
    sub = lax.broadcasted_iota(jnp.int32, (1, 8, 128), 1)
    row = lax.broadcasted_iota(jnp.int32, (CAP, 128), 0)
    rows_ref[...] = jnp.zeros((COLS, 128), f32)

    def place(b, off):
        count = counts_ref[b]
        shift = off & 7
        base = pl.multiple_of(off - shift + R, 8)
        x = jnp.where(row < count, kv_ref[b].astype(f32), 0.0)
        turned = pltpu.roll(x.reshape(32, 8, 128), shift, axis=1)
        before = rows_ref[pl.ds(base, 8), :].reshape(1, 8, 128)
        shifted = jnp.concatenate([before, turned], 0)
        turned = jnp.concatenate([turned, jnp.zeros((1, 8, 128), f32)], 0)
        rows_ref[pl.ds(base, 264), :] = jnp.where(sub < shift, shifted, turned).reshape(264, 128)
        return off + count

    total = lax.fori_loop(0, BANDS, place, jnp.int32(0))
    kvt_ref[128:, :] = jnp.ones((TURNED - 128, COLS), bf16)
    lane = lanes(128)
    tile_row = lax.broadcasted_iota(jnp.int32, (128, 128), 0)
    ones = jnp.where(lane < BIAS - ONES, 1.0, 0.0)
    for t in range(COLS // 128):
        span = slice(t * 128, t * 128 + 128)
        position = tile_row + (t * 128 - R)
        side = jnp.where((lane == BIAS - ONES) & ((position < 0) | (position >= total)), DEAD, ones)
        if R <= t * 128 < R + BANDS * CAP:
            tile = rows_ref[span, :]
            kvx_ref[span, :128] = tile.astype(bf16)
            kvx_ref[span, 128:] = jnp.where(lane < HEAD, side, swap(tile)).astype(bf16)
            kvt_ref[:128, span] = tile.T.astype(bf16)
        else:
            kvx_ref[span, :128] = jnp.zeros((128, 128), bf16)
            kvx_ref[span, 128:] = side.astype(bf16)
            kvt_ref[:128, span] = jnp.zeros((128, 128), bf16)


def query_columns(q, log_sum):
    lane = lanes(CAP)
    low = lane < HEAD
    scaled = q * LOG2E
    high = scaled.astype(bf16).astype(f32)
    rest = jnp.where(low, scaled - high, 0.0)
    second = jnp.where(low, 0.0, swap(rest))
    second = jnp.where(lane == BIAS - ONES, 1.0, second)
    if log_sum is not None:
        for i, piece in enumerate(split3(-log_sum)):
            second = jnp.where(lane == i, piece, second)
    return jnp.concatenate([jnp.where(low, high, 0.0), second], 1).astype(bf16)


def masked(p, first, size, rel):
    gap = lax.broadcasted_iota(jnp.int32, (EDGE, CAP), 0) - lax.broadcasted_iota(
        jnp.int32, (EDGE, CAP), 1
    )
    if first == 0:
        edge = jnp.where(gap >= rel, p[:EDGE], 0.0)
        p = edge if size == EDGE else jnp.concatenate([edge, p[EDGE:]], 0)
    if first + size == WIDTH:
        edge = jnp.where(gap <= rel, p[size - EDGE :], 0.0)
        p = edge if size == EDGE else jnp.concatenate([p[: size - EDGE], edge], 0)
    return p


def each_band(counts_ref, band):
    def some(i, off):
        for j in range(UNROLL):
            b = UNROLL * i + j
            band(b, pl.multiple_of(off - (off & 127), 128), off & 127)
            off = off + counts_ref[b]
        return off

    lax.fori_loop(0, BANDS // UNROLL, some, jnp.int32(0))


def forward_kernel(counts_ref, kvx_ref, kvt_ref, q_ref, mixed_ref, exact_ref):
    low = low_lanes(CAP)

    def band(b, start, rel):
        q = query_columns(unfold(q_ref[b]), None)
        out = jnp.zeros((TURNED - HEAD, CAP), f32)
        for first, size in STEPS:
            span = pl.ds(pl.multiple_of(start + first, 128), size)
            p = masked(jnp.exp2(dot_nt(kvx_ref[span, :], q)), first, size, rel)
            out = out + dot(kvt_ref[HEAD:, span], p.astype(bf16))
        out = jnp.concatenate([out, jnp.zeros((128 + HEAD - TURNED, CAP), f32)], 0).T
        total = jnp.broadcast_to(out[:, HEAD : HEAD + 1], (CAP, 128))
        out = jnp.where(low, out * (1.0 / total), jnp.log2(total))
        exact_ref[b] = out
        mixed_ref[b] = refold(out).astype(bf16)

    each_band(counts_ref, band)


def head_kernel(halves, mixed_ref, lat_ref, wo_ref, gain_ref, wh_ref, hidden_ref, pred_ref, rows_ref):
    unfold_heads(parts(mixed_ref, len(halves)), rows_ref)
    hidden = lat_ref[...].astype(f32) + dot(rows_ref[...], wo_ref[...])
    hidden_ref[...] = hidden
    head_in = (hidden * inverse_rms(hidden) * gain_ref[...]).astype(bf16)
    predicted = dot(head_in, wh_ref[...]).astype(bf16)
    for j in range(MEMBERS):
        pred_ref[j] = predicted


def loss_kernel(
    halves, last, place_ref, counts_ref, pred_ref, obs_ref, area_ref, hidden_ref, gain_ref, wh_ref, wo_ref,
    *refs,
):
    refs = list(refs)
    before = None if halves[0] == 0 else (refs.pop(0), refs.pop(0))
    grad_ref, out_ref = refs[:2]
    me, band = place_ref[0], place_ref[1]
    total = lax.fori_loop(0, BANDS, lambda b, t: t + counts_ref[b], jnp.int32(0))
    area = area_ref[...]
    rows = HALF * len(halves)
    weight = jnp.concatenate(
        [jnp.broadcast_to(area[i : i + 1, :], (128, 128)).T for i in halves], 0
    )
    row = lax.broadcasted_iota(jnp.int32, (rows, CH), 0) + halves[0] * HALF
    weight = jnp.where(row < counts_ref[band], weight, 0.0) / (total.astype(f32) * CH)
    mine = pred_ref[me].astype(f32)

    def smooth(gap):
        square = gap * gap + SMOOTH
        inverse = lax.rsqrt(square)
        return square * inverse, gap * inverse

    size, slope = smooth(mine - obs_ref[...].astype(f32))
    pair_size = jnp.zeros((rows, CH), f32)
    pair_slope = jnp.zeros((rows, CH), f32)
    for k in range(MEMBERS):
        a, da = smooth(mine - pred_ref[k].astype(f32))
        pair_size = pair_size + jnp.where(me == k, 0.0, 1.0) * a
        pair_slope = pair_slope + da
    loss = jnp.sum(weight * (size / MEMBERS - (0.5 * PAIR_SCALE) * pair_size), axis=0, keepdims=True)
    grad_pred = (weight * (slope / MEMBERS - PAIR_SCALE * pair_slope)).astype(bf16)

    hidden = hidden_ref[...]
    gain = gain_ref[...]
    inverse = inverse_rms(hidden)
    scaled = dot_nt(grad_pred, wh_ref[...]) * gain
    grad_hidden = norm_backward(hidden, inverse, scaled)
    grad_ref[...] = grad_hidden
    fold_heads(dot_nt(grad_hidden.astype(bf16), wo_ref[...]), parts(out_ref, len(halves)))

    head_in = (hidden * inverse * gain).astype(bf16)
    grad_head = dot_tn(head_in, grad_pred)
    if before is not None:
        grad_head = grad_head + before[0][...]
        loss = loss + before[1][0:1, :]
    if not last:
        refs[2][...] = grad_head
        refs[3][...] = jnp.broadcast_to(loss, (8, 128))
        return
    pieces = jnp.concatenate(list(split3(loss)) + [jnp.zeros((13, 128), f32)], 0).astype(bf16)
    sent_ref = refs[2]
    for b in range(BANDS):
        sent_ref[b, :HEAD_ROWS, :] = grad_head[b * HEAD_ROWS : (b + 1) * HEAD_ROWS].astype(bf16)
        sent_ref[b, HEAD_ROWS:, :] = pieces


def share_kernel(sent_ref, out_ref):
    grad = jnp.zeros((HEAD_ROWS, CH), f32)
    loss = jnp.zeros((16, 128), f32)
    for b in range(BANDS):
        grad = grad + sent_ref[b, :HEAD_ROWS, :].astype(f32)
        loss = loss + sent_ref[b, HEAD_ROWS:, :].astype(f32)
    loss = jnp.sum(loss, axis=0, keepdims=True)
    pieces = jnp.concatenate(list(split3(loss)) + [jnp.zeros((13, 128), f32)], 0).astype(bf16)
    grad = grad.astype(bf16)
    for j in range(MEMBERS):
        out_ref[j, :HEAD_ROWS, :] = grad
        out_ref[j, HEAD_ROWS:, :] = pieces


def total_kernel(shared_ref, grad_ref, loss_ref):
    grad = jnp.zeros((HEAD_ROWS, CH), f32)
    loss = jnp.zeros((16, 128), f32)
    for j in range(MEMBERS):
        grad = grad + shared_ref[j, :HEAD_ROWS, :].astype(f32)
        loss = loss + shared_ref[j, HEAD_ROWS:, :].astype(f32)
    grad_ref[...] = grad
    loss_ref[...] = jnp.sum(jnp.sum(loss, axis=0, keepdims=True), axis=1, keepdims=True)


def backward_kernel(counts_ref, kvx_ref, kvt_ref, q_ref, g_ref, exact_ref, dq_ref, acc_ref):
    acc_ref[...] = jnp.zeros((128, COLS), f32)
    low, lane = low_lanes(CAP), lanes(CAP)

    def band(b, start, rel):
        q = unfold(q_ref[b])
        g = unfold(g_ref[b])
        exact = exact_ref[b]
        inner = jnp.broadcast_to(
            jnp.sum(jnp.where(low, g * exact, 0.0), axis=1, keepdims=True), (CAP, 128)
        )
        right = query_columns(q, swap(exact))
        both = jnp.where(low, q, swap(g)).T.astype(bf16)
        side = jnp.zeros((CAP, 128), f32)
        for j, piece in enumerate(split3(-inner)):
            side = jnp.where(lane == j, piece, side)
        up = jnp.concatenate([jnp.where(low, 0.0, swap(g)), side], 1).astype(bf16)
        dq = jnp.zeros((HEAD, CAP), f32)
        for first, size in STEPS:
            span = pl.ds(pl.multiple_of(start + first, 128), size)
            kvx = kvx_ref[span, :]
            p = masked(jnp.exp2(dot_nt(kvx, right)), first, size, rel)
            ds = (p * dot_nt(kvx, up)).astype(bf16)
            acc_ref[:HEAD, span] += dot_nt(both[:HEAD], ds)
            acc_ref[HEAD:, span] += dot_nt(both[HEAD:], p.astype(bf16))
            dq = dq + dot(kvt_ref[:HEAD, span], ds)
        dq = jnp.concatenate([dq * 0.125, jnp.zeros((HEAD, CAP), f32)], 0).T
        dq_ref[b] = refold(dq).astype(bf16)

    each_band(counts_ref, band)


def give_kernel(counts_ref, acc_ref, out_ref, rows_ref):
    for t in range(R // 128, (R + BANDS * CAP) // 128 + 1):
        rows_ref[t * 128 : t * 128 + 128, :] = acc_ref[:, t * 128 : t * 128 + 128].T
    sub = lax.broadcasted_iota(jnp.int32, (1, 8, 128), 1)
    row = lax.broadcasted_iota(jnp.int32, (CAP, 128), 0)

    def give(b, off):
        count = counts_ref[b]
        shift = off & 7
        base = pl.multiple_of(off - shift + R, 8)
        x = rows_ref[pl.ds(base, 264), :].reshape(33, 8, 128)
        turned = pltpu.roll(x, (8 - shift) & 7, axis=1)
        x = jnp.where(sub + shift < 8, turned[:32], turned[1:]).reshape(CAP, 128)
        out_ref[b] = jnp.where(row < count, x, 0.0).astype(bf16)
        return off + count

    lax.fori_loop(0, BANDS, give, jnp.int32(0))


def grad_q_kernel(*refs):
    *dq_refs, wq_ref, out_ref, rows_ref = refs
    unfold_heads([part for ref in dq_refs for part in parts(ref, 2 // len(dq_refs))], rows_ref)
    out_ref[...] = dot_nt(rows_ref[...], wq_ref[...])


def latent_kernel(*refs):
    d_ref, part_ref, lat_ref, gain_ref, wk_ref, wv_ref, *grad_refs, out_ref, dk_ref, dv_ref = refs
    low = low_lanes(CAP)
    for pair in range(HEADS // 2):
        cols = slice(pair * 128, pair * 128 + 128)
        first = d_ref[2 * pair].astype(f32)
        second = d_ref[2 * pair + 1].astype(f32)
        dk_ref[:, cols] = jnp.where(low, first, swap(second)).astype(bf16)
        dv_ref[:, cols] = jnp.where(low, swap(first), second).astype(bf16)
    normed = (
        part_ref[...] + dot_nt(dk_ref[...], wk_ref[...]) + dot_nt(dv_ref[...], wv_ref[...])
    )
    x = lat_ref[...].astype(f32)
    out = norm_backward(x, inverse_rms(x), normed * gain_ref[...])
    rows = CAP // len(grad_refs)
    for i, ref in enumerate(grad_refs):
        part = slice(i * rows, i * rows + rows)
        out_ref[part, :] = (ref[...] + out[part]).astype(bf16)


VMEM_MIB = dict(
    keys=12, queries=8, compact=16, forward=16, head=12, loss=20, share=4, total=2, backward=24,
    give=12, grad_q=10, latent=20,
)


def call(name, kernel, outs, scalars, arrays, scratch=()):
    vmem = pl.BlockSpec(memory_space=pltpu.VMEM)
    smem = pl.BlockSpec(memory_space=pltpu.SMEM)
    return pl.pallas_call(
        kernel,
        out_shape=tuple(jax.ShapeDtypeStruct(s, d) for s, d in outs),
        in_specs=[smem] * len(scalars) + [vmem] * len(arrays),
        out_specs=tuple(vmem for _ in outs),
        scratch_shapes=[pltpu.VMEM(s, d) for s, d in scratch],
        compiler_params=pltpu.CompilerParams(vmem_limit_bytes=VMEM_MIB[name] << 20),
        name=name,
    )(*scalars, *arrays)


def exchange(x, axis):
    return lax.all_to_all(x, axis, split_axis=0, concat_axis=0, tiled=True)


STREAMS = ((0, 1),)


def body(
    latent, observed, area_weight, counts, gain_attn, w_query, w_key, w_value, w_out, gain_head, w_head
):
    members, cap, width = latent.shape
    lat = latent.reshape(cap, width)
    gain_a = gain_attn.reshape(1, width)
    gain_h = gain_head.reshape(1, width)
    area = area_weight.reshape(2, 128)
    place = jnp.stack([lax.axis_index("member"), lax.axis_index("band")]).astype(jnp.int32)

    def rows(x, halves):
        return x[halves[0] * HALF : (halves[-1] + 1) * HALF]

    kv, normed = call(
        "keys", keys_kernel, [((HEADS, cap, 128), bf16), ((cap, width), bf16)], [], [lat, gain_a, w_key, w_value]
    )
    kv = exchange(kv, "band")
    packed = [((HEADS, 64 * len(halves), 128), bf16) for halves in STREAMS]
    qs = call("queries", queries_kernel, packed, [], [normed, w_query])
    qs = [exchange(q, "band") for q in qs]
    keys = call(
        "compact",
        compact_kernel,
        [((COLS, DEPTH), bf16), ((TURNED, COLS), bf16)],
        [counts],
        [kv],
        [((COLS, 128), f32)],
    )
    mixed, exact = [], []
    for i, halves in enumerate(STREAMS):
        m, e = call(
            "forward",
            forward_kernel,
            [packed[i], ((BANDS, CAP, 128), f32)],
            [counts],
            [*keys, qs[i]],
        )
        mixed.append(exchange(m, "band"))
        exact.append(e)
    hidden, predicted = [], []
    for i, halves in enumerate(STREAMS):
        h, p = call(
            "head",
            functools.partial(head_kernel, halves),
            [((HALF * len(halves), width), f32), ((MEMBERS, HALF * len(halves), CH), bf16)],
            [],
            [mixed[i], rows(lat, halves), w_out, gain_h, w_head],
            [((HALF * len(halves), width), bf16)],
        )
        hidden.append(h)
        predicted.append(exchange(p, "member"))
    grad_hidden, gs, before = [], [], []
    for i, halves in enumerate(STREAMS):
        last = i == len(STREAMS) - 1
        extra = (
            [((BANDS, HEAD_ROWS + 16, 128), bf16)] if last else [((width, CH), f32), ((8, 128), f32)]
        )
        gh, g, *before = call(
            "loss",
            functools.partial(loss_kernel, halves, last),
            [((HALF * len(halves), width), f32), packed[i]] + extra,
            [place, counts],
            [predicted[i], rows(observed, halves), area, hidden[i], gain_h, w_head, w_out] + before,
        )
        grad_hidden.append(gh)
        gs.append(exchange(g, "band"))
    sent = exchange(before[0], "band")
    dqs, acc = [], []
    for i, halves in enumerate(STREAMS):
        dq, *acc = call(
            "backward",
            backward_kernel,
            [packed[i], ((128, COLS), f32)],
            [counts],
            [*keys, qs[i], gs[i], exact[i]],
        )
        dqs.append(exchange(dq, "band"))
    (shared,) = call("share", share_kernel, [((MEMBERS, HEAD_ROWS + 16, 128), bf16)], [], [sent])
    shared = exchange(shared, "member")
    (dkv,) = call(
        "give", give_kernel, [((BANDS, cap, 128), bf16)], [counts], acc, [((COLS, 128), f32)]
    )
    dkv = exchange(dkv, "band")
    (part,) = call(
        "grad_q", grad_q_kernel, [((cap, width), f32)], [], dqs + [w_query], [((cap, width), bf16)]
    )
    grad_head, loss = call(
        "total", total_kernel, [((HEAD_ROWS, CH), f32), ((1, 1), f32)], [], [shared]
    )
    (grad_latent,) = call(
        "latent",
        latent_kernel,
        [((cap, width), bf16)],
        [],
        [dkv, part, lat, gain_a, w_key, w_value] + grad_hidden,
        [((cap, width), bf16)] * 2,
    )
    return grad_latent.reshape(latent.shape), grad_head, loss.reshape(())


def solution(mesh):
    rows = P("member", "band", None)
    placed = (rows, P("band", None), P("band")) + (P(),) * 8
    return jax.shard_map(
        body,
        mesh=mesh,
        in_specs=placed,
        out_specs=(rows, P("band", None), P()),
        check_vma=False,
    )
```

time: 182 us -> 212 us (1.16)
  blocking collectives: 63.6 us -> 25.4 us
  local copies, waits for them, and re-layouts: 1.96 us -> 33.2 us
  waiting for transfers between devices: 33.5 us -> 61.9 us
  starting transfers between devices: 12.5 us -> 31.9 us
  Pallas kernels: 68.9 us -> 57.4 us
    all_to_all x3 -> x2, blocking collectives: 63.6 us -> 25.4 us  [exchange(): return lax.all_to_all(x, axis, split_axis=0, concat_axis=0, tiled=True)]
    unnamed x6 -> x82, local copies, waits for them, and re-layouts: 1.96 us -> 33.2 us
    all_to_all x3 -> x7, waiting for transfers between devices: 33.5 us -> 61.9 us  [exchange(): return lax.all_to_all(x, axis, split_axis=0, concat_axis=0, tiled=True)]
    all_to_all x3 -> x7, starting transfers between devices: 12.5 us -> 31.9 us  [exchange(): return lax.all_to_all(x, axis, split_axis=0, concat_axis=0, tiled=True)]
    pallas_call x8 -> x12, Pallas kernels: 68.9 us -> 57.4 us  [call(): pl.pallas_call(kernel, out_shape=tuple((jax.ShapeDtypeStruct(s, d) for s,...]
  transfers between devices with their start and end apart: 3 -> 7, of which waited for: 2 -> 6; matrix products, arithmetic and copies ran while one was open for 0% -> 0% of each run, Pallas kernels for 15% -> 17%
where the time goes in v2:
time: 212 us; the launch traced here: 211 us
  waiting for transfers between devices  61.9 us (29%)
  Pallas kernels  57.4 us (27%)
  local copies, waits for them, and re-layouts  33.2 us (16%)
  starting transfers between devices  31.9 us (15%)
  blocking collectives  25.4 us (12%)
    all_to_all x7, waiting for transfers between devices, exchange(): return lax.all_to_all(x, axis, split_axis=0, concat_axis=0, tiled=True)  61.9 us
    pallas_call x12, Pallas kernels, call(): pl.pallas_call(kernel, out_shape=tuple((jax.ShapeDtypeStruct(s, d) for s,...  57.4 us
    unnamed x82, local copies, waits for them, and re-layouts  33.2 us
    all_to_all x7, starting transfers between devices, exchange(): return lax.all_to_all(x, axis, split_axis=0, concat_axis=0, tiled=True)  31.9 us
    all_to_all x2, blocking collectives, exchange(): return lax.all_to_all(x, axis, split_axis=0, concat_axis=0, tiled=True)  25.4 us
  transfers between devices with their start and end apart: 7, of which 6 were waited for; matrix products, arithmetic and copies ran while one was open for 0% of the time, Pallas kernels for 17%

profile of v2, /device:TPU:0, one launch (start us, length us, event | category | flops | bytes accessed | tf_op | source)
XLA Modules:
  0.0 210.8 jit_solution(602013833967314587)
XLA Ops:
  0.6 1.6 copy-done.4
  2.2 1.6 copy-done.6
  5.5 1.5 keys.1
  8.9 7.3 %all-to-all-start = ((bf16[16,256,128]{2,1,0:T(8,128)(2,1)}), bf16[16,256,128]{2,1,0:T(8,128)(2,1)S(1)}, u32[]{:S(2)}, u32[]{:S(2)}) async-start(bf16[16,256,128]{2,1,0:T(8,128)(2,1)} %copy-done.23), calls=%async_computation | async-start | bytes 2097152 | tf_op jit(solution)/shard_map/all_to_all | solution.py:422
  18.8 15.1 %all-to-all-done.kv_ref = bf16[16,256,128]{2,1,0:T(8,128)(2,1)S(1)} async-done(((bf16[16,256,128]{2,1,0:T(8,128)(2,1)}), bf16[16,256,128]{2,1,0:T(8,128)(2,1)S(1)}, u32[]{:S(2)}, u32[]{:S(2)}) %all-to-all-start) | async-done | bytes 1048608 | tf_op jit(solution)/shard_map/all_to_all | solution.py:422
  35.0 3.6 %all-to-all-start.1 = ((bf16[16,128,128]{2,1,0:T(8,128)(2,1)}), bf16[16,128,128]{2,1,0:T(8,128)(2,1)S(1)}, u32[]{:S(2)}, u32[]{:S(2)}) async-start(bf16[16,128,128]{2,1,0:T(8,128)(2,1)} %copy-done.22), calls=%async_computation.1 | async-start | bytes 1048576 | tf_op jit(solution)/shard_map/all_to_all | solution.py:422
  39.8 2.1 compact.1
  43.0 5.6 %all-to-all-done.1.q_ref = bf16[16,128,128]{2,1,0:T(8,128)(2,1)S(1)} async-done(((bf16[16,128,128]{2,1,0:T(8,128)(2,1)}), bf16[16,128,128]{2,1,0:T(8,128)(2,1)S(1)}, u32[]{:S(2)}, u32[]{:S(2)}) %all-to-all-start.1) | async-done | bytes 524320 | tf_op jit(solution)/shard_map/all_to_all | solution.py:422
  48.6 1.4 copy-done.9
  50.0 12.5 %forward.1 = (bf16[16,128,128]{2,1,0:T(8,128)(2,1)S(1)}, f32[16,256,128]{2,1,0:T(8,128)S(1)}) custom-call(s32[16]{0:T(128)S(1)} %copy-done.39, bf16[5248,256]{1,0:T(8,128)(2,1)S(1)} %get-tuple-element.19.kvx_ref, bf16[144,5248]{1,0:T(8,128)(2,1)S(1)} %copy-done.9, bf16[16,128,128]{2,1,0:T(8,128)(2,1)S(1)} %all-to-all-done.1.q_ref), custom_call_target="tpu_custom_call" | custom-call | tf_op jit(solution)/shard_map/forward/pallas_call | solution.py:410
  62.5 13.3 %all_to_all.45.mixed_ref = bf16[16,128,128]{2,1,0:T(8,128)(2,1)S(1)} all-to-all(bf16[16,128,128]{2,1,0:T(8,128)(2,1)S(1)} %get-tuple-element.22), channel_id=1, replica_groups=mesh['member'=8,'band'=16] {'band'}, dimensions={0} | all-to-all | bytes 1048576 | tf_op jit(solution)/shard_map/all_to_all | solution.py:422
  78.8 5.3 %all-to-all-start.3 = ((bf16[8,256,128]{2,1,0:T(8,128)(2,1)}), bf16[8,256,128]{2,1,0:T(8,128)(2,1)}, u32[]{:S(2)}, u32[]{:S(2)}) async-start(bf16[8,256,128]{2,1,0:T(8,128)(2,1)} %copy-done.30), calls=%async_computation.3 | async-start | bytes 1048576 | tf_op jit(solution)/shard_map/all_to_all | solution.py:422
  84.2 10.3 %all-to-all-done.3.pred_ref = bf16[8,256,128]{2,1,0:T(8,128)(2,1)} async-done(((bf16[8,256,128]{2,1,0:T(8,128)(2,1)}), bf16[8,256,128]{2,1,0:T(8,128)(2,1)}, u32[]{:S(2)}, u32[]{:S(2)}) %all-to-all-start.3) | async-done | bytes 524320 | tf_op jit(solution)/shard_map/all_to_all | solution.py:422
  94.6 1.6 copy-done.3
  97.4 2.9 %loss.1 = (f32[256,1024]{1,0:T(8,128)S(1)}, bf16[16,128,128]{2,1,0:T(8,128)(2,1)S(1)}, bf16[16,80,128]{2,1,0:T(8,128)(2,1)S(1)}) custom-call(s32[2]{0:T(128)S(1)} %pad_add_fusion.place_ref, s32[16]{0:T(128)S(1)} %copy-done.39, bf16[8,256,128]{2,1,0:T(8,128)(2,1)} %all-to-all-done.3.pred_ref, bf16[256,128]{1,0:T(8,128)(2,1)S(1)} %copy-done.35, ...), custom_call_target="tpu_custom_call" | custom-call | tf_op jit(solution)/shard_map/loss/pallas_call | solution.py:410
  101.3 12.1 %all_to_all.46.sent_ref = bf16[16,80,128]{2,1,0:T(8,128)(2,1)S(1)} all-to-all(bf16[16,80,128]{2,1,0:T(8,128)(2,1)S(1)} %get-tuple-element.30), channel_id=1, replica_groups=mesh['member'=8,'band'=16] {'band'}, dimensions={0} | all-to-all | bytes 655360 | tf_op jit(solution)/shard_map/all_to_all | solution.py:422
  113.4 4.3 %all-to-all-start.4 = ((bf16[16,128,128]{2,1,0:T(8,128)(2,1)}), bf16[16,128,128]{2,1,0:T(8,128)(2,1)}, u32[]{:S(2)}, u32[]{:S(2)}) async-start(bf16[16,128,128]{2,1,0:T(8,128)(2,1)} %copy-done.32), calls=%async_computation.4 | async-start | bytes 1048576 | tf_op jit(solution)/shard_map/all_to_all | solution.py:422
  118.4 9.4 %all-to-all-done.4.g_ref = bf16[16,128,128]{2,1,0:T(8,128)(2,1)} async-done(((bf16[16,128,128]{2,1,0:T(8,128)(2,1)}), bf16[16,128,128]{2,1,0:T(8,128)(2,1)}, u32[]{:S(2)}, u32[]{:S(2)}) %all-to-all-start.4) | async-done | bytes 524320 | tf_op jit(solution)/shard_map/all_to_all | solution.py:422
  127.8 3.4 %all-to-all-start.8 = ((bf16[8,80,128]{2,1,0:T(8,128)(2,1)}), bf16[8,80,128]{2,1,0:T(8,128)(2,1)S(1)}, u32[]{:S(2)}, u32[]{:S(2)}) async-start(bf16[8,80,128]{2,1,0:T(8,128)(2,1)} %copy-done.29), calls=%async_computation.8 | async-start | bytes 327680 | tf_op jit(solution)/shard_map/all_to_all | solution.py:422
  131.2 1.4 copy-done.10
  132.6 1.6 copy-done.21
  134.2 28.6 %backward.1 = (bf16[16,128,128]{2,1,0:T(8,128)(2,1)S(1)}, f32[128,5248]{1,0:T(8,128)S(1)}) custom-call(s32[16]{0:T(128)S(1)} %copy-done.39, bf16[5248,256]{1,0:T(8,128)(2,1)S(1)} %get-tuple-element.19.kvx_ref, bf16[144,5248]{1,0:T(8,128)(2,1)S(1)} %copy-done.10, bf16[16,128,128]{2,1,0:T(8,128)(2,1)S(1)} %all-to-all-done.1.q_ref, ...), custom_call_target="tpu_custom_call" | custom-call | tf_op jit(solution)/shard_map/backward/pallas_call | solution.py:410
  162.8 1.5 copy-done.18
  165.1 3.8 %all-to-all-start.6 = ((bf16[16,128,128]{2,1,0:T(8,128)(2,1)}), bf16[16,128,128]{2,1,0:T(8,128)(2,1)S(1)}, u32[]{:S(2)}, u32[]{:S(2)}) async-start(bf16[16,128,128]{2,1,0:T(8,128)(2,1)} %copy-done.31), calls=%async_computation.6 | async-start | bytes 1048576 | tf_op jit(solution)/shard_map/all_to_all | solution.py:422
  168.9 1.7 copy-done.19
  170.6 2.6 %give.1 = bf16[16,256,128]{2,1,0:T(8,128)(2,1)} custom-call(s32[16]{0:T(128)S(1)} %copy-done.39, f32[128,5248]{1,0:T(8,128)S(1)} %copy-done.19), custom_call_target="tpu_custom_call" | custom-call | tf_op jit(solution)/shard_map/give/pallas_call | solution.py:410
  173.2 7.8 %all-to-all-done.6.refs_0_ = bf16[16,128,128]{2,1,0:T(8,128)(2,1)S(1)} async-done(((bf16[16,128,128]{2,1,0:T(8,128)(2,1)}), bf16[16,128,128]{2,1,0:T(8,128)(2,1)S(1)}, u32[]{:S(2)}, u32[]{:S(2)}) %all-to-all-start.6) | async-done | bytes 524320 | tf_op jit(solution)/shard_map/all_to_all | solution.py:422
  181.0 4.3 %all-to-all-start.5 = ((bf16[16,256,128]{2,1,0:T(8,128)(2,1)}), bf16[16,256,128]{2,1,0:T(8,128)(2,1)}, u32[]{:S(2)}, u32[]{:S(2)}) async-start(bf16[16,256,128]{2,1,0:T(8,128)(2,1)} %give.1), calls=%async_computation.5 | async-start | bytes 2097152 | tf_op jit(solution)/shard_map/all_to_all | solution.py:422
  187.8 13.7 %all-to-all-done.5.refs_0_ = bf16[16,256,128]{2,1,0:T(8,128)(2,1)} async-done(((bf16[16,256,128]{2,1,0:T(8,128)(2,1)}), bf16[16,256,128]{2,1,0:T(8,128)(2,1)}, u32[]{:S(2)}, u32[]{:S(2)}) %all-to-all-start.5) | async-done | bytes 1048608 | tf_op jit(solution)/shard_map/all_to_all | solution.py:422
  201.5 1.6 copy-done.5
  203.1 1.6 copy-done.7
  207.1 3.7 %latent.1 = bf16[256,1024]{1,0:T(8,128)(2,1)} custom-call(bf16[16,256,128]{2,1,0:T(8,128)(2,1)} %all-to-all-done.5.refs_0_, f32[256,1024]{1,0:T(8,128)S(1)} %copy-done.17, bf16[256,1024]{1,0:T(8,128)(2,1)S(1)} %bitcast.10, f32[1,1024]{1,0:T(1,128)S(1)} %bitcast.14, bf16[1024,1024]{1,0:T(8,128)(2,1)S(1)} %copy-done.5, bf16[1024,1024]{1,0:T(8,128)(2,1)S(1)} %copy-done.7, ...), custom_call_target="tpu_custom_call" | custom-call | tf_op jit(solution)/shard_map/latent/pallas_call | solution.py:410
  (79 shorter events, 21.1 us)
Async XLA Ops:
  0.6 1.6 copy-start.4
  2.2 1.6 copy-start.6
  8.9 7.3 %copy-start = (bf16[1024,1024]{1,0:T(8,128)(2,1)S(1)}, bf16[1024,1024]{1,0:T(8,128)(2,1)}, u32[]{:S(2)}) copy-start(bf16[1024,1024]{1,0:T(8,128)(2,1)} %refs_1_.1) | copy-start | bytes 6291460
  8.9 25.0 %all-to-all-start = ((bf16[16,256,128]{2,1,0:T(8,128)(2,1)}), bf16[16,256,128]{2,1,0:T(8,128)(2,1)S(1)}, u32[]{:S(2)}, u32[]{:S(2)}) async-start(bf16[16,256,128]{2,1,0:T(8,128)(2,1)} %copy-done.23), calls=%async_computation | async-start | bytes 2097152 | tf_op jit(solution)/shard_map/all_to_all | solution.py:422
  17.3 21.3 %copy-start.39 = (s32[16]{0:T(128)S(1)}, s32[16]{0:T(128)}, u32[]{:S(2)}) copy-start(s32[16]{0:T(128)} %counts_ref.9) | copy-start | bytes 196
  35.0 13.6 %all-to-all-start.1 = ((bf16[16,128,128]{2,1,0:T(8,128)(2,1)}), bf16[16,128,128]{2,1,0:T(8,128)(2,1)S(1)}, u32[]{:S(2)}, u32[]{:S(2)}) async-start(bf16[16,128,128]{2,1,0:T(8,128)(2,1)} %copy-done.22), calls=%async_computation.1 | async-start | bytes 1048576 | tf_op jit(solution)/shard_map/all_to_all | solution.py:422
  38.6 1.2 copy-start.15
  48.6 1.4 copy-start.9
  50.0 25.8 %copy-start.2 = (bf16[1024,1024]{1,0:T(8,128)(2,1)S(1)}, bf16[1024,1024]{1,0:T(8,128)(2,1)}, u32[]{:S(2)}) copy-start(bf16[1024,1024]{1,0:T(8,128)(2,1)} %wo_ref.3) | copy-start | bytes 6291460
  50.0 25.8 %copy-start.12 = (bf16[1,256,1024]{2,1,0:T(8,128)(2,1)S(1)}, bf16[1,256,1024]{2,1,0:T(8,128)(2,1)}, u32[]{:S(2)}) copy-start(bf16[1,256,1024]{2,1,0:T(8,128)(2,1)} %param.11) | copy-start | bytes 1572868
  50.0 25.8 %copy-start.26 = (bf16[1024,128]{1,0:T(8,128)(2,1)S(1)}, bf16[1024,128]{1,0:T(8,128)(2,1)}, u32[]{:S(2)}) copy-start(bf16[1024,128]{1,0:T(8,128)(2,1)} %wh_ref.3) | copy-start | bytes 786436
  50.0 25.8 %copy-start.36 = (f32[1024]{0:T(1024)S(1)}, f32[1024]{0:T(1024)}, u32[]{:S(2)}) copy-start(f32[1024]{0:T(1024)} %param.20) | copy-start | bytes 12292
  62.5 14.5 %copy-start.20 = (f32[16,256,128]{2,1,0:T(8,128)}, f32[16,256,128]{2,1,0:T(8,128)S(1)}, u32[]{:S(2)}) copy-start(f32[16,256,128]{2,1,0:T(8,128)S(1)} %get-tuple-element.26.exact_ref) | copy-start | bytes 6291460
  75.9 18.7 %copy-start.35 = (bf16[256,128]{1,0:T(8,128)(2,1)S(1)}, bf16[256,128]{1,0:T(8,128)(2,1)}, u32[]{:S(2)}) copy-start(bf16[256,128]{1,0:T(8,128)(2,1)} %obs_ref.1) | copy-start | bytes 196612
  75.9 18.7 %copy-start.40 = (f32[256]{0:T(256)S(1)}, f32[256]{0:T(256)}, u32[]{:S(2)}) copy-start(f32[256]{0:T(256)} %param.13) | copy-start | bytes 3076
  78.8 15.7 %all-to-all-start.3 = ((bf16[8,256,128]{2,1,0:T(8,128)(2,1)}), bf16[8,256,128]{2,1,0:T(8,128)(2,1)}, u32[]{:S(2)}, u32[]{:S(2)}) async-start(bf16[8,256,128]{2,1,0:T(8,128)(2,1)} %copy-done.30), calls=%async_computation.3 | async-start | bytes 1048576 | tf_op jit(solution)/shard_map/all_to_all | solution.py:422
  94.6 1.6 copy-start.3
  96.1 1.2 copy-start.25
  101.3 12.1 %copy-start.32 = (bf16[16,128,128]{2,1,0:T(8,128)(2,1)}, bf16[16,128,128]{2,1,0:T(8,128)(2,1)S(1)}, u32[]{:S(2)}) copy-start(bf16[16,128,128]{2,1,0:T(8,128)(2,1)S(1)} %get-tuple-element.25) | copy-start | bytes 1572868
  113.4 14.4 %all-to-all-start.4 = ((bf16[16,128,128]{2,1,0:T(8,128)(2,1)}), bf16[16,128,128]{2,1,0:T(8,128)(2,1)}, u32[]{:S(2)}, u32[]{:S(2)}) async-start(bf16[16,128,128]{2,1,0:T(8,128)(2,1)} %copy-done.32), calls=%async_computation.4 | async-start | bytes 1048576 | tf_op jit(solution)/shard_map/all_to_all | solution.py:422
  127.8 37.3 %all-to-all-start.8 = ((bf16[8,80,128]{2,1,0:T(8,128)(2,1)}), bf16[8,80,128]{2,1,0:T(8,128)(2,1)S(1)}, u32[]{:S(2)}, u32[]{:S(2)}) async-start(bf16[8,80,128]{2,1,0:T(8,128)(2,1)} %copy-done.29), calls=%async_computation.8 | async-start | bytes 327680 | tf_op jit(solution)/shard_map/all_to_all | solution.py:422
  131.2 1.4 copy-start.10
  132.6 1.6 copy-start.21
  162.8 1.5 copy-start.18
  165.1 15.9 %all-to-all-start.6 = ((bf16[16,128,128]{2,1,0:T(8,128)(2,1)}), bf16[16,128,128]{2,1,0:T(8,128)(2,1)S(1)}, u32[]{:S(2)}, u32[]{:S(2)}) async-start(bf16[16,128,128]{2,1,0:T(8,128)(2,1)} %copy-done.31), calls=%async_computation.6 | async-start | bytes 1048576 | tf_op jit(solution)/shard_map/all_to_all | solution.py:422
  168.9 1.8 copy-start.19
  170.6 15.4 %copy-start.1 = (bf16[1024,1024]{1,0:T(8,128)(2,1)S(1)}, bf16[1024,1024]{1,0:T(8,128)(2,1)}, u32[]{:S(2)}) copy-start(bf16[1024,1024]{1,0:T(8,128)(2,1)} %refs_1_.1) | copy-start | bytes 6291460
  181.0 20.5 %all-to-all-start.5 = ((bf16[16,256,128]{2,1,0:T(8,128)(2,1)}), bf16[16,256,128]{2,1,0:T(8,128)(2,1)}, u32[]{:S(2)}, u32[]{:S(2)}) async-start(bf16[16,256,128]{2,1,0:T(8,128)(2,1)} %give.1), calls=%async_computation.5 | async-start | bytes 2097152 | tf_op jit(solution)/shard_map/all_to_all | solution.py:422
  185.3 16.1 %copy-start.13 = (bf16[1,256,1024]{2,1,0:T(8,128)(2,1)S(1)}, bf16[1,256,1024]{2,1,0:T(8,128)(2,1)}, u32[]{:S(2)}) copy-start(bf16[1,256,1024]{2,1,0:T(8,128)(2,1)} %param.11) | copy-start | bytes 1572868
  185.3 16.1 %copy-start.38 = (f32[1024]{0:T(1024)S(1)}, f32[1024]{0:T(1024)}, u32[]{:S(2)}) copy-start(f32[1024]{0:T(1024)} %param.15) | copy-start | bytes 12292
  201.5 1.6 copy-start.5
  203.1 1.6 copy-start.7
  (16 other events, 15.2 us)

commit v3 on v2

v3 whole, which is shorter than its diff:
```python
import jax
import jax.numpy as jnp
from jax import lax
from jax.experimental import pallas as pl
from jax.experimental.pallas import tpu as pltpu
from jax.sharding import PartitionSpec as P


HEADS = 16
HEAD = 64
CH = 128
R = 512
CAP = 256
MEMBERS = 8
BANDS = 16
LOG2E = 1.4426950408889634
EPS = 1e-06
SMOOTH = 0.0625
FAIR = 1.0 - 0.05 / MEMBERS
PAIR_SCALE = FAIR / (MEMBERS * (MEMBERS - 1.0))

HALF = CAP // 2
WIDTH = 2 * R + CAP + 128
ROWS = BANDS * CAP - CAP + WIDTH
EDGE = CAP + 128
CHUNKS = ((0, 512), (512, 512), (1024, 384))
TURNED = 144
DEAD = -32768.0
HEAD_ROWS = 64

f32 = jnp.float32
bf16 = jnp.bfloat16


def dot(a, b):
    return lax.dot_general(a, b, (((1,), (0,)), ((), ())), preferred_element_type=f32)


def dot_tn(a, b):
    return lax.dot_general(a, b, (((0,), (0,)), ((), ())), preferred_element_type=f32)


def swap(x):
    return pltpu.roll(x, HEAD, axis=1)


def low_lanes(rows):
    return lax.broadcasted_iota(jnp.int32, (rows, 128), 1) < HEAD


def fold(first, second):
    low = low_lanes(64)
    return jnp.where(low, first, swap(second)), jnp.where(low, swap(first), second)


def unfold(packed):
    packed = packed.astype(f32)
    other = swap(packed)
    return jnp.concatenate([packed[:64], other[:64], packed[64:], other[64:]], 0)


def refold(rows):
    return jnp.concatenate(
        [jnp.concatenate([rows[i : i + 64], rows[i + 64 : i + 128]], 1) for i in (0, 128)], 0
    )


def split3(x):
    high = x.astype(bf16).astype(f32)
    middle = (x - high).astype(bf16).astype(f32)
    return high, middle, (x - high - middle).astype(bf16).astype(f32)


def inverse_rms(x):
    return lax.rsqrt(jnp.mean(x * x, axis=-1, keepdims=True) + EPS)


def norm_backward(x, inverse, scaled):
    return inverse * scaled - x * (inverse * inverse * inverse) * jnp.mean(
        x * scaled, axis=-1, keepdims=True
    )


def fetch(copies, sems):
    started = [pltpu.make_async_copy(a, b, sems.at[i]) for i, (a, b) in enumerate(copies)]
    for copy in started:
        copy.start()

    def wait(count):
        for _ in range(count):
            started.pop(0).wait()

    return wait


def project_kernel(
    gain_ref, lat_hbm, wq_hbm, wk_hbm, wv_hbm, out_ref, lat_ref, wq_ref, wk_ref, wv_ref, sems
):
    wait = fetch([(lat_hbm, lat_ref), (wk_hbm, wk_ref), (wv_hbm, wv_ref), (wq_hbm, wq_ref)], sems)
    wait(1)
    x = lat_ref[...].astype(f32)
    normed = (x * inverse_rms(x) * gain_ref[...]).astype(bf16)
    low = low_lanes(CAP)
    wait(2)
    for quad in range(4):
        cols = slice(quad * 256, quad * 256 + 256)
        k = dot(normed, wk_ref[:, cols])
        v = dot(normed, wv_ref[:, cols])
        for half in range(2):
            head = quad * 4 + half * 2
            part = slice(half * 128, half * 128 + 128)
            kp, vp = k[:, part], v[:, part]
            out_ref[head, 128:, :] = jnp.where(low, kp, swap(vp)).astype(bf16)
            out_ref[head + 1, 128:, :] = jnp.where(low, swap(kp), vp).astype(bf16)
    wait(1)
    fold_heads(dot(normed, wq_ref[...]) * 0.125, parts(out_ref, 2))


def fold_heads(x, refs):
    for i, ref in enumerate(refs):
        for pair in range(HEADS // 2):
            part = x[i * HALF : (i + 1) * HALF, pair * 128 : pair * 128 + 128]
            first, second = fold(part[:64], part[64:])
            ref[2 * pair, 0:64, :] = first.astype(bf16)
            ref[2 * pair + 1, 0:64, :] = second.astype(bf16)


def unfold_heads(refs, rows_ref):
    for i, ref in enumerate(refs):
        for pair in range(HEADS // 2):
            first, second = fold(ref[2 * pair, 0:64, :].astype(f32), ref[2 * pair + 1, 0:64, :].astype(f32))
            cols = slice(pair * 128, pair * 128 + 128)
            rows_ref[i * HALF : i * HALF + 64, cols] = first.astype(bf16)
            rows_ref[i * HALF + 64 : (i + 1) * HALF, cols] = second.astype(bf16)


def parts(ref, n):
    return [ref.at[:, i * 64 : i * 64 + 64, :] for i in range(n)]


def turn_kernel(*refs):
    n = (len(refs) - 2) // 3
    w_hbm, outs, w_refs = refs[:n], refs[n : 2 * n], refs[2 * n : 3 * n]
    turned_ref, sems = refs[3 * n :]
    wait = fetch(list(zip(w_hbm, w_refs)), sems)
    for k, (w_ref, out) in enumerate(zip(w_refs, outs)):
        wait(1)
        rows = w_ref.shape[0]
        to = out if k < 2 else turned_ref
        for i in range(0, rows, 128):
            to[:, i : i + 128] = w_ref[i : i + 128, :].astype(f32).T.astype(bf16)
        if k >= 2:
            fetch([(turned_ref, out)], sems)(1)


def offsets(counts_ref, off_ref):
    def step(b, off):
        off_ref[b] = off
        return off + counts_ref[b]

    total = lax.fori_loop(0, BANDS, step, jnp.int32(0))
    off_ref[BANDS] = total
    return total


def compact(counts_ref, off_ref, x_ref, total, kv_ref, side_ref, kvt_ref, rows_ref):
    sub = lax.broadcasted_iota(jnp.int32, (1, 8, 128), 1)
    row = lax.broadcasted_iota(jnp.int32, (CAP, 128), 0)
    rows_ref[...] = jnp.zeros((ROWS, 128), f32)

    def place(b, carry):
        off = off_ref[b]
        shift = off & 7
        base = pl.multiple_of(off - shift + R, 8)
        x = jnp.where(row < counts_ref[b], x_ref[b, 128:, :].astype(f32), 0.0)
        turned = pltpu.roll(x.reshape(32, 8, 128), shift, axis=1)
        before = rows_ref[pl.ds(base, 8), :].reshape(1, 8, 128)
        shifted = jnp.concatenate([before, turned], 0)
        turned = jnp.concatenate([turned, jnp.zeros((1, 8, 128), f32)], 0)
        rows_ref[pl.ds(base, 264), :] = jnp.where(sub < shift, shifted, turned).reshape(264, 128)
        return carry

    lax.fori_loop(0, BANDS, place, 0)
    kvt_ref[128:, :] = jnp.ones((TURNED - 128, ROWS), bf16)
    lane = lax.broadcasted_iota(jnp.int32, (128, 128), 1)
    none = jnp.where(lane == 0, DEAD, 0.0)
    tile_row = lax.broadcasted_iota(jnp.int32, (128, 128), 0)
    for t in range(ROWS // 128):
        span = slice(t * 128, t * 128 + 128)
        bias = none if t * 128 < R else jnp.where(tile_row >= total + (R - t * 128), none, 0.0)
        if R <= t * 128 < R + BANDS * CAP:
            tile = rows_ref[span, :]
            kv_ref[span, :] = tile.astype(bf16)
            side_ref[span, :] = jnp.where(lane < HEAD, bias, swap(tile)).astype(bf16)
            kvt_ref[:128, span] = tile.T.astype(bf16)
        else:
            kv_ref[span, :] = jnp.zeros((128, 128), bf16)
            side_ref[span, :] = bias.astype(bf16)
            kvt_ref[:128, span] = jnp.zeros((128, 128), bf16)


def window(off_ref, k):
    off = off_ref[k]
    return pl.multiple_of(off - (off & 127), 128), off & 127


def masked(e, first, least):
    gap = lax.broadcasted_iota(jnp.int32, (EDGE, CAP), 0) - lax.broadcasted_iota(
        jnp.int32, (EDGE, CAP), 1
    )
    if first == 0:
        return jnp.concatenate([jnp.where(gap >= least, e[:EDGE], 0.0), e[EDGE:]], 0)
    return e if first < 2 * R else jnp.where(gap <= least, e, 0.0)


def by_two(count, step):
    def two(i, carry):
        for j in range(2):
            step(2 * i + j, j)
        return carry

    lax.fori_loop(0, count // 2, two, 0)


def forward_kernel(counts_ref, x_ref, *refs):
    blocks = BANDS
    mixed_ref, inverse_ref, e_hbm, kv_hbm, kt_hbm, q_hbm, own_hbm = refs[:7]
    off_ref, kv_ref, side_ref, kvt_ref, rows_ref = refs[7:12]
    qx0, qx1, e0, e1, out0, out1, sems, e_sems = refs[-8:]
    qx, e_refs, outs = (qx0, qx1), (e0, e1), (out0, out1)
    q_ref = x_ref.at[:, pl.ds(0, 128), :]
    total = offsets(counts_ref, off_ref)
    compact(counts_ref, off_ref, x_ref, total, kv_ref, side_ref, kvt_ref, rows_ref)
    give = fetch([(kv_ref, kv_hbm), (kvt_ref.at[pl.ds(0, HEAD), :], kt_hbm), (q_ref, q_hbm)], sems)
    lane = lax.broadcasted_iota(jnp.int32, (CAP, 128), 1)
    low = lane < HEAD
    one = jnp.where(lane == 0, 1.0, 0.0)

    def prepare(k, slot):
        scaled = jnp.where(low, unfold(q_ref[k]), 0.0) * LOG2E
        high = scaled.astype(bf16).astype(f32)
        columns = jnp.concatenate([high, jnp.where(low, one, swap(scaled - high))], 1)
        qx[slot][...] = columns.T.astype(bf16)

    def copy(k, slot):
        return pltpu.make_async_copy(e_refs[slot], e_hbm.at[k], e_sems.at[slot])

    def finish(k, slot):
        out = outs[slot][...]
        inverse = 1.0 / out[HEAD : HEAD + 1, :]
        inverse_ref[pl.ds(k, 1), :] = inverse
        mixed_ref[k] = refold((out[:HEAD] * inverse).T).astype(bf16)

    prepare(0, 0)

    def step(k, j):
        other = 1 - j

        @pl.when(k > 1)
        def _():
            copy(k - 2, j).wait()

        start, least = window(off_ref, k)
        out = None
        for first, size in CHUNKS:
            span = pl.ds(pl.multiple_of(start + first, 128), size)
            rows = jnp.concatenate([kv_ref[span, :], side_ref[span, :]], 1)
            e = masked(jnp.exp2(dot(rows, qx[j][...])), first, least)
            e_refs[j][first : first + size, :] = e.astype(bf16)
            part = dot(kvt_ref[HEAD:, span], e_refs[j][first : first + size, :])
            out = part if out is None else out + part
        outs[j][...] = out
        finish(jnp.maximum(k - 1, 0), other)
        prepare(jnp.minimum(k + 1, blocks - 1), other)
        copy(k, j).start()

    by_two(blocks, step)
    finish(blocks - 1, 1)
    give(3)
    fetch([(mixed_ref, own_hbm)], sems)(1)
    copy(blocks - 2, 0).wait()
    copy(blocks - 1, 1).wait()


def head_kernel(
    mixed_ref, wo_ref, gain_ref, wh_ref, lat_hbm, pred_ref, hidden_hbm, rows_ref, lat_ref, hidden_ref, sems
):
    wait = fetch([(lat_hbm, lat_ref)], sems)
    unfold_heads(parts(mixed_ref, 2), rows_ref)
    hidden = dot(rows_ref[...], wo_ref[...])
    wait(1)
    hidden = hidden + lat_ref[...].astype(f32)
    hidden_ref[...] = hidden
    give = fetch([(hidden_ref, hidden_hbm)], sems)
    head_in = (hidden * inverse_rms(hidden) * gain_ref[...]).astype(bf16)
    predicted = dot(head_in, wh_ref[...]).astype(bf16)
    for j in range(MEMBERS):
        pred_ref[j] = predicted
    give(1)


def loss_kernel(
    counts_ref, pred_ref, area_ref, obs_ref, gain_ref, wh_ref, wo_ref, hidden_hbm,
    out_ref, sent_ref, grad_hbm, hidden_ref, grad_ref, sems,
):
    wait = fetch([(hidden_hbm, hidden_ref)], sems)
    me, band = lax.axis_index("member"), lax.axis_index("band")
    total = lax.fori_loop(0, BANDS, lambda b, t: t + counts_ref[b], jnp.int32(0))
    area = area_ref[...]
    weight = jnp.concatenate(
        [jnp.broadcast_to(area[i : i + 1, :], (128, 128)).T for i in range(2)], 0
    )
    row = lax.broadcasted_iota(jnp.int32, (CAP, CH), 0)
    weight = jnp.where(row < counts_ref[band], weight, 0.0) / (total.astype(f32) * CH)
    mine = pred_ref[me].astype(f32)

    def smooth(gap):
        square = gap * gap + SMOOTH
        inverse = lax.rsqrt(square)
        return square * inverse, gap * inverse

    size, slope = smooth(mine - obs_ref[...].astype(f32))
    pair_size = jnp.zeros((CAP, CH), f32)
    pair_slope = jnp.zeros((CAP, CH), f32)
    for k in range(MEMBERS):
        a, da = smooth(mine - pred_ref[k].astype(f32))
        pair_size = pair_size + jnp.where(me == k, 0.0, 1.0) * a
        pair_slope = pair_slope + da
    loss = jnp.sum(weight * (size / MEMBERS - (0.5 * PAIR_SCALE) * pair_size), axis=0, keepdims=True)
    grad_pred = (weight * (slope / MEMBERS - PAIR_SCALE * pair_slope)).astype(bf16)

    wait(1)
    hidden = hidden_ref[...]
    gain = gain_ref[...]
    inverse = inverse_rms(hidden)
    scaled = dot(grad_pred, wh_ref[...]) * gain
    grad_hidden = norm_backward(hidden, inverse, scaled)
    grad_ref[...] = grad_hidden
    give = fetch([(grad_ref, grad_hbm)], sems)
    fold_heads(dot(grad_hidden.astype(bf16), wo_ref[...]), parts(out_ref, 2))

    head_in = (hidden * inverse * gain).astype(bf16)
    grad_head = dot_tn(head_in, grad_pred)
    pieces = jnp.concatenate(list(split3(loss)) + [jnp.zeros((13, 128), f32)], 0).astype(bf16)
    for b in range(BANDS):
        sent_ref[b, :HEAD_ROWS, :] = grad_head[b * HEAD_ROWS : (b + 1) * HEAD_ROWS].astype(bf16)
        sent_ref[b, HEAD_ROWS:, :] = pieces
    give(1)


def share_kernel(sent_ref, out_ref):
    grad = jnp.zeros((HEAD_ROWS, CH), f32)
    loss = jnp.zeros((16, 128), f32)
    for b in range(BANDS):
        grad = grad + sent_ref[b, :HEAD_ROWS, :].astype(f32)
        loss = loss + sent_ref[b, HEAD_ROWS:, :].astype(f32)
    loss = jnp.sum(loss, axis=0, keepdims=True)
    pieces = jnp.concatenate(list(split3(loss)) + [jnp.zeros((13, 128), f32)], 0).astype(bf16)
    out_ref[:HEAD_ROWS, :] = grad.astype(bf16)
    out_ref[HEAD_ROWS:, :] = pieces


def total_kernel(me_ref, *refs):
    *shared_refs, grad_ref, loss_ref, all_ref = refs
    for k, ref in enumerate(shared_refs):
        all_ref[(me_ref[0] + MEMBERS - k) % MEMBERS] = ref[...]
    grad = jnp.zeros((HEAD_ROWS, CH), f32)
    loss = jnp.zeros((16, 128), f32)
    for j in range(MEMBERS):
        grad = grad + all_ref[j, :HEAD_ROWS, :].astype(f32)
        loss = loss + all_ref[j, HEAD_ROWS:, :].astype(f32)
    grad_ref[...] = grad
    loss_ref[...] = jnp.sum(jnp.sum(loss, axis=0, keepdims=True), axis=1, keepdims=True)


def backward_kernel(
    counts_ref, inverse_ref, q_hbm, g_hbm, mixed_hbm, kv_hbm, kt_hbm, p_hbm, out_hbm,
    off_ref, q_ref, g_ref, mixed_ref, kv_ref, kt_ref, acc_ref, dq_ref, dkv_ref,
    both0, both1, up0, up1, inner0, inner1, p0, p1, dq0, dq1, sems, p_sems, out_sems,
):
    blocks = BANDS
    boths, ups, inners, p_refs, dqs = (both0, both1), (up0, up1), (inner0, inner1), (p0, p1), (dq0, dq1)

    def copy(k, slot):
        return pltpu.make_async_copy(p_hbm.at[k], p_refs[slot], p_sems.at[slot])

    wait = fetch(
        [
            (q_hbm, q_ref),
            (g_hbm, g_ref),
            (mixed_hbm, mixed_ref),
            (kv_hbm, kv_ref),
            (kt_hbm, kt_ref),
        ],
        sems,
    )
    copy(0, 0).start()
    copy(1, 1).start()
    offsets(counts_ref, off_ref)
    acc_ref[...] = jnp.zeros((ROWS, 128), f32)
    low = low_lanes(CAP)

    def prepare(k, slot):
        q = unfold(q_ref[k])
        g = unfold(g_ref[k])
        mixed = unfold(mixed_ref[k])
        inner = jnp.sum(jnp.where(low, g * mixed, 0.0).T, axis=0, keepdims=True)
        inners[slot][...] = jnp.broadcast_to(inner, (8, CAP))
        boths[slot][:CAP, :] = jnp.where(low, q, 0.0).astype(bf16)
        g = jnp.where(low, 0.0, swap(g))
        boths[slot][CAP:, :] = g.astype(bf16)
        ups[slot][...] = g.T.astype(bf16)

    def finish(k, slot):
        dq_ref[k] = refold((dqs[slot][...] * 0.125).T).astype(bf16)

    wait(3)
    prepare(0, 0)
    wait(2)

    def step(k, j):
        other = 1 - j
        copy(k, j).wait()
        start, _ = window(off_ref, k)
        inner = inners[j][0:1, :]
        inverse = inverse_ref[pl.ds(k, 1), :]
        dq = None
        for first, size in CHUNKS:
            span = pl.ds(pl.multiple_of(start + first, 128), size)
            p = p_refs[j][first : first + size, :].astype(f32) * inverse
            ds = (p * (dot(kv_ref[span, :], ups[j][...]) - inner)).astype(bf16)
            acc_ref[span, :] += dot(jnp.concatenate([ds, p.astype(bf16)], 1), boths[j][...])
            part = dot(kt_ref[:, span], ds)
            dq = part if dq is None else dq + part
        dqs[j][...] = dq
        prepare(jnp.minimum(k + 1, blocks - 1), other)
        finish(jnp.maximum(k - 1, 0), other)

        @pl.when(k < blocks - 2)
        def _():
            copy(k + 2, j).start()

    by_two(blocks, step)
    finish(blocks - 1, 1)
    out_dq = pltpu.make_async_copy(dq_ref, out_hbm.at[:, pl.ds(0, 128), :], out_sems.at[0])
    out_dq.start()
    sub = lax.broadcasted_iota(jnp.int32, (1, 8, 128), 1)
    row = lax.broadcasted_iota(jnp.int32, (CAP, 128), 0)

    def give(b, carry):
        off = off_ref[b]
        shift = off & 7
        x = acc_ref[pl.ds(pl.multiple_of(off - shift + R, 8), 264), :].reshape(33, 8, 128)
        turned = pltpu.roll(x, (8 - shift) & 7, axis=1)
        x = jnp.where(sub + shift < 8, turned[:32], turned[1:]).reshape(CAP, 128)
        dkv_ref[b] = jnp.where(row < counts_ref[b], x, 0.0).astype(bf16)
        return carry

    some = BANDS // 4
    out_dkv = []
    for i in range(4):
        lax.fori_loop(i * some, (i + 1) * some, give, 0)
        bands = pl.ds(i * some, some)
        out_dkv.append(
            pltpu.make_async_copy(
                dkv_ref.at[bands], out_hbm.at[bands, pl.ds(128, CAP), :], out_sems.at[1 + i]
            )
        )
        out_dkv[-1].start()
    for out in [out_dq, *out_dkv]:
        out.wait()


def latent_kernel(
    d_ref, gain_ref, wq_hbm, wk_hbm, wv_hbm, lat_hbm, grad_hbm, out_ref,
    wq_ref, wk_ref, wv_ref, lat_ref, grad_ref, dq_ref, dk_ref, dv_ref, sems,
):
    wait = fetch(
        [(wq_hbm, wq_ref), (wk_hbm, wk_ref), (wv_hbm, wv_ref), (lat_hbm, lat_ref), (grad_hbm, grad_ref)],
        sems,
    )
    low = low_lanes(CAP)
    unfold_heads(parts(d_ref, 2), dq_ref)
    for pair in range(HEADS // 2):
        cols = slice(pair * 128, pair * 128 + 128)
        first = d_ref[2 * pair, 128:, :].astype(f32)
        second = d_ref[2 * pair + 1, 128:, :].astype(f32)
        dk_ref[:, cols] = jnp.where(low, first, swap(second)).astype(bf16)
        dv_ref[:, cols] = jnp.where(low, swap(first), second).astype(bf16)
    wait(1)
    normed = dot(dq_ref[...], wq_ref[...])
    wait(1)
    normed = normed + dot(dk_ref[...], wk_ref[...])
    wait(1)
    normed = normed + dot(dv_ref[...], wv_ref[...])
    wait(2)
    x = lat_ref[...].astype(f32)
    out = norm_backward(x, inverse_rms(x), normed * gain_ref[...])
    out_ref[...] = (grad_ref[...] + out).astype(bf16)


VMEM_MIB = dict(project=20, turn=20, forward=24, head=12, loss=20, share=8, total=8, latent=24)


def call(name, kernel, outs, scalars, arrays, held=(), held_out=(), scratch=(), sems=()):
    vmem = pl.BlockSpec(memory_space=pltpu.VMEM)
    smem = pl.BlockSpec(memory_space=pltpu.SMEM)
    hbm = pl.BlockSpec(memory_space=pltpu.HBM)
    return pl.pallas_call(
        kernel,
        out_shape=tuple(jax.ShapeDtypeStruct(s, d) for s, d in outs)
        + tuple(pltpu.HBM(s, d) for s, d in held_out),
        in_specs=[smem] * len(scalars) + [vmem] * len(arrays) + [hbm] * len(held),
        out_specs=(vmem,) * len(outs) + (hbm,) * len(held_out),
        scratch_shapes=[s if not isinstance(s, tuple) else pltpu.VMEM(*s) for s in scratch]
        + [pltpu.SemaphoreType.DMA((n,)) for n in sems],
        compiler_params=pltpu.CompilerParams(
            vmem_limit_bytes=VMEM_MIB[name] << 20 if name in VMEM_MIB else None
        ),
    )(*scalars, *arrays, *(pltpu.with_memory_space_constraint(a, pltpu.HBM) for a in held))


def exchange(x, axis):
    return lax.all_to_all(x, axis, split_axis=0, concat_axis=0, tiled=True)


def body(
    latent, observed, area_weight, counts, gain_attn, w_query, w_key, w_value, w_out, gain_head, w_head
):
    _, cap, width = latent.shape
    lat = latent.reshape(cap, width)
    gain_a = gain_attn.reshape(1, width)
    gain_h = gain_head.reshape(1, width)
    area = area_weight.reshape(2, 128)
    weight = ((width, width), bf16)
    offs = pltpu.SMEM((BANDS + 1,), jnp.int32)
    (x,) = call(
        "project",
        project_kernel,
        [((HEADS, 384, 128), bf16)],
        [],
        [gain_a],
        [lat, w_query, w_key, w_value],
        scratch=[((cap, width), bf16)] + [weight] * 3,
        sems=[4],
    )
    x, *weights = lax.optimization_barrier((x, w_head, w_out, w_query, w_key, w_value))
    turned = call(
        "turn",
        turn_kernel,
        [((CH, width), bf16), weight],
        [],
        [],
        weights,
        [weight] * 3,
        [((width, CH), bf16)] + [weight] * 5,
        [5],
    )
    x = exchange(x, "band")
    packed = ((BANDS, 128, 128), bf16)
    acc = ((ROWS, 128), f32)
    run = ((WIDTH, CAP), bf16)
    mixed, inverse, probs, kv, kt, q, own = call(
        "forward",
        forward_kernel,
        [packed, ((BANDS, CAP), f32)],
        [counts],
        [x],
        [],
        [((BANDS, WIDTH, CAP), bf16), ((ROWS, 128), bf16), ((HEAD, ROWS), bf16), packed, packed],
        [offs, ((ROWS, 128), bf16), ((ROWS, 128), bf16), ((TURNED, ROWS), bf16), acc]
        + [((256, CAP), bf16)] * 2
        + [run] * 2
        + [((TURNED - HEAD, CAP), f32)] * 2,
        [3, 2],
    )
    mixed = exchange(mixed, "band")
    predicted, hidden = call(
        "head",
        head_kernel,
        [((MEMBERS, cap, CH), bf16)],
        [],
        [mixed, w_out, gain_h, w_head],
        [lat],
        [((cap, width), f32)],
        [((cap, width), bf16)] * 2 + [((cap, width), f32)],
        sems=[1],
    )
    predicted = exchange(predicted, "member")
    g, sent, grad_hidden = call(
        "loss",
        loss_kernel,
        [packed, ((BANDS, HEAD_ROWS + 16, 128), bf16)],
        [counts],
        [predicted, area, observed, gain_h, turned[0], turned[1]],
        [hidden],
        [((cap, width), f32)],
        [((cap, width), f32)] * 2,
        [1],
    )
    g = exchange(g, "band")
    g, sent = lax.optimization_barrier((g, sent))
    sent = exchange(sent, "band")
    (d,) = call(
        "backward",
        backward_kernel,
        [],
        [counts],
        [inverse],
        [q, g, own, kv, kt, probs],
        [((BANDS, 384, 128), bf16)],
        [offs, packed, packed, packed, ((ROWS, 128), bf16), ((HEAD, ROWS), bf16), acc]
        + [packed, ((BANDS, CAP, 128), bf16)]
        + [((2 * CAP, 128), bf16)] * 2
        + [((128, CAP), bf16)] * 2
        + [((8, CAP), f32)] * 2
        + [run] * 2
        + [((HEAD, CAP), f32)] * 2,
        [5, 2, 5],
    )
    d, sent = lax.optimization_barrier((d, sent))
    d = exchange(d, "band")
    (share,) = call("share", share_kernel, [((HEAD_ROWS + 16, 128), bf16)], [], [sent])
    shared = [share]
    for k in range(1, MEMBERS):
        shared.append(lax.ppermute(share, "member", [(j, (j + k) % MEMBERS) for j in range(MEMBERS)]))
    me = lax.axis_index("member").astype(jnp.int32).reshape(1)
    grad_head, loss = call(
        "total",
        total_kernel,
        [((HEAD_ROWS, CH), f32), ((1, 1), f32)],
        [me],
        shared,
        scratch=[((MEMBERS, HEAD_ROWS + 16, 128), bf16)],
    )
    (grad_latent,) = call(
        "latent",
        latent_kernel,
        [((cap, width), bf16)],
        [],
        [d, gain_a],
        [turned[2], turned[3], turned[4], lat, grad_hidden],
        scratch=[weight] * 3
        + [((cap, width), bf16), ((cap, width), f32)]
        + [((cap, width), bf16)] * 3,
        sems=[5],
    )
    return grad_latent.reshape(latent.shape), grad_head, loss.reshape(())


def solution(mesh):
    rows = P("member", "band", None)
    placed = (rows, P("band", None), P("band")) + (P(),) * 8
    return jax.shard_map(
        body,
        mesh=mesh,
        in_specs=placed,
        out_specs=(rows, P("band", None), P()),
        check_vma=False,
    )
```

time: 212 us -> 161 us (0.76)
  waiting for transfers between devices: 61.9 us -> 14.6 us
  blocking collectives: 25.4 us -> 58.3 us
  local copies, waits for them, and re-layouts: 33.2 us -> 0.72 us
  starting transfers between devices: 31.9 us -> 24.1 us
  Pallas kernels: 57.4 us -> 62 us
    all_to_all x7 -> x3, waiting for transfers between devices: 61.9 us -> 12.3 us  [exchange(): return lax.all_to_all(x, axis, split_axis=0, concat_axis=0, tiled=True)]
    all_to_all x2 -> x3, blocking collectives: 25.4 us -> 58.3 us  [exchange(): return lax.all_to_all(x, axis, split_axis=0, concat_axis=0, tiled=True)]
    unnamed x82 -> x18, local copies, waits for them, and re-layouts: 33.2 us -> 0.72 us
    all_to_all x7 -> x3, starting transfers between devices: 31.9 us -> 16.1 us  [exchange(): return lax.all_to_all(x, axis, split_axis=0, concat_axis=0, tiled=True)]
    ppermute x0 -> x7, starting transfers between devices: none -> 8.02 us  [body(): lax.ppermute(share, 'member', [(j, (j + k) % MEMBERS) for j in range(MEMB...]
    pallas_call x12 -> x9, Pallas kernels: 57.4 us -> 62 us  [call(): pl.pallas_call(kernel, out_shape=tuple((jax.ShapeDtypeStruct(s, d) for s,...]
    ppermute x0 -> x7, waiting for transfers between devices: none -> 2.33 us  [body(): lax.ppermute(share, 'member', [(j, (j + k) % MEMBERS) for j in range(MEMB...]
  transfers between devices with their start and end apart: 7 -> 10, of which waited for: 6 -> 4; matrix products, arithmetic and copies ran while one was open for 0% -> 0% of each run, Pallas kernels for 17% -> 18%
where the time goes in v3:
time: 161 us
  Pallas kernels  62 us (39%)
  blocking collectives  58.3 us (36%)
  starting transfers between devices  24.1 us (15%)
  waiting for transfers between devices  14.6 us (9%)
    pallas_call x9, Pallas kernels, call(): pl.pallas_call(kernel, out_shape=tuple((jax.ShapeDtypeStruct(s, d) for s,...  62 us
    all_to_all x3, blocking collectives, exchange(): return lax.all_to_all(x, axis, split_axis=0, concat_axis=0, tiled=True)  58.3 us
    all_to_all x3, starting transfers between devices, exchange(): return lax.all_to_all(x, axis, split_axis=0, concat_axis=0, tiled=True)  16.1 us
    all_to_all x3, waiting for transfers between devices, exchange(): return lax.all_to_all(x, axis, split_axis=0, concat_axis=0, tiled=True)  12.3 us
    ppermute x7, starting transfers between devices, body(): lax.ppermute(share, 'member', [(j, (j + k) % MEMBERS) for j in range(MEMB...  8.02 us
  transfers between devices with their start and end apart: 10, of which 4 were waited for; matrix products, arithmetic and copies ran while one was open for 0% of the time, Pallas kernels for 18%

profile of v3, /device:TPU:0, one launch (start us, length us, event | category | flops | bytes accessed | tf_op | source)
XLA Modules:
  0.0 160.6 jit_solution(5885494761962995616)
XLA Ops:
  0.6 0.0 copy-start.4
  0.6 0.7 copy-done.4
  1.3 4.6 %shard_map.130 = bf16[16,384,128]{2,1,0:T(8,128)(2,1)S(1)} custom-call(f32[1,1024]{1,0:T(1,128)S(1)} %bitcast.7, bf16[256,1024]{1,0:T(8,128)(2,1)} %bitcast.12, bf16[1024,1024]{1,0:T(8,128)(2,1)} %refs_2_, bf16[1024,1024]{1,0:T(8,128)(2,1)} %refs_3_, bf16[1024,1024]{1,0:T(8,128)(2,1)} %refs_4_), custom_call_target="tpu_custom_call" | custom-call | tf_op jit(solution)/shard_map/pallas_call | solution.py:509
  5.9 0.0 copy-start.7
  5.9 29.5 %all_to_all.30.x_ref = bf16[16,384,128]{2,1,0:T(8,128)(2,1)S(1)} all-to-all(bf16[16,384,128]{2,1,0:T(8,128)(2,1)S(1)} %shard_map.130), channel_id=1, replica_groups=mesh['member'=8,'band'=16] {'band'}, dimensions={0} | all-to-all | bytes 3145728 | tf_op jit(solution)/shard_map/all_to_all | solution.py:524
  35.4 14.2 %shard_map.131 = (bf16[16,128,128]{2,1,0:T(8,128)(2,1)S(1)}, f32[16,256]{1,0:T(8,128)S(1)}, bf16[16,1408,256]{2,1,0:T(8,128)(2,1)}, bf16[5248,128]{1,0:T(8,128)(...) custom-call(s32[16]{0:T(128)S(1)} %copy-done.7, ...), custom_call_target="tpu_custom_call" | custom-call | tf_op jit(solution)/shard_map/pallas_call | solution.py:509
  49.7 0.0 copy-start.3
  49.7 14.0 %all_to_all.31.mixed_ref = bf16[16,128,128]{2,1,0:T(8,128)(2,1)S(1)} all-to-all(bf16[16,128,128]{2,1,0:T(8,128)(2,1)S(1)} %get-tuple-element.35), channel_id=1, replica_groups=mesh['member'=8,'band'=16] {'band'}, dimensions={0} | all-to-all | bytes 1048576 | tf_op jit(solution)/shard_map/all_to_all | solution.py:524
  63.7 3.8 %shard_map.132 = (bf16[8,256,128]{2,1,0:T(8,128)(2,1)}, f32[256,1024]{1,0:T(8,128)}) custom-call(bf16[16,128,128]{2,1,0:T(8,128)(2,1)S(1)} %all_to_all.31.mixed_ref, bf16[1024,1024]{1,0:T(8,128)(2,1)S(1)} %copy-done, f32[1,1024]{1,0:T(1,128)S(1)} %bitcast.9, bf16[1024,128]{1,0:T(8,128)(2,1)S(1)} %copy-done.1, bf16[256,1024]{1,0:T(8,128)(2,1)} %bitcast.13), custom_call_target="tpu_custom_call" | custom-call | tf_op jit(solution)/shard_map/pallas_call | solution.py:509
  67.6 5.3 %all-to-all-start.2 = ((bf16[8,256,128]{2,1,0:T(8,128)(2,1)}), bf16[8,256,128]{2,1,0:T(8,128)(2,1)S(1)}, u32[]{:S(2)}, u32[]{:S(2)}) async-start(bf16[8,256,128]{2,1,0:T(8,128)(2,1)} %get-tuple-element.36), calls=%async_computation.2 | async-start | bytes 1048576 | tf_op jit(solution)/shard_map/all_to_all | solution.py:524
  72.9 0.0 copy-start.8
  72.9 8.5 %shard_map.133 = (bf16[128,1024]{1,0:T(8,128)(2,1)S(1)}, bf16[1024,1024]{1,0:T(8,128)(2,1)S(1)}, bf16[1024,1024]{1,0:T(8,128)(2,1)}, bf16[1024,1024]{1,0:T(8,128)(2,1)}, bf16[1024,1024]{1,0:T(8,128)(2,1)}) custom-call(bf16[1024,128]{1,0:T(8,128)(2,1)} %refs_0_, bf16[1024,1024]{1,0:T(8,128)(2,1)} %refs_1_, bf16[1024,1024]{1,0:T(8,128)(2,1)} %refs_2_, ...), custom_call_target="tpu_custom_call" | custom-call | tf_op jit(solution)/shard_map/pallas_call | solution.py:509
  81.5 1.8 %all-to-all-done.2.pred_ref = bf16[8,256,128]{2,1,0:T(8,128)(2,1)S(1)} async-done(((bf16[8,256,128]{2,1,0:T(8,128)(2,1)}), bf16[8,256,128]{2,1,0:T(8,128)(2,1)S(1)}, u32[]{:S(2)}, u32[]{:S(2)}) %all-to-all-start.2) | async-done | bytes 524320 | tf_op jit(solution)/shard_map/all_to_all | solution.py:524
  83.2 4.2 %shard_map.134 = (bf16[16,128,128]{2,1,0:T(8,128)(2,1)S(1)}, bf16[16,80,128]{2,1,0:T(8,128)(2,1)}, f32[256,1024]{1,0:T(8,128)}) custom-call(s32[16]{0:T(128)S(1)} %copy-done.7, bf16[8,256,128]{2,1,0:T(8,128)(2,1)S(1)} %all-to-all-done.2.pred_ref, f32[2,128]{1,0:T(2,128)S(1)} %bitcast.11, bf16[256,128]{1,0:T(8,128)(2,1)S(1)} %copy-done.2, ...), custom_call_target="tpu_custom_call" | custom-call | tf_op jit(solution)/shard_map/pallas_call | solution.py:509
  87.4 14.7 %all_to_all.32.g_hbm = bf16[16,128,128]{2,1,0:T(8,128)(2,1)} all-to-all(bf16[16,128,128]{2,1,0:T(8,128)(2,1)S(1)} %get-tuple-element.45), channel_id=1, replica_groups=mesh['member'=8,'band'=16] {'band'}, dimensions={0} | all-to-all | bytes 1048576 | tf_op jit(solution)/shard_map/all_to_all | solution.py:524
  102.2 3.7 %all-to-all-start.4 = ((bf16[16,80,128]{2,1,0:T(8,128)(2,1)}), bf16[16,80,128]{2,1,0:T(8,128)(2,1)S(1)}, u32[]{:S(2)}, u32[]{:S(2)}) async-start(bf16[16,80,128]{2,1,0:T(8,128)(2,1)} %get-tuple-element.52), calls=%async_computation.4 | async-start | bytes 655360 | tf_op jit(solution)/shard_map/all_to_all | solution.py:524
  105.9 19.9 %shard_map.135 = bf16[16,384,128]{2,1,0:T(8,128)(2,1)} custom-call(s32[16]{0:T(128)} %counts_ref.5, f32[16,256]{1,0:T(8,128)} %copy-done.3, bf16[16,128,128]{2,1,0:T(8,128)(2,1)} %get-tuple-element.34.q_hbm, bf16[16,128,128]{2,1,0:T(8,128)(2,1)} %all_to_all.32.g_hbm, bf16[16,128,128]{2,1,0:T(8,128)(2,1)} %get-tuple-element.48.mixed_hbm, ...), custom_call_target="tpu_custom_call" | custom-call | tf_op jit(solution)/shard_map/pallas_call | solution.py:509
  125.8 0.0 copy-start.5
  125.9 0.0 all-to-all-done.4.sent_ref
  125.9 7.0 %all-to-all-start.5 = ((bf16[16,384,128]{2,1,0:T(8,128)(2,1)}), bf16[16,384,128]{2,1,0:T(8,128)(2,1)S(1)}, u32[]{:S(2)}, u32[]{:S(2)}) async-start(bf16[16,384,128]{2,1,0:T(8,128)(2,1)} %shard_map.135), calls=%async_computation.5 | async-start | bytes 3145728 | tf_op jit(solution)/shard_map/all_to_all | solution.py:524
  132.9 0.1 shard_map.137.refs_0_
  132.9 0.0 collective-permute-start
  133.0 0.9 collective-permute-start.1
  133.9 2.0 %collective-permute-start.2 = (bf16[80,128]{1,0:T(8,128)(2,1)S(1)}, bf16[80,128]{1,0:T(8,128)(2,1)S(1)}, u32[]{:S(2)}, u32[]{:S(2)}) collective-permute-start(bf16[80,128]{1,0:T(8,128)(2,1)S(1)} %shard_map.137.refs_0_), channel_id=1, source_target_pairs={{0,48},{16,64},{32,80},{48,96},{64,112},{80,0},{96,16},{112,32},{1... | collective-permute-start | bytes 61448 | tf_op jit(solution)/shard_map/ppermute | solution.py:626
  135.9 2.0 %collective-permute-start.3 = (bf16[80,128]{1,0:T(8,128)(2,1)S(1)}, bf16[80,128]{1,0:T(8,128)(2,1)S(1)}, u32[]{:S(2)}, u32[]{:S(2)}) collective-permute-start(bf16[80,128]{1,0:T(8,128)(2,1)S(1)} %shard_map.137.refs_0_), channel_id=1, source_target_pairs={{0,64},{16,80},{32,96},{48,112},{64,0},{80,16},{96,32},{112,48},{1... | collective-permute-start | bytes 61448 | tf_op jit(solution)/shard_map/ppermute | solution.py:626
  137.9 1.6 collective-permute-start.4
  139.5 1.4 collective-permute-start.5
  141.0 0.2 collective-permute-done.3.refs_4_
  141.2 2.1 %collective-permute-done.5.refs_6_ = bf16[80,128]{1,0:T(8,128)(2,1)S(1)} collective-permute-done((bf16[80,128]{1,0:T(8,128)(2,1)S(1)}, bf16[80,128]{1,0:T(8,128)(2,1)S(1)}, u32[]{:S(2)}, u32[]{:S(2)}) %collective-permute-start.5) | collective-permute-done | bytes 20512 | tf_op jit(solution)/shard_map/ppermute | solution.py:626
  143.3 0.7 shard_map.138
  144.0 10.5 %all-to-all-done.5.d_ref = bf16[16,384,128]{2,1,0:T(8,128)(2,1)S(1)} async-done(((bf16[16,384,128]{2,1,0:T(8,128)(2,1)}), bf16[16,384,128]{2,1,0:T(8,128)(2,1)S(1)}, u32[]{:S(2)}, u32[]{:S(2)}) %all-to-all-start.5) | async-done | bytes 1572896 | tf_op jit(solution)/shard_map/all_to_all | solution.py:524
  154.5 5.9 %shard_map.136 = bf16[256,1024]{1,0:T(8,128)(2,1)} custom-call(bf16[16,384,128]{2,1,0:T(8,128)(2,1)S(1)} %all-to-all-done.5.d_ref, f32[1,1024]{1,0:T(1,128)S(1)} %bitcast.8, bf16[1024,1024]{1,0:T(8,128)(2,1)} %get-tuple-element.54.wq_hbm, bf16[1024,1024]{1,0:T(8,128)(2,1)} %get-tuple-element.55.wk_hbm, bf16[1024,1024]{1,0:T(8,128)(2,1)} %get-tuple-element.56.wv_hbm, ...), custom_call_target="tpu_custom_call" | custom-call | tf_op jit(solution)/shard_map/pallas_call | solution.py:509
  (18 shorter events, 0.0 us)
Async XLA Ops:
  0.6 0.7 copy-start.4
  5.9 29.5 %copy-start.7 = (s32[16]{0:T(128)S(1)}, s32[16]{0:T(128)}, u32[]{:S(2)}) copy-start(s32[16]{0:T(128)} %counts_ref.5) | copy-start | bytes 196
  35.4 28.3 %copy-start = (bf16[1024,1024]{1,0:T(8,128)(2,1)S(1)}, bf16[1024,1024]{1,0:T(8,128)(2,1)}, u32[]{:S(2)}) copy-start(bf16[1024,1024]{1,0:T(8,128)(2,1)} %refs_1_) | copy-start | bytes 6291460
  35.4 28.3 %copy-start.1 = (bf16[1024,128]{1,0:T(8,128)(2,1)S(1)}, bf16[1024,128]{1,0:T(8,128)(2,1)}, u32[]{:S(2)}) copy-start(bf16[1024,128]{1,0:T(8,128)(2,1)} %refs_0_) | copy-start | bytes 786436
  35.4 28.3 %copy-start.6 = (f32[1024]{0:T(1024)S(1)}, f32[1024]{0:T(1024)}, u32[]{:S(2)}) copy-start(f32[1024]{0:T(1024)} %param.20) | copy-start | bytes 12292
  49.7 17.9 %copy-start.3 = (f32[16,256]{1,0:T(8,128)}, f32[16,256]{1,0:T(8,128)S(1)}, u32[]{:S(2)}) copy-start(f32[16,256]{1,0:T(8,128)S(1)} %get-tuple-element.33.inverse_ref) | copy-start | bytes 49156
  67.6 15.6 %all-to-all-start.2 = ((bf16[8,256,128]{2,1,0:T(8,128)(2,1)}), bf16[8,256,128]{2,1,0:T(8,128)(2,1)S(1)}, u32[]{:S(2)}, u32[]{:S(2)}) async-start(bf16[8,256,128]{2,1,0:T(8,128)(2,1)} %get-tuple-element.36), calls=%async_computation.2 | async-start | bytes 1048576 | tf_op jit(solution)/shard_map/all_to_all | solution.py:524
  72.9 10.3 %copy-start.2 = (bf16[256,128]{1,0:T(8,128)(2,1)S(1)}, bf16[256,128]{1,0:T(8,128)(2,1)}, u32[]{:S(2)}) copy-start(bf16[256,128]{1,0:T(8,128)(2,1)} %obs_ref.1) | copy-start | bytes 196612
  72.9 10.3 %copy-start.8 = (f32[256]{0:T(256)S(1)}, f32[256]{0:T(256)}, u32[]{:S(2)}) copy-start(f32[256]{0:T(256)} %param.13) | copy-start | bytes 3076
  102.2 23.7 %all-to-all-start.4 = ((bf16[16,80,128]{2,1,0:T(8,128)(2,1)}), bf16[16,80,128]{2,1,0:T(8,128)(2,1)S(1)}, u32[]{:S(2)}, u32[]{:S(2)}) async-start(bf16[16,80,128]{2,1,0:T(8,128)(2,1)} %get-tuple-element.52), calls=%async_computation.4 | async-start | bytes 655360 | tf_op jit(solution)/shard_map/all_to_all | solution.py:524
  125.8 28.7 %copy-start.5 = (f32[1024]{0:T(1024)S(1)}, f32[1024]{0:T(1024)}, u32[]{:S(2)}) copy-start(f32[1024]{0:T(1024)} %param.15) | copy-start | bytes 12292
  125.9 28.6 %all-to-all-start.5 = ((bf16[16,384,128]{2,1,0:T(8,128)(2,1)}), bf16[16,384,128]{2,1,0:T(8,128)(2,1)S(1)}, u32[]{:S(2)}, u32[]{:S(2)}) async-start(bf16[16,384,128]{2,1,0:T(8,128)(2,1)} %shard_map.135), calls=%async_computation.5 | async-start | bytes 3145728 | tf_op jit(solution)/shard_map/all_to_all | solution.py:524
  132.9 6.6 %collective-permute-start = (bf16[80,128]{1,0:T(8,128)(2,1)S(1)}, bf16[80,128]{1,0:T(8,128)(2,1)S(1)}, u32[]{:S(2)}, u32[]{:S(2)}) collective-permute-start(bf16[80,128]{1,0:T(8,128)(2,1)S(1)} %shard_map.137.refs_0_), channel_id=1, source_target_pairs={{0,16},{16,32},{32,48},{48,64},{64,80},{80,96},{96,112},{112,0},{1... | collective-permute-start | bytes 61448 | tf_op jit(solution)/shard_map/ppermute | solution.py:626
  133.0 8.0 %collective-permute-start.1 = (bf16[80,128]{1,0:T(8,128)(2,1)S(1)}, bf16[80,128]{1,0:T(8,128)(2,1)S(1)}, u32[]{:S(2)}, u32[]{:S(2)}) collective-permute-start(bf16[80,128]{1,0:T(8,128)(2,1)S(1)} %shard_map.137.refs_0_), channel_id=1, source_target_pairs={{0,32},{16,48},{32,64},{48,80},{64,96},{80,112},{96,0},{112,16},{1... | collective-permute-start | bytes 61448 | tf_op jit(solution)/shard_map/ppermute | solution.py:626
  133.9 7.1 %collective-permute-start.2 = (bf16[80,128]{1,0:T(8,128)(2,1)S(1)}, bf16[80,128]{1,0:T(8,128)(2,1)S(1)}, u32[]{:S(2)}, u32[]{:S(2)}) collective-permute-start(bf16[80,128]{1,0:T(8,128)(2,1)S(1)} %shard_map.137.refs_0_), channel_id=1, source_target_pairs={{0,48},{16,64},{32,80},{48,96},{64,112},{80,0},{96,16},{112,32},{1... | collective-permute-start | bytes 61448 | tf_op jit(solution)/shard_map/ppermute | solution.py:626
  135.9 5.3 %collective-permute-start.3 = (bf16[80,128]{1,0:T(8,128)(2,1)S(1)}, bf16[80,128]{1,0:T(8,128)(2,1)S(1)}, u32[]{:S(2)}, u32[]{:S(2)}) collective-permute-start(bf16[80,128]{1,0:T(8,128)(2,1)S(1)} %shard_map.137.refs_0_), channel_id=1, source_target_pairs={{0,64},{16,80},{32,96},{48,112},{64,0},{80,16},{96,32},{112,48},{1... | collective-permute-start | bytes 61448 | tf_op jit(solution)/shard_map/ppermute | solution.py:626
  137.9 3.3 %collective-permute-start.4 = (bf16[80,128]{1,0:T(8,128)(2,1)S(1)}, bf16[80,128]{1,0:T(8,128)(2,1)S(1)}, u32[]{:S(2)}, u32[]{:S(2)}) collective-permute-start(bf16[80,128]{1,0:T(8,128)(2,1)S(1)} %shard_map.137.refs_0_), channel_id=1, source_target_pairs={{0,80},{16,96},{32,112},{48,0},{64,16},{80,32},{96,48},{112,64},{1... | collective-permute-start | bytes 61448 | tf_op jit(solution)/shard_map/ppermute | solution.py:626
  139.5 3.8 %collective-permute-start.5 = (bf16[80,128]{1,0:T(8,128)(2,1)S(1)}, bf16[80,128]{1,0:T(8,128)(2,1)S(1)}, u32[]{:S(2)}, u32[]{:S(2)}) collective-permute-start(bf16[80,128]{1,0:T(8,128)(2,1)S(1)} %shard_map.137.refs_0_), channel_id=1, source_target_pairs={{0,96},{16,112},{32,0},{48,16},{64,32},{80,48},{96,64},{112,80},{1... | collective-permute-start | bytes 61448 | tf_op jit(solution)/shard_map/ppermute | solution.py:626
  141.0 2.3 %collective-permute-start.6 = (bf16[80,128]{1,0:T(8,128)(2,1)S(1)}, bf16[80,128]{1,0:T(8,128)(2,1)S(1)}, u32[]{:S(2)}, u32[]{:S(2)}) collective-permute-start(bf16[80,128]{1,0:T(8,128)(2,1)S(1)} %shard_map.137.refs_0_), channel_id=1, source_target_pairs={{0,112},{16,0},{32,16},{48,32},{64,48},{80,64},{96,80},{112,96},{1... | collective-permute-start | bytes 61448 | tf_op jit(solution)/shard_map/ppermute | solution.py:626

commit v4 on v3

--- a/solution.py
+++ b/solution.py
@@ -26,6 +26,7 @@
 CHUNKS = ((0, 512), (512, 512), (1024, 384))
 TURNED = 144
 DEAD = -32768.0
+UNROLL = 4
 HEAD_ROWS = 64
 
 f32 = jnp.float32
@@ -94,10 +95,12 @@
 
 
 def project_kernel(
-    gain_ref, lat_hbm, wq_hbm, wk_hbm, wv_hbm, out_ref, lat_ref, wq_ref, wk_ref, wv_ref, sems
+    gain_hbm, lat_hbm, wq_hbm, wk_hbm, wv_hbm, out_ref, gain_ref, lat_ref, wq_ref, wk_ref, wv_ref, sems
 ):
-    wait = fetch([(lat_hbm, lat_ref), (wk_hbm, wk_ref), (wv_hbm, wv_ref), (wq_hbm, wq_ref)], sems)
-    wait(1)
+    wait = fetch(
+        [(gain_hbm, gain_ref), (lat_hbm, lat_ref), (wk_hbm, wk_ref), (wv_hbm, wv_ref), (wq_hbm, wq_ref)], sems
+    )
+    wait(2)
     x = lat_ref[...].astype(f32)
     normed = (x * inverse_rms(x) * gain_ref[...]).astype(bf16)
     low = low_lanes(CAP)
@@ -192,7 +195,7 @@
             tile = rows_ref[span, :]
             kv_ref[span, :] = tile.astype(bf16)
             side_ref[span, :] = jnp.where(lane < HEAD, bias, swap(tile)).astype(bf16)
-            kvt_ref[:128, span] = tile.T.astype(bf16)
+            kvt_ref[:128, span] = tile.astype(bf16).T
         else:
             kv_ref[span, :] = jnp.zeros((128, 128), bf16)
             side_ref[span, :] = bias.astype(bf16)
@@ -214,12 +217,12 @@
 
 
 def by_two(count, step):
-    def two(i, carry):
-        for j in range(2):
-            step(2 * i + j, j)
+    def some(i, carry):
+        for j in range(UNROLL):
+            step(UNROLL * i + j, j % 2)
         return carry
 
-    lax.fori_loop(0, count // 2, two, 0)
+    lax.fori_loop(0, count // UNROLL, some, 0)
 
 
 def forward_kernel(counts_ref, x_ref, *refs):
@@ -283,25 +286,32 @@
 
 
 def head_kernel(
-    mixed_ref, wo_ref, gain_ref, wh_ref, lat_hbm, pred_ref, hidden_hbm, rows_ref, lat_ref, hidden_ref, sems
+    mixed_ref, wo_ref, gain_ref, wh_ref, lat_hbm, hidden_hbm, pred_hbm,
+    rows_ref, lat_ref, hidden_ref, pred_ref, sems, hidden_sems, pred_sems,
 ):
     wait = fetch([(lat_hbm, lat_ref)], sems)
     unfold_heads(parts(mixed_ref, 2), rows_ref)
-    hidden = dot(rows_ref[...], wo_ref[...])
     wait(1)
-    hidden = hidden + lat_ref[...].astype(f32)
-    hidden_ref[...] = hidden
-    give = fetch([(hidden_ref, hidden_hbm)], sems)
+    gives = []
+    for i in range(4):
+        cols = pl.ds(i * 256, 256)
+        hidden_ref[:, cols] = lat_ref[:, cols].astype(f32) + dot(rows_ref[...], wo_ref[:, cols])
+        gives.append(
+            pltpu.make_async_copy(hidden_ref.at[:, cols], hidden_hbm.at[:, cols], hidden_sems.at[i])
+        )
+        gives[-1].start()
+    hidden = hidden_ref[...]
     head_in = (hidden * inverse_rms(hidden) * gain_ref[...]).astype(bf16)
-    predicted = dot(head_in, wh_ref[...]).astype(bf16)
-    for j in range(MEMBERS):
-        pred_ref[j] = predicted
-    give(1)
+    pred_ref[...] = dot(head_in, wh_ref[...]).astype(bf16)
+    out = fetch([(pred_ref, pred_hbm.at[j]) for j in range(MEMBERS)], pred_sems)
+    for give in gives:
+        give.wait()
+    out(MEMBERS)
 
 
 def loss_kernel(
     counts_ref, pred_ref, area_ref, obs_ref, gain_ref, wh_ref, wo_ref, hidden_hbm,
-    out_ref, sent_ref, grad_hbm, hidden_ref, grad_ref, sems,
+    grad_pred_ref, loss_ref, grad_hbm, out_hbm, hidden_ref, grad_ref, out_ref, sems, out_sems,
 ):
     wait = fetch([(hidden_hbm, hidden_ref)], sems)
     me, band = lax.axis_index("member"), lax.axis_index("band")
@@ -338,14 +348,24 @@
     grad_ref[...] = grad_hidden
     give = fetch([(grad_ref, grad_hbm)], sems)
     fold_heads(dot(grad_hidden.astype(bf16), wo_ref[...]), parts(out_ref, 2))
-
-    head_in = (hidden * inverse * gain).astype(bf16)
-    grad_head = dot_tn(head_in, grad_pred)
-    pieces = jnp.concatenate(list(split3(loss)) + [jnp.zeros((13, 128), f32)], 0).astype(bf16)
+    out = fetch([(out_ref, out_hbm)], out_sems)
+    grad_pred_ref[...] = grad_pred
+    loss_ref[...] = jnp.broadcast_to(loss, (8, 128))
+    give(1)
+    out(1)
+
+
+def grad_head_kernel(grad_pred_ref, loss_ref, gain_ref, hidden_hbm, sent_ref, hidden_ref, sems):
+    fetch([(hidden_hbm, hidden_ref)], sems)(1)
+    hidden = hidden_ref[...]
+    head_in = (hidden * inverse_rms(hidden) * gain_ref[...]).astype(bf16)
+    grad_head = dot_tn(head_in, grad_pred_ref[...])
+    pieces = jnp.concatenate(
+        list(split3(loss_ref[0:1, :])) + [jnp.zeros((13, 128), f32)], 0
+    ).astype(bf16)
     for b in range(BANDS):
         sent_ref[b, :HEAD_ROWS, :] = grad_head[b * HEAD_ROWS : (b + 1) * HEAD_ROWS].astype(bf16)
         sent_ref[b, HEAD_ROWS:, :] = pieces
-    give(1)
 
 
 def share_kernel(sent_ref, out_ref):
@@ -374,8 +394,8 @@
 
 
 def backward_kernel(
-    counts_ref, inverse_ref, q_hbm, g_hbm, mixed_hbm, kv_hbm, kt_hbm, p_hbm, out_hbm,
-    off_ref, q_ref, g_ref, mixed_ref, kv_ref, kt_ref, acc_ref, dq_ref, dkv_ref,
+    counts_ref, inverse_ref, q_ref, g_ref, kv_ref, kt_ref, mixed_hbm, p_hbm, out_hbm,
+    off_ref, mixed_ref, acc_ref, dq_ref, dkv_ref,
     both0, both1, up0, up1, inner0, inner1, p0, p1, dq0, dq1, sems, p_sems, out_sems,
 ):
     blocks = BANDS
@@ -384,16 +404,7 @@
     def copy(k, slot):
         return pltpu.make_async_copy(p_hbm.at[k], p_refs[slot], p_sems.at[slot])
 
-    wait = fetch(
-        [
-            (q_hbm, q_ref),
-            (g_hbm, g_ref),
-            (mixed_hbm, mixed_ref),
-            (kv_hbm, kv_ref),
-            (kt_hbm, kt_ref),
-        ],
-        sems,
-    )
+    wait = fetch([(mixed_hbm, mixed_ref)], sems)
     copy(0, 0).start()
     copy(1, 1).start()
     offsets(counts_ref, off_ref)
@@ -414,9 +425,8 @@
     def finish(k, slot):
         dq_ref[k] = refold((dqs[slot][...] * 0.125).T).astype(bf16)
 
-    wait(3)
+    wait(1)
     prepare(0, 0)
-    wait(2)
 
     def step(k, j):
         other = 1 - j
@@ -499,7 +509,7 @@
     out_ref[...] = (grad_ref[...] + out).astype(bf16)
 
 
-VMEM_MIB = dict(project=20, turn=20, forward=24, head=12, loss=20, share=8, total=8, latent=24)
+VMEM_MIB = dict(project=20, turn=20, forward=24, head=12, loss=20, share=8, total=8, latent=24, backward=24, grad_head=12)
 
 
 def call(name, kernel, outs, scalars, arrays, held=(), held_out=(), scratch=(), sems=()):
@@ -539,10 +549,10 @@
         project_kernel,
         [((HEADS, 384, 128), bf16)],
         [],
-        [gain_a],
-        [lat, w_query, w_key, w_value],
-        scratch=[((cap, width), bf16)] + [weight] * 3,
-        sems=[4],
+        [],
+        [gain_a, lat, w_query, w_key, w_value],
+        scratch=[((1, width), f32), ((cap, width), bf16)] + [weight] * 3,
+        sems=[5],
     )
     x, *weights = lax.optimization_barrier((x, w_head, w_out, w_query, w_key, w_value))
     turned = call(
@@ -575,28 +585,38 @@
         [3, 2],
     )
     mixed = exchange(mixed, "band")
-    predicted, hidden = call(
+    hidden, predicted = call(
         "head",
         head_kernel,
-        [((MEMBERS, cap, CH), bf16)],
+        [],
         [],
         [mixed, w_out, gain_h, w_head],
         [lat],
-        [((cap, width), f32)],
-        [((cap, width), bf16)] * 2 + [((cap, width), f32)],
-        sems=[1],
+        [((cap, width), f32), ((MEMBERS, cap, CH), bf16)],
+        [((cap, width), bf16)] * 2 + [((cap, width), f32), ((cap, CH), bf16)],
+        sems=[1, 4, MEMBERS],
     )
     predicted = exchange(predicted, "member")
-    g, sent, grad_hidden = call(
+    grad_pred, loss, grad_hidden, g = call(
         "loss",
         loss_kernel,
-        [packed, ((BANDS, HEAD_ROWS + 16, 128), bf16)],
+        [((cap, CH), bf16), ((8, 128), f32)],
         [counts],
         [predicted, area, observed, gain_h, turned[0], turned[1]],
         [hidden],
-        [((cap, width), f32)],
-        [((cap, width), f32)] * 2,
-        [1],
+        [((cap, width), f32), packed],
+        [((cap, width), f32)] * 2 + [packed],
+        [1, 1],
+    )
+    (sent,) = call(
+        "grad_head",
+        grad_head_kernel,
+        [((BANDS, HEAD_ROWS + 16, 128), bf16)],
+        [],
+        [grad_pred, loss, gain_h],
+        [hidden],
+        scratch=[((cap, width), f32)],
+        sems=[1],
     )
     g = exchange(g, "band")
     g, sent = lax.optimization_barrier((g, sent))
@@ -606,17 +626,16 @@
         backward_kernel,
         [],
         [counts],
-        [inverse],
-        [q, g, own, kv, kt, probs],
+        [inverse, q, g, kv, kt],
+        [own, probs],
         [((BANDS, 384, 128), bf16)],
-        [offs, packed, packed, packed, ((ROWS, 128), bf16), ((HEAD, ROWS), bf16), acc]
-        + [packed, ((BANDS, CAP, 128), bf16)]
+        [offs, packed, acc, packed, ((BANDS, CAP, 128), bf16)]
         + [((2 * CAP, 128), bf16)] * 2
         + [((128, CAP), bf16)] * 2
         + [((8, CAP), f32)] * 2
         + [run] * 2
         + [((HEAD, CAP), f32)] * 2,
-        [5, 2, 5],
+        [1, 2, 5],
     )
     d, sent = lax.optimization_barrier((d, sent))
     d = exchange(d, "band")

time: 161 us -> 160 us (level)
  blocking collectives: 58.3 us -> 43.5 us
  waiting for transfers between devices: 14.6 us -> 23.8 us
  starting transfers between devices: 24.1 us -> 27.8 us
    all_to_all x3 -> x2, blocking collectives: 58.3 us -> 43.5 us  [exchange(): return lax.all_to_all(x, axis, split_axis=0, concat_axis=0, tiled=True)]
    all_to_all x3 -> x4, waiting for transfers between devices: 12.3 us -> 21.5 us  [exchange(): return lax.all_to_all(x, axis, split_axis=0, concat_axis=0, tiled=True)]
    all_to_all x3 -> x4, starting transfers between devices: 16.1 us -> 19.8 us  [exchange(): return lax.all_to_all(x, axis, split_axis=0, concat_axis=0, tiled=True)]
    pallas_call x9 -> x10, Pallas kernels: 62 us -> 62.5 us  [call(): pl.pallas_call(kernel, out_shape=tuple((jax.ShapeDtypeStruct(s, d) for s,...]
  transfers between devices with their start and end apart: 10 -> 11, of which waited for: 4 -> 5; matrix products, arithmetic and copies ran while one was open for 0% -> 0% of each run, Pallas kernels for 18% -> 19%
where the time goes in v4:
time: 160 us; the launch traced here: 159 us
  Pallas kernels  62.5 us (39%)
  blocking collectives  43.5 us (27%)
  starting transfers between devices  27.8 us (17%)
  waiting for transfers between devices  23.8 us (15%)
    pallas_call x10, Pallas kernels, call(): pl.pallas_call(kernel, out_shape=tuple((jax.ShapeDtypeStruct(s, d) for s,...  62.5 us
    all_to_all x2, blocking collectives, exchange(): return lax.all_to_all(x, axis, split_axis=0, concat_axis=0, tiled=True)  43.5 us
    all_to_all x4, waiting for transfers between devices, exchange(): return lax.all_to_all(x, axis, split_axis=0, concat_axis=0, tiled=True)  21.5 us
    all_to_all x4, starting transfers between devices, exchange(): return lax.all_to_all(x, axis, split_axis=0, concat_axis=0, tiled=True)  19.8 us
    ppermute x7, starting transfers between devices, body(): lax.ppermute(share, 'member', [(j, (j + k) % MEMBERS) for j in range(MEMB...  8 us
  transfers between devices with their start and end apart: 11, of which 5 were waited for; matrix products, arithmetic and copies ran while one was open for 0% of the time, Pallas kernels for 19%

profile of v4, /device:TPU:0, one launch (start us, length us, event | category | flops | bytes accessed | tf_op | source)
XLA Modules:
  0.0 158.6 jit_solution(8571817333730196056)
XLA Ops:
  0.6 4.6 %shard_map.130 = bf16[16,384,128]{2,1,0:T(8,128)(2,1)S(1)} custom-call(f32[1,1024]{1,0:T(1,128)} %bitcast.10, bf16[256,1024]{1,0:T(8,128)(2,1)} %bitcast.13, bf16[1024,1024]{1,0:T(8,128)(2,1)} %refs_2_, bf16[1024,1024]{1,0:T(8,128)(2,1)} %refs_3_, bf16[1024,1024]{1,0:T(8,128)(2,1)} %refs_4_), custom_call_target="tpu_custom_call" | custom-call | tf_op jit(solution)/shard_map/pallas_call | solution.py:519
  5.2 0.0 copy-start.8
  5.3 29.5 %all_to_all.30.x_ref = bf16[16,384,128]{2,1,0:T(8,128)(2,1)S(1)} all-to-all(bf16[16,384,128]{2,1,0:T(8,128)(2,1)S(1)} %shard_map.130), channel_id=1, replica_groups=mesh['member'=8,'band'=16] {'band'}, dimensions={0} | all-to-all | bytes 3145728 | tf_op jit(solution)/shard_map/all_to_all | solution.py:534
  34.8 13.9 %shard_map.131 = (bf16[16,128,128]{2,1,0:T(8,128)(2,1)S(1)}, f32[16,256]{1,0:T(8,128)S(1)}, bf16[16,1408,256]{2,1,0:T(8,128)(2,1)}, bf16[5248,128]{1,0:T(8,128)(...) custom-call(s32[16]{0:T(128)S(1)} %copy-done.8, ...), custom_call_target="tpu_custom_call" | custom-call | tf_op jit(solution)/shard_map/pallas_call | solution.py:519
  48.7 14.0 %all_to_all.31.mixed_ref = bf16[16,128,128]{2,1,0:T(8,128)(2,1)S(1)} all-to-all(bf16[16,128,128]{2,1,0:T(8,128)(2,1)S(1)} %get-tuple-element.36), channel_id=1, replica_groups=mesh['member'=8,'band'=16] {'band'}, dimensions={0} | all-to-all | bytes 1048576 | tf_op jit(solution)/shard_map/all_to_all | solution.py:534
  62.7 3.2 %shard_map.132 = (f32[256,1024]{1,0:T(8,128)}, bf16[8,256,128]{2,1,0:T(8,128)(2,1)}) custom-call(bf16[16,128,128]{2,1,0:T(8,128)(2,1)S(1)} %all_to_all.31.mixed_ref, bf16[1024,1024]{1,0:T(8,128)(2,1)S(1)} %copy-done, f32[1,1024]{1,0:T(1,128)S(1)} %bitcast.7, bf16[1024,128]{1,0:T(8,128)(2,1)S(1)} %copy-done.2, bf16[256,1024]{1,0:T(8,128)(2,1)} %bitcast.14), custom_call_target="tpu_custom_call" | custom-call | tf_op jit(solution)/shard_map/pallas_call | solution.py:519
  65.9 5.3 %all-to-all-start.2 = ((bf16[8,256,128]{2,1,0:T(8,128)(2,1)}), bf16[8,256,128]{2,1,0:T(8,128)(2,1)S(1)}, u32[]{:S(2)}, u32[]{:S(2)}) async-start(bf16[8,256,128]{2,1,0:T(8,128)(2,1)} %get-tuple-element.37), calls=%async_computation.2 | async-start | bytes 1048576 | tf_op jit(solution)/shard_map/all_to_all | solution.py:534
  71.3 0.0 copy-start.9
  71.3 8.5 %shard_map.133 = (bf16[128,1024]{1,0:T(8,128)(2,1)S(1)}, bf16[1024,1024]{1,0:T(8,128)(2,1)S(1)}, bf16[1024,1024]{1,0:T(8,128)(2,1)}, bf16[1024,1024]{1,0:T(8,128)(2,1)}, bf16[1024,1024]{1,0:T(8,128)(2,1)}) custom-call(bf16[1024,128]{1,0:T(8,128)(2,1)} %refs_0_, bf16[1024,1024]{1,0:T(8,128)(2,1)} %refs_1_, bf16[1024,1024]{1,0:T(8,128)(2,1)} %refs_2_, ...), custom_call_target="tpu_custom_call" | custom-call | tf_op jit(solution)/shard_map/pallas_call | solution.py:519
  79.8 1.8 %all-to-all-done.2.pred_ref = bf16[8,256,128]{2,1,0:T(8,128)(2,1)S(1)} async-done(((bf16[8,256,128]{2,1,0:T(8,128)(2,1)}), bf16[8,256,128]{2,1,0:T(8,128)(2,1)S(1)}, u32[]{:S(2)}, u32[]{:S(2)}) %all-to-all-start.2) | async-done | bytes 524320 | tf_op jit(solution)/shard_map/all_to_all | solution.py:534
  81.6 4.1 %shard_map.134 = (bf16[256,128]{1,0:T(8,128)(2,1)S(1)}, f32[8,128]{1,0:T(8,128)S(1)}, f32[256,1024]{1,0:T(8,128)}, bf16[16,128,128]{2,1,0:T(8,128)(2,1)}) custom-call(s32[16]{0:T(128)S(1)} %copy-done.8, bf16[8,256,128]{2,1,0:T(8,128)(2,1)S(1)} %all-to-all-done.2.pred_ref, f32[2,128]{1,0:T(2,128)S(1)} %bitcast.12, bf16[256,128]{1,0:T(8,128)(2,1)S(1)} %copy-done.5, ...), custom_call_target="tpu_custom_call" | custom-call | tf_op jit(solution)/shard_map/pallas_call | solution.py:519
  85.7 0.0 copy-start.4
  85.7 3.7 %all-to-all-start.3 = ((bf16[16,128,128]{2,1,0:T(8,128)(2,1)}), bf16[16,128,128]{2,1,0:T(8,128)(2,1)S(1)}, u32[]{:S(2)}, u32[]{:S(2)}) async-start(bf16[16,128,128]{2,1,0:T(8,128)(2,1)} %get-tuple-element.46), calls=%async_computation.3 | async-start | bytes 1048576 | tf_op jit(solution)/shard_map/all_to_all | solution.py:534
  89.5 2.4 %shard_map.135 = bf16[16,80,128]{2,1,0:T(8,128)(2,1)} custom-call(bf16[256,128]{1,0:T(8,128)(2,1)S(1)} %get-tuple-element.47.grad_pred_ref, f32[8,128]{1,0:T(8,128)S(1)} %get-tuple-element.48.loss_ref, f32[1,1024]{1,0:T(1,128)S(1)} %bitcast.9, f32[256,1024]{1,0:T(8,128)} %get-tuple-element.45.hidden_hbm), custom_call_target="tpu_custom_call" | custom-call | tf_op jit(solution)/shard_map/pallas_call | solution.py:519
  91.9 9.0 %all-to-all-done.3.g_ref = bf16[16,128,128]{2,1,0:T(8,128)(2,1)S(1)} async-done(((bf16[16,128,128]{2,1,0:T(8,128)(2,1)}), bf16[16,128,128]{2,1,0:T(8,128)(2,1)S(1)}, u32[]{:S(2)}, u32[]{:S(2)}) %all-to-all-start.3) | async-done | bytes 524320 | tf_op jit(solution)/shard_map/all_to_all | solution.py:534
  100.9 3.7 %all-to-all-start.4 = ((bf16[16,80,128]{2,1,0:T(8,128)(2,1)}), bf16[16,80,128]{2,1,0:T(8,128)(2,1)S(1)}, u32[]{:S(2)}, u32[]{:S(2)}) async-start(bf16[16,80,128]{2,1,0:T(8,128)(2,1)} %shard_map.135), calls=%async_computation.4 | async-start | bytes 655360 | tf_op jit(solution)/shard_map/all_to_all | solution.py:534
  104.6 19.1 %shard_map.136 = bf16[16,384,128]{2,1,0:T(8,128)(2,1)} custom-call(s32[16]{0:T(128)S(1)} %copy-done.8, f32[16,256]{1,0:T(8,128)S(1)} %get-tuple-element.34.inverse_ref, bf16[16,128,128]{2,1,0:T(8,128)(2,1)S(1)} %copy-done.4, bf16[16,128,128]{2,1,0:T(8,128)(2,1)S(1)} %all-to-all-done.3.g_ref, bf16[5248,128]{1,0:T(8,128)(2,1)S(1)} %copy-done.1, ...), custom_call_target="tpu_custom_call" | custom-call | tf_op jit(solution)/shard_map/pallas_call | solution.py:519
  123.7 0.0 copy-start.7
  123.8 7.0 %all-to-all-start.5 = ((bf16[16,384,128]{2,1,0:T(8,128)(2,1)}), bf16[16,384,128]{2,1,0:T(8,128)(2,1)S(1)}, u32[]{:S(2)}, u32[]{:S(2)}) async-start(bf16[16,384,128]{2,1,0:T(8,128)(2,1)} %shard_map.136), calls=%async_computation.5 | async-start | bytes 3145728 | tf_op jit(solution)/shard_map/all_to_all | solution.py:534
  130.8 0.1 shard_map.138.refs_0_
  130.8 0.0 collective-permute-start
  130.8 0.9 collective-permute-start.1
  131.7 2.0 %collective-permute-start.2 = (bf16[80,128]{1,0:T(8,128)(2,1)S(1)}, bf16[80,128]{1,0:T(8,128)(2,1)S(1)}, u32[]{:S(2)}, u32[]{:S(2)}) collective-permute-start(bf16[80,128]{1,0:T(8,128)(2,1)S(1)} %shard_map.138.refs_0_), channel_id=1, source_target_pairs={{0,48},{16,64},{32,80},{48,96},{64,112},{80,0},{96,16},{112,32},{1... | collective-permute-start | bytes 61448 | tf_op jit(solution)/shard_map/ppermute | solution.py:645
  133.7 2.1 %collective-permute-start.3 = (bf16[80,128]{1,0:T(8,128)(2,1)S(1)}, bf16[80,128]{1,0:T(8,128)(2,1)S(1)}, u32[]{:S(2)}, u32[]{:S(2)}) collective-permute-start(bf16[80,128]{1,0:T(8,128)(2,1)S(1)} %shard_map.138.refs_0_), channel_id=1, source_target_pairs={{0,64},{16,80},{32,96},{48,112},{64,0},{80,16},{96,32},{112,48},{1... | collective-permute-start | bytes 61448 | tf_op jit(solution)/shard_map/ppermute | solution.py:645
  135.8 1.6 %collective-permute-start.4 = (bf16[80,128]{1,0:T(8,128)(2,1)S(1)}, bf16[80,128]{1,0:T(8,128)(2,1)S(1)}, u32[]{:S(2)}, u32[]{:S(2)}) collective-permute-start(bf16[80,128]{1,0:T(8,128)(2,1)S(1)} %shard_map.138.refs_0_), channel_id=1, source_target_pairs={{0,80},{16,96},{32,112},{48,0},{64,16},{80,32},{96,48},{112,64},{1... | collective-permute-start | bytes 61448 | tf_op jit(solution)/shard_map/ppermute | solution.py:645
  137.4 0.0 collective-permute-done.refs_1_
  137.4 1.5 collective-permute-start.5
  138.8 0.2 collective-permute-done.3.refs_4_
  139.0 2.1 %collective-permute-done.5.refs_6_ = bf16[80,128]{1,0:T(8,128)(2,1)S(1)} collective-permute-done((bf16[80,128]{1,0:T(8,128)(2,1)S(1)}, bf16[80,128]{1,0:T(8,128)(2,1)S(1)}, u32[]{:S(2)}, u32[]{:S(2)}) %collective-permute-start.5) | collective-permute-done | bytes 20512 | tf_op jit(solution)/shard_map/ppermute | solution.py:645
  141.1 0.7 shard_map.139
  141.8 10.7 %all-to-all-done.5.d_ref = bf16[16,384,128]{2,1,0:T(8,128)(2,1)S(1)} async-done(((bf16[16,384,128]{2,1,0:T(8,128)(2,1)}), bf16[16,384,128]{2,1,0:T(8,128)(2,1)S(1)}, u32[]{:S(2)}, u32[]{:S(2)}) %all-to-all-start.5) | async-done | bytes 1572896 | tf_op jit(solution)/shard_map/all_to_all | solution.py:534
  152.5 5.9 %shard_map.137 = bf16[256,1024]{1,0:T(8,128)(2,1)} custom-call(bf16[16,384,128]{2,1,0:T(8,128)(2,1)S(1)} %all-to-all-done.5.d_ref, f32[1,1024]{1,0:T(1,128)S(1)} %bitcast.11, bf16[1024,1024]{1,0:T(8,128)(2,1)} %get-tuple-element.56.wq_hbm, bf16[1024,1024]{1,0:T(8,128)(2,1)} %get-tuple-element.57.wk_hbm, bf16[1024,1024]{1,0:T(8,128)(2,1)} %get-tuple-element.58.wv_hbm, ...), custom_call_target="tpu_custom_call" | custom-call | tf_op jit(solution)/shard_map/pallas_call | solution.py:519
  (22 shorter events, 0.0 us)
Async XLA Ops:
  5.2 29.5 %copy-start.8 = (s32[16]{0:T(128)S(1)}, s32[16]{0:T(128)}, u32[]{:S(2)}) copy-start(s32[16]{0:T(128)} %counts_ref.5) | copy-start | bytes 196
  34.8 27.9 %copy-start = (bf16[1024,1024]{1,0:T(8,128)(2,1)S(1)}, bf16[1024,1024]{1,0:T(8,128)(2,1)}, u32[]{:S(2)}) copy-start(bf16[1024,1024]{1,0:T(8,128)(2,1)} %refs_1_) | copy-start | bytes 6291460
  34.8 27.9 %copy-start.2 = (bf16[1024,128]{1,0:T(8,128)(2,1)S(1)}, bf16[1024,128]{1,0:T(8,128)(2,1)}, u32[]{:S(2)}) copy-start(bf16[1024,128]{1,0:T(8,128)(2,1)} %refs_0_) | copy-start | bytes 786436
  34.8 27.9 %copy-start.6 = (f32[1024]{0:T(1024)S(1)}, f32[1024]{0:T(1024)}, u32[]{:S(2)}) copy-start(f32[1024]{0:T(1024)} %param.20) | copy-start | bytes 12292
  65.9 15.6 %all-to-all-start.2 = ((bf16[8,256,128]{2,1,0:T(8,128)(2,1)}), bf16[8,256,128]{2,1,0:T(8,128)(2,1)S(1)}, u32[]{:S(2)}, u32[]{:S(2)}) async-start(bf16[8,256,128]{2,1,0:T(8,128)(2,1)} %get-tuple-element.37), calls=%async_computation.2 | async-start | bytes 1048576 | tf_op jit(solution)/shard_map/all_to_all | solution.py:534
  71.3 10.3 %copy-start.5 = (bf16[256,128]{1,0:T(8,128)(2,1)S(1)}, bf16[256,128]{1,0:T(8,128)(2,1)}, u32[]{:S(2)}) copy-start(bf16[256,128]{1,0:T(8,128)(2,1)} %obs_ref.1) | copy-start | bytes 196612
  71.3 10.3 %copy-start.9 = (f32[256]{0:T(256)S(1)}, f32[256]{0:T(256)}, u32[]{:S(2)}) copy-start(f32[256]{0:T(256)} %param.13) | copy-start | bytes 3076
  85.7 18.9 %copy-start.1 = (bf16[5248,128]{1,0:T(8,128)(2,1)S(1)}, bf16[5248,128]{1,0:T(8,128)(2,1)}, u32[]{:S(2)}) copy-start(bf16[5248,128]{1,0:T(8,128)(2,1)} %get-tuple-element.50.kv_ref) | copy-start | bytes 4030468
  85.7 18.9 %copy-start.3 = (bf16[64,5248]{1,0:T(8,128)(2,1)S(1)}, bf16[64,5248]{1,0:T(8,128)(2,1)}, u32[]{:S(2)}) copy-start(bf16[64,5248]{1,0:T(8,128)(2,1)} %get-tuple-element.51.kt_ref) | copy-start | bytes 2015236
  85.7 18.9 %copy-start.4 = (bf16[16,128,128]{2,1,0:T(8,128)(2,1)S(1)}, bf16[16,128,128]{2,1,0:T(8,128)(2,1)}, u32[]{:S(2)}) copy-start(bf16[16,128,128]{2,1,0:T(8,128)(2,1)} %get-tuple-element.35.q_ref) | copy-start | bytes 1572868
  85.7 15.2 %all-to-all-start.3 = ((bf16[16,128,128]{2,1,0:T(8,128)(2,1)}), bf16[16,128,128]{2,1,0:T(8,128)(2,1)S(1)}, u32[]{:S(2)}, u32[]{:S(2)}) async-start(bf16[16,128,128]{2,1,0:T(8,128)(2,1)} %get-tuple-element.46), calls=%async_computation.3 | async-start | bytes 1048576 | tf_op jit(solution)/shard_map/all_to_all | solution.py:534
  100.9 22.9 %all-to-all-start.4 = ((bf16[16,80,128]{2,1,0:T(8,128)(2,1)}), bf16[16,80,128]{2,1,0:T(8,128)(2,1)S(1)}, u32[]{:S(2)}, u32[]{:S(2)}) async-start(bf16[16,80,128]{2,1,0:T(8,128)(2,1)} %shard_map.135), calls=%async_computation.4 | async-start | bytes 655360 | tf_op jit(solution)/shard_map/all_to_all | solution.py:534
  123.7 28.8 %copy-start.7 = (f32[1024]{0:T(1024)S(1)}, f32[1024]{0:T(1024)}, u32[]{:S(2)}) copy-start(f32[1024]{0:T(1024)} %param.15) | copy-start | bytes 12292
  123.8 28.8 %all-to-all-start.5 = ((bf16[16,384,128]{2,1,0:T(8,128)(2,1)}), bf16[16,384,128]{2,1,0:T(8,128)(2,1)S(1)}, u32[]{:S(2)}, u32[]{:S(2)}) async-start(bf16[16,384,128]{2,1,0:T(8,128)(2,1)} %shard_map.136), calls=%async_computation.5 | async-start | bytes 3145728 | tf_op jit(solution)/shard_map/all_to_all | solution.py:534
  130.8 6.5 %collective-permute-start = (bf16[80,128]{1,0:T(8,128)(2,1)S(1)}, bf16[80,128]{1,0:T(8,128)(2,1)S(1)}, u32[]{:S(2)}, u32[]{:S(2)}) collective-permute-start(bf16[80,128]{1,0:T(8,128)(2,1)S(1)} %shard_map.138.refs_0_), channel_id=1, source_target_pairs={{0,16},{16,32},{32,48},{48,64},{64,80},{80,96},{96,112},{112,0},{1... | collective-permute-start | bytes 61448 | tf_op jit(solution)/shard_map/ppermute | solution.py:645
  130.8 8.0 %collective-permute-start.1 = (bf16[80,128]{1,0:T(8,128)(2,1)S(1)}, bf16[80,128]{1,0:T(8,128)(2,1)S(1)}, u32[]{:S(2)}, u32[]{:S(2)}) collective-permute-start(bf16[80,128]{1,0:T(8,128)(2,1)S(1)} %shard_map.138.refs_0_), channel_id=1, source_target_pairs={{0,32},{16,48},{32,64},{48,80},{64,96},{80,112},{96,0},{112,16},{1... | collective-permute-start | bytes 61448 | tf_op jit(solution)/shard_map/ppermute | solution.py:645
  131.7 7.1 %collective-permute-start.2 = (bf16[80,128]{1,0:T(8,128)(2,1)S(1)}, bf16[80,128]{1,0:T(8,128)(2,1)S(1)}, u32[]{:S(2)}, u32[]{:S(2)}) collective-permute-start(bf16[80,128]{1,0:T(8,128)(2,1)S(1)} %shard_map.138.refs_0_), channel_id=1, source_target_pairs={{0,48},{16,64},{32,80},{48,96},{64,112},{80,0},{96,16},{112,32},{1... | collective-permute-start | bytes 61448 | tf_op jit(solution)/shard_map/ppermute | solution.py:645
  133.7 5.3 %collective-permute-start.3 = (bf16[80,128]{1,0:T(8,128)(2,1)S(1)}, bf16[80,128]{1,0:T(8,128)(2,1)S(1)}, u32[]{:S(2)}, u32[]{:S(2)}) collective-permute-start(bf16[80,128]{1,0:T(8,128)(2,1)S(1)} %shard_map.138.refs_0_), channel_id=1, source_target_pairs={{0,64},{16,80},{32,96},{48,112},{64,0},{80,16},{96,32},{112,48},{1... | collective-permute-start | bytes 61448 | tf_op jit(solution)/shard_map/ppermute | solution.py:645
  135.8 3.3 %collective-permute-start.4 = (bf16[80,128]{1,0:T(8,128)(2,1)S(1)}, bf16[80,128]{1,0:T(8,128)(2,1)S(1)}, u32[]{:S(2)}, u32[]{:S(2)}) collective-permute-start(bf16[80,128]{1,0:T(8,128)(2,1)S(1)} %shard_map.138.refs_0_), channel_id=1, source_target_pairs={{0,80},{16,96},{32,112},{48,0},{64,16},{80,32},{96,48},{112,64},{1... | collective-permute-start | bytes 61448 | tf_op jit(solution)/shard_map/ppermute | solution.py:645
  137.4 3.8 %collective-permute-start.5 = (bf16[80,128]{1,0:T(8,128)(2,1)S(1)}, bf16[80,128]{1,0:T(8,128)(2,1)S(1)}, u32[]{:S(2)}, u32[]{:S(2)}) collective-permute-start(bf16[80,128]{1,0:T(8,128)(2,1)S(1)} %shard_map.138.refs_0_), channel_id=1, source_target_pairs={{0,96},{16,112},{32,0},{48,16},{64,32},{80,48},{96,64},{112,80},{1... | collective-permute-start | bytes 61448 | tf_op jit(solution)/shard_map/ppermute | solution.py:645
  138.8 2.3 %collective-permute-start.6 = (bf16[80,128]{1,0:T(8,128)(2,1)S(1)}, bf16[80,128]{1,0:T(8,128)(2,1)S(1)}, u32[]{:S(2)}, u32[]{:S(2)}) collective-permute-start(bf16[80,128]{1,0:T(8,128)(2,1)S(1)} %shard_map.138.refs_0_), channel_id=1, source_target_pairs={{0,112},{16,0},{32,16},{48,32},{64,48},{80,64},{96,80},{112,96},{1... | collective-permute-start | bytes 61448 | tf_op jit(solution)/shard_map/ppermute | solution.py:645

commit v5 on v4

--- a/solution.py
+++ b/solution.py
@@ -24,9 +24,10 @@
 ROWS = BANDS * CAP - CAP + WIDTH
 EDGE = CAP + 128
 CHUNKS = ((0, 512), (512, 512), (1024, 384))
+BACK_CHUNKS = ((0, 768), (768, 640))
 TURNED = 144
 DEAD = -32768.0
-UNROLL = 4
+UNROLL = 2
 HEAD_ROWS = 64
 
 f32 = jnp.float32
@@ -169,7 +170,8 @@
 def compact(counts_ref, off_ref, x_ref, total, kv_ref, side_ref, kvt_ref, rows_ref):
     sub = lax.broadcasted_iota(jnp.int32, (1, 8, 128), 1)
     row = lax.broadcasted_iota(jnp.int32, (CAP, 128), 0)
-    rows_ref[...] = jnp.zeros((ROWS, 128), f32)
+    tail = R + BANDS * HALF
+    rows_ref[tail:, :] = jnp.zeros((ROWS - tail, 128), f32)
 
     def place(b, carry):
         off = off_ref[b]
@@ -229,12 +231,13 @@
     blocks = BANDS
     mixed_ref, inverse_ref, e_hbm, kv_hbm, kt_hbm, q_hbm, own_hbm = refs[:7]
     off_ref, kv_ref, side_ref, kvt_ref, rows_ref = refs[7:12]
-    qx0, qx1, e0, e1, out0, out1, sems, e_sems = refs[-8:]
+    qx0, qx1, e0, e1, out0, out1, sems, e_sems, q_sems, own_sems = refs[-10:]
     qx, e_refs, outs = (qx0, qx1), (e0, e1), (out0, out1)
     q_ref = x_ref.at[:, pl.ds(0, 128), :]
+    give_q = fetch([(q_ref, q_hbm)], q_sems)
     total = offsets(counts_ref, off_ref)
     compact(counts_ref, off_ref, x_ref, total, kv_ref, side_ref, kvt_ref, rows_ref)
-    give = fetch([(kv_ref, kv_hbm), (kvt_ref.at[pl.ds(0, HEAD), :], kt_hbm), (q_ref, q_hbm)], sems)
+    give = fetch([(kv_ref, kv_hbm), (kvt_ref.at[pl.ds(0, HEAD), :], kt_hbm)], sems)
     lane = lax.broadcasted_iota(jnp.int32, (CAP, 128), 1)
     low = lane < HEAD
     one = jnp.where(lane == 0, 1.0, 0.0)
@@ -254,10 +257,18 @@
         inverse_ref[pl.ds(k, 1), :] = inverse
         mixed_ref[k] = refold((out[:HEAD] * inverse).T).astype(bf16)
 
+    def own(half):
+        bands = pl.ds(half * (BANDS // 2), BANDS // 2)
+        return pltpu.make_async_copy(mixed_ref.at[bands], own_hbm.at[bands], own_sems.at[half])
+
     prepare(0, 0)
 
     def step(k, j):
         other = 1 - j
+
+        @pl.when(k == BANDS // 2 + 1)
+        def _():
+            own(0).start()
 
         @pl.when(k > 1)
         def _():
@@ -279,10 +290,13 @@
 
     by_two(blocks, step)
     finish(blocks - 1, 1)
-    give(3)
-    fetch([(mixed_ref, own_hbm)], sems)(1)
+    own(1).start()
+    give(2)
+    give_q(1)
     copy(blocks - 2, 0).wait()
     copy(blocks - 1, 1).wait()
+    own(0).wait()
+    own(1).wait()
 
 
 def head_kernel(
@@ -435,11 +449,11 @@
         inner = inners[j][0:1, :]
         inverse = inverse_ref[pl.ds(k, 1), :]
         dq = None
-        for first, size in CHUNKS:
+        for first, size in BACK_CHUNKS:
             span = pl.ds(pl.multiple_of(start + first, 128), size)
             p = p_refs[j][first : first + size, :].astype(f32) * inverse
             ds = (p * (dot(kv_ref[span, :], ups[j][...]) - inner)).astype(bf16)
-            acc_ref[span, :] += dot(jnp.concatenate([ds, p.astype(bf16)], 1), boths[j][...])
+            acc_ref[span, :] += dot(ds, boths[j][:CAP, :]) + dot(p.astype(bf16), boths[j][CAP:, :])
             part = dot(kt_ref[:, span], ds)
             dq = part if dq is None else dq + part
         dqs[j][...] = dq
@@ -582,7 +596,7 @@
         + [((256, CAP), bf16)] * 2
         + [run] * 2
         + [((TURNED - HEAD, CAP), f32)] * 2,
-        [3, 2],
+        [2, 2, 1, 2],
     )
     mixed = exchange(mixed, "band")
     hidden, predicted = call(

time: 160 us -> 159 us (level)
  no operation moved by 1% of the time
where the time goes in v5:
time: 159 us; the launch traced here: 158 us
  Pallas kernels  62.1 us (39%)
  blocking collectives  43.5 us (27%)
  starting transfers between devices  27.7 us (17%)
  waiting for transfers between devices  23.9 us (15%)
    pallas_call x10, Pallas kernels, call(): pl.pallas_call(kernel, out_shape=tuple((jax.ShapeDtypeStruct(s, d) for s,...  62.1 us
    all_to_all x2, blocking collectives, exchange(): return lax.all_to_all(x, axis, split_axis=0, concat_axis=0, tiled=True)  43.5 us
    all_to_all x4, waiting for transfers between devices, exchange(): return lax.all_to_all(x, axis, split_axis=0, concat_axis=0, tiled=True)  21.6 us
    all_to_all x4, starting transfers between devices, exchange(): return lax.all_to_all(x, axis, split_axis=0, concat_axis=0, tiled=True)  19.7 us
    ppermute x7, starting transfers between devices, body(): lax.ppermute(share, 'member', [(j, (j + k) % MEMBERS) for j in range(MEMB...  7.97 us
  transfers between devices with their start and end apart: 11, of which 5 were waited for; matrix products, arithmetic and copies ran while one was open for 0% of the time, Pallas kernels for 19%

profile of v5, /device:TPU:0, one launch (start us, length us, event | category | flops | bytes accessed | tf_op | source)
XLA Modules:
  0.0 158.3 jit_solution(113847448726978671)
XLA Ops:
  0.6 4.6 %shard_map.130 = bf16[16,384,128]{2,1,0:T(8,128)(2,1)S(1)} custom-call(f32[1,1024]{1,0:T(1,128)} %bitcast.10, bf16[256,1024]{1,0:T(8,128)(2,1)} %bitcast.13, bf16[1024,1024]{1,0:T(8,128)(2,1)} %refs_2_, bf16[1024,1024]{1,0:T(8,128)(2,1)} %refs_3_, bf16[1024,1024]{1,0:T(8,128)(2,1)} %refs_4_), custom_call_target="tpu_custom_call" | custom-call | tf_op jit(solution)/shard_map/pallas_call | solution.py:533
  5.2 0.0 copy-start.8
  5.3 29.5 %all_to_all.30.x_ref = bf16[16,384,128]{2,1,0:T(8,128)(2,1)S(1)} all-to-all(bf16[16,384,128]{2,1,0:T(8,128)(2,1)S(1)} %shard_map.130), channel_id=1, replica_groups=mesh['member'=8,'band'=16] {'band'}, dimensions={0} | all-to-all | bytes 3145728 | tf_op jit(solution)/shard_map/all_to_all | solution.py:548
  34.8 13.5 %shard_map.131 = (bf16[16,128,128]{2,1,0:T(8,128)(2,1)S(1)}, f32[16,256]{1,0:T(8,128)S(1)}, bf16[16,1408,256]{2,1,0:T(8,128)(2,1)}, bf16[5248,128]{1,0:T(8,128)(...) custom-call(s32[16]{0:T(128)S(1)} %copy-done.8, ...), custom_call_target="tpu_custom_call" | custom-call | tf_op jit(solution)/shard_map/pallas_call | solution.py:533
  48.3 14.0 %all_to_all.31.mixed_ref = bf16[16,128,128]{2,1,0:T(8,128)(2,1)S(1)} all-to-all(bf16[16,128,128]{2,1,0:T(8,128)(2,1)S(1)} %get-tuple-element.36), channel_id=1, replica_groups=mesh['member'=8,'band'=16] {'band'}, dimensions={0} | all-to-all | bytes 1048576 | tf_op jit(solution)/shard_map/all_to_all | solution.py:548
  62.3 3.2 %shard_map.132 = (f32[256,1024]{1,0:T(8,128)}, bf16[8,256,128]{2,1,0:T(8,128)(2,1)}) custom-call(bf16[16,128,128]{2,1,0:T(8,128)(2,1)S(1)} %all_to_all.31.mixed_ref, bf16[1024,1024]{1,0:T(8,128)(2,1)S(1)} %copy-done, f32[1,1024]{1,0:T(1,128)S(1)} %bitcast.7, bf16[1024,128]{1,0:T(8,128)(2,1)S(1)} %copy-done.2, bf16[256,1024]{1,0:T(8,128)(2,1)} %bitcast.14), custom_call_target="tpu_custom_call" | custom-call | tf_op jit(solution)/shard_map/pallas_call | solution.py:533
  65.6 5.3 %all-to-all-start.2 = ((bf16[8,256,128]{2,1,0:T(8,128)(2,1)}), bf16[8,256,128]{2,1,0:T(8,128)(2,1)S(1)}, u32[]{:S(2)}, u32[]{:S(2)}) async-start(bf16[8,256,128]{2,1,0:T(8,128)(2,1)} %get-tuple-element.37), calls=%async_computation.2 | async-start | bytes 1048576 | tf_op jit(solution)/shard_map/all_to_all | solution.py:548
  70.9 0.0 copy-start.9
  70.9 8.5 %shard_map.133 = (bf16[128,1024]{1,0:T(8,128)(2,1)S(1)}, bf16[1024,1024]{1,0:T(8,128)(2,1)S(1)}, bf16[1024,1024]{1,0:T(8,128)(2,1)}, bf16[1024,1024]{1,0:T(8,128)(2,1)}, bf16[1024,1024]{1,0:T(8,128)(2,1)}) custom-call(bf16[1024,128]{1,0:T(8,128)(2,1)} %refs_0_, bf16[1024,1024]{1,0:T(8,128)(2,1)} %refs_1_, bf16[1024,1024]{1,0:T(8,128)(2,1)} %refs_2_, ...), custom_call_target="tpu_custom_call" | custom-call | tf_op jit(solution)/shard_map/pallas_call | solution.py:533
  79.4 1.8 %all-to-all-done.2.pred_ref = bf16[8,256,128]{2,1,0:T(8,128)(2,1)S(1)} async-done(((bf16[8,256,128]{2,1,0:T(8,128)(2,1)}), bf16[8,256,128]{2,1,0:T(8,128)(2,1)S(1)}, u32[]{:S(2)}, u32[]{:S(2)}) %all-to-all-start.2) | async-done | bytes 524320 | tf_op jit(solution)/shard_map/all_to_all | solution.py:548
  81.2 4.1 %shard_map.134 = (bf16[256,128]{1,0:T(8,128)(2,1)S(1)}, f32[8,128]{1,0:T(8,128)S(1)}, f32[256,1024]{1,0:T(8,128)}, bf16[16,128,128]{2,1,0:T(8,128)(2,1)}) custom-call(s32[16]{0:T(128)S(1)} %copy-done.8, bf16[8,256,128]{2,1,0:T(8,128)(2,1)S(1)} %all-to-all-done.2.pred_ref, f32[2,128]{1,0:T(2,128)S(1)} %bitcast.12, bf16[256,128]{1,0:T(8,128)(2,1)S(1)} %copy-done.5, ...), custom_call_target="tpu_custom_call" | custom-call | tf_op jit(solution)/shard_map/pallas_call | solution.py:533
  85.3 0.0 copy-start.4
  85.4 3.7 %all-to-all-start.3 = ((bf16[16,128,128]{2,1,0:T(8,128)(2,1)}), bf16[16,128,128]{2,1,0:T(8,128)(2,1)S(1)}, u32[]{:S(2)}, u32[]{:S(2)}) async-start(bf16[16,128,128]{2,1,0:T(8,128)(2,1)} %get-tuple-element.46), calls=%async_computation.3 | async-start | bytes 1048576 | tf_op jit(solution)/shard_map/all_to_all | solution.py:548
  89.1 2.4 %shard_map.135 = bf16[16,80,128]{2,1,0:T(8,128)(2,1)} custom-call(bf16[256,128]{1,0:T(8,128)(2,1)S(1)} %get-tuple-element.47.grad_pred_ref, f32[8,128]{1,0:T(8,128)S(1)} %get-tuple-element.48.loss_ref, f32[1,1024]{1,0:T(1,128)S(1)} %bitcast.9, f32[256,1024]{1,0:T(8,128)} %get-tuple-element.45.hidden_hbm), custom_call_target="tpu_custom_call" | custom-call | tf_op jit(solution)/shard_map/pallas_call | solution.py:533
  91.5 9.0 %all-to-all-done.3.g_ref = bf16[16,128,128]{2,1,0:T(8,128)(2,1)S(1)} async-done(((bf16[16,128,128]{2,1,0:T(8,128)(2,1)}), bf16[16,128,128]{2,1,0:T(8,128)(2,1)S(1)}, u32[]{:S(2)}, u32[]{:S(2)}) %all-to-all-start.3) | async-done | bytes 524320 | tf_op jit(solution)/shard_map/all_to_all | solution.py:548
  100.5 3.7 %all-to-all-start.4 = ((bf16[16,80,128]{2,1,0:T(8,128)(2,1)}), bf16[16,80,128]{2,1,0:T(8,128)(2,1)S(1)}, u32[]{:S(2)}, u32[]{:S(2)}) async-start(bf16[16,80,128]{2,1,0:T(8,128)(2,1)} %shard_map.135), calls=%async_computation.4 | async-start | bytes 655360 | tf_op jit(solution)/shard_map/all_to_all | solution.py:548
  104.3 19.1 %shard_map.136 = bf16[16,384,128]{2,1,0:T(8,128)(2,1)} custom-call(s32[16]{0:T(128)S(1)} %copy-done.8, f32[16,256]{1,0:T(8,128)S(1)} %get-tuple-element.34.inverse_ref, bf16[16,128,128]{2,1,0:T(8,128)(2,1)S(1)} %copy-done.4, bf16[16,128,128]{2,1,0:T(8,128)(2,1)S(1)} %all-to-all-done.3.g_ref, bf16[5248,128]{1,0:T(8,128)(2,1)S(1)} %copy-done.1, ...), custom_call_target="tpu_custom_call" | custom-call | tf_op jit(solution)/shard_map/pallas_call | solution.py:533
  123.4 0.0 copy-start.7
  123.4 7.0 %all-to-all-start.5 = ((bf16[16,384,128]{2,1,0:T(8,128)(2,1)}), bf16[16,384,128]{2,1,0:T(8,128)(2,1)S(1)}, u32[]{:S(2)}, u32[]{:S(2)}) async-start(bf16[16,384,128]{2,1,0:T(8,128)(2,1)} %shard_map.136), calls=%async_computation.5 | async-start | bytes 3145728 | tf_op jit(solution)/shard_map/all_to_all | solution.py:548
  130.4 0.1 shard_map.138.refs_0_
  130.5 0.0 collective-permute-start
  130.5 0.9 collective-permute-start.1
  131.3 2.0 %collective-permute-start.2 = (bf16[80,128]{1,0:T(8,128)(2,1)S(1)}, bf16[80,128]{1,0:T(8,128)(2,1)S(1)}, u32[]{:S(2)}, u32[]{:S(2)}) collective-permute-start(bf16[80,128]{1,0:T(8,128)(2,1)S(1)} %shard_map.138.refs_0_), channel_id=1, source_target_pairs={{0,48},{16,64},{32,80},{48,96},{64,112},{80,0},{96,16},{112,32},{1... | collective-permute-start | bytes 61448 | tf_op jit(solution)/shard_map/ppermute | solution.py:659
  133.3 2.1 %collective-permute-start.3 = (bf16[80,128]{1,0:T(8,128)(2,1)S(1)}, bf16[80,128]{1,0:T(8,128)(2,1)S(1)}, u32[]{:S(2)}, u32[]{:S(2)}) collective-permute-start(bf16[80,128]{1,0:T(8,128)(2,1)S(1)} %shard_map.138.refs_0_), channel_id=1, source_target_pairs={{0,64},{16,80},{32,96},{48,112},{64,0},{80,16},{96,32},{112,48},{1... | collective-permute-start | bytes 61448 | tf_op jit(solution)/shard_map/ppermute | solution.py:659
  135.4 1.6 %collective-permute-start.4 = (bf16[80,128]{1,0:T(8,128)(2,1)S(1)}, bf16[80,128]{1,0:T(8,128)(2,1)S(1)}, u32[]{:S(2)}, u32[]{:S(2)}) collective-permute-start(bf16[80,128]{1,0:T(8,128)(2,1)S(1)} %shard_map.138.refs_0_), channel_id=1, source_target_pairs={{0,80},{16,96},{32,112},{48,0},{64,16},{80,32},{96,48},{112,64},{1... | collective-permute-start | bytes 61448 | tf_op jit(solution)/shard_map/ppermute | solution.py:659
  137.0 0.0 collective-permute-done.refs_1_
  137.0 1.5 collective-permute-start.5
  138.5 0.2 collective-permute-done.3.refs_4_
  138.7 2.1 %collective-permute-done.5.refs_6_ = bf16[80,128]{1,0:T(8,128)(2,1)S(1)} collective-permute-done((bf16[80,128]{1,0:T(8,128)(2,1)S(1)}, bf16[80,128]{1,0:T(8,128)(2,1)S(1)}, u32[]{:S(2)}, u32[]{:S(2)}) %collective-permute-start.5) | collective-permute-done | bytes 20512 | tf_op jit(solution)/shard_map/ppermute | solution.py:659
  140.8 0.7 shard_map.139
  141.4 10.7 %all-to-all-done.5.d_ref = bf16[16,384,128]{2,1,0:T(8,128)(2,1)S(1)} async-done(((bf16[16,384,128]{2,1,0:T(8,128)(2,1)}), bf16[16,384,128]{2,1,0:T(8,128)(2,1)S(1)}, u32[]{:S(2)}, u32[]{:S(2)}) %all-to-all-start.5) | async-done | bytes 1572896 | tf_op jit(solution)/shard_map/all_to_all | solution.py:548
  152.2 5.9 %shard_map.137 = bf16[256,1024]{1,0:T(8,128)(2,1)} custom-call(bf16[16,384,128]{2,1,0:T(8,128)(2,1)S(1)} %all-to-all-done.5.d_ref, f32[1,1024]{1,0:T(1,128)S(1)} %bitcast.11, bf16[1024,1024]{1,0:T(8,128)(2,1)} %get-tuple-element.56.wq_hbm, bf16[1024,1024]{1,0:T(8,128)(2,1)} %get-tuple-element.57.wk_hbm, bf16[1024,1024]{1,0:T(8,128)(2,1)} %get-tuple-element.58.wv_hbm, ...), custom_call_target="tpu_custom_call" | custom-call | tf_op jit(solution)/shard_map/pallas_call | solution.py:533
  (22 shorter events, 0.0 us)
Async XLA Ops:
  5.2 29.5 %copy-start.8 = (s32[16]{0:T(128)S(1)}, s32[16]{0:T(128)}, u32[]{:S(2)}) copy-start(s32[16]{0:T(128)} %counts_ref.5) | copy-start | bytes 196
  34.8 27.6 %copy-start = (bf16[1024,1024]{1,0:T(8,128)(2,1)S(1)}, bf16[1024,1024]{1,0:T(8,128)(2,1)}, u32[]{:S(2)}) copy-start(bf16[1024,1024]{1,0:T(8,128)(2,1)} %refs_1_) | copy-start | bytes 6291460
  34.8 27.6 %copy-start.2 = (bf16[1024,128]{1,0:T(8,128)(2,1)S(1)}, bf16[1024,128]{1,0:T(8,128)(2,1)}, u32[]{:S(2)}) copy-start(bf16[1024,128]{1,0:T(8,128)(2,1)} %refs_0_) | copy-start | bytes 786436
  34.8 27.6 %copy-start.6 = (f32[1024]{0:T(1024)S(1)}, f32[1024]{0:T(1024)}, u32[]{:S(2)}) copy-start(f32[1024]{0:T(1024)} %param.20) | copy-start | bytes 12292
  65.6 15.6 %all-to-all-start.2 = ((bf16[8,256,128]{2,1,0:T(8,128)(2,1)}), bf16[8,256,128]{2,1,0:T(8,128)(2,1)S(1)}, u32[]{:S(2)}, u32[]{:S(2)}) async-start(bf16[8,256,128]{2,1,0:T(8,128)(2,1)} %get-tuple-element.37), calls=%async_computation.2 | async-start | bytes 1048576 | tf_op jit(solution)/shard_map/all_to_all | solution.py:548
  70.9 10.3 %copy-start.5 = (bf16[256,128]{1,0:T(8,128)(2,1)S(1)}, bf16[256,128]{1,0:T(8,128)(2,1)}, u32[]{:S(2)}) copy-start(bf16[256,128]{1,0:T(8,128)(2,1)} %obs_ref.1) | copy-start | bytes 196612
  70.9 10.3 %copy-start.9 = (f32[256]{0:T(256)S(1)}, f32[256]{0:T(256)}, u32[]{:S(2)}) copy-start(f32[256]{0:T(256)} %param.13) | copy-start | bytes 3076
  85.3 18.9 %copy-start.1 = (bf16[5248,128]{1,0:T(8,128)(2,1)S(1)}, bf16[5248,128]{1,0:T(8,128)(2,1)}, u32[]{:S(2)}) copy-start(bf16[5248,128]{1,0:T(8,128)(2,1)} %get-tuple-element.50.kv_ref) | copy-start | bytes 4030468
  85.3 18.9 %copy-start.3 = (bf16[64,5248]{1,0:T(8,128)(2,1)S(1)}, bf16[64,5248]{1,0:T(8,128)(2,1)}, u32[]{:S(2)}) copy-start(bf16[64,5248]{1,0:T(8,128)(2,1)} %get-tuple-element.51.kt_ref) | copy-start | bytes 2015236
  85.3 18.9 %copy-start.4 = (bf16[16,128,128]{2,1,0:T(8,128)(2,1)S(1)}, bf16[16,128,128]{2,1,0:T(8,128)(2,1)}, u32[]{:S(2)}) copy-start(bf16[16,128,128]{2,1,0:T(8,128)(2,1)} %get-tuple-element.35.q_ref) | copy-start | bytes 1572868
  85.4 15.2 %all-to-all-start.3 = ((bf16[16,128,128]{2,1,0:T(8,128)(2,1)}), bf16[16,128,128]{2,1,0:T(8,128)(2,1)S(1)}, u32[]{:S(2)}, u32[]{:S(2)}) async-start(bf16[16,128,128]{2,1,0:T(8,128)(2,1)} %get-tuple-element.46), calls=%async_computation.3 | async-start | bytes 1048576 | tf_op jit(solution)/shard_map/all_to_all | solution.py:548
  100.5 22.9 %all-to-all-start.4 = ((bf16[16,80,128]{2,1,0:T(8,128)(2,1)}), bf16[16,80,128]{2,1,0:T(8,128)(2,1)S(1)}, u32[]{:S(2)}, u32[]{:S(2)}) async-start(bf16[16,80,128]{2,1,0:T(8,128)(2,1)} %shard_map.135), calls=%async_computation.4 | async-start | bytes 655360 | tf_op jit(solution)/shard_map/all_to_all | solution.py:548
  123.4 28.8 %copy-start.7 = (f32[1024]{0:T(1024)S(1)}, f32[1024]{0:T(1024)}, u32[]{:S(2)}) copy-start(f32[1024]{0:T(1024)} %param.15) | copy-start | bytes 12292
  123.4 28.8 %all-to-all-start.5 = ((bf16[16,384,128]{2,1,0:T(8,128)(2,1)}), bf16[16,384,128]{2,1,0:T(8,128)(2,1)S(1)}, u32[]{:S(2)}, u32[]{:S(2)}) async-start(bf16[16,384,128]{2,1,0:T(8,128)(2,1)} %shard_map.136), calls=%async_computation.5 | async-start | bytes 3145728 | tf_op jit(solution)/shard_map/all_to_all | solution.py:548
  130.5 6.5 %collective-permute-start = (bf16[80,128]{1,0:T(8,128)(2,1)S(1)}, bf16[80,128]{1,0:T(8,128)(2,1)S(1)}, u32[]{:S(2)}, u32[]{:S(2)}) collective-permute-start(bf16[80,128]{1,0:T(8,128)(2,1)S(1)} %shard_map.138.refs_0_), channel_id=1, source_target_pairs={{0,16},{16,32},{32,48},{48,64},{64,80},{80,96},{96,112},{112,0},{1... | collective-permute-start | bytes 61448 | tf_op jit(solution)/shard_map/ppermute | solution.py:659
  130.5 8.0 %collective-permute-start.1 = (bf16[80,128]{1,0:T(8,128)(2,1)S(1)}, bf16[80,128]{1,0:T(8,128)(2,1)S(1)}, u32[]{:S(2)}, u32[]{:S(2)}) collective-permute-start(bf16[80,128]{1,0:T(8,128)(2,1)S(1)} %shard_map.138.refs_0_), channel_id=1, source_target_pairs={{0,32},{16,48},{32,64},{48,80},{64,96},{80,112},{96,0},{112,16},{1... | collective-permute-start | bytes 61448 | tf_op jit(solution)/shard_map/ppermute | solution.py:659
  131.3 7.1 %collective-permute-start.2 = (bf16[80,128]{1,0:T(8,128)(2,1)S(1)}, bf16[80,128]{1,0:T(8,128)(2,1)S(1)}, u32[]{:S(2)}, u32[]{:S(2)}) collective-permute-start(bf16[80,128]{1,0:T(8,128)(2,1)S(1)} %shard_map.138.refs_0_), channel_id=1, source_target_pairs={{0,48},{16,64},{32,80},{48,96},{64,112},{80,0},{96,16},{112,32},{1... | collective-permute-start | bytes 61448 | tf_op jit(solution)/shard_map/ppermute | solution.py:659
  133.3 5.3 %collective-permute-start.3 = (bf16[80,128]{1,0:T(8,128)(2,1)S(1)}, bf16[80,128]{1,0:T(8,128)(2,1)S(1)}, u32[]{:S(2)}, u32[]{:S(2)}) collective-permute-start(bf16[80,128]{1,0:T(8,128)(2,1)S(1)} %shard_map.138.refs_0_), channel_id=1, source_target_pairs={{0,64},{16,80},{32,96},{48,112},{64,0},{80,16},{96,32},{112,48},{1... | collective-permute-start | bytes 61448 | tf_op jit(solution)/shard_map/ppermute | solution.py:659
  135.4 3.3 %collective-permute-start.4 = (bf16[80,128]{1,0:T(8,128)(2,1)S(1)}, bf16[80,128]{1,0:T(8,128)(2,1)S(1)}, u32[]{:S(2)}, u32[]{:S(2)}) collective-permute-start(bf16[80,128]{1,0:T(8,128)(2,1)S(1)} %shard_map.138.refs_0_), channel_id=1, source_target_pairs={{0,80},{16,96},{32,112},{48,0},{64,16},{80,32},{96,48},{112,64},{1... | collective-permute-start | bytes 61448 | tf_op jit(solution)/shard_map/ppermute | solution.py:659
  137.0 3.8 %collective-permute-start.5 = (bf16[80,128]{1,0:T(8,128)(2,1)S(1)}, bf16[80,128]{1,0:T(8,128)(2,1)S(1)}, u32[]{:S(2)}, u32[]{:S(2)}) collective-permute-start(bf16[80,128]{1,0:T(8,128)(2,1)S(1)} %shard_map.138.refs_0_), channel_id=1, source_target_pairs={{0,96},{16,112},{32,0},{48,16},{64,32},{80,48},{96,64},{112,80},{1... | collective-permute-start | bytes 61448 | tf_op jit(solution)/shard_map/ppermute | solution.py:659
  138.4 2.3 %collective-permute-start.6 = (bf16[80,128]{1,0:T(8,128)(2,1)S(1)}, bf16[80,128]{1,0:T(8,128)(2,1)S(1)}, u32[]{:S(2)}, u32[]{:S(2)}) collective-permute-start(bf16[80,128]{1,0:T(8,128)(2,1)S(1)} %shard_map.138.refs_0_), channel_id=1, source_target_pairs={{0,112},{16,0},{32,16},{48,32},{64,48},{80,64},{96,80},{112,96},{1... | collective-permute-start | bytes 61448 | tf_op jit(solution)/shard_map/ppermute | solution.py:659

commit v6 on v5

--- a/solution.py
+++ b/solution.py
@@ -24,10 +24,9 @@
 ROWS = BANDS * CAP - CAP + WIDTH
 EDGE = CAP + 128
 CHUNKS = ((0, 512), (512, 512), (1024, 384))
-BACK_CHUNKS = ((0, 768), (768, 640))
 TURNED = 144
 DEAD = -32768.0
-UNROLL = 2
+UNROLL = 4
 HEAD_ROWS = 64
 
 f32 = jnp.float32
@@ -449,11 +448,11 @@
         inner = inners[j][0:1, :]
         inverse = inverse_ref[pl.ds(k, 1), :]
         dq = None
-        for first, size in BACK_CHUNKS:
+        for first, size in CHUNKS:
             span = pl.ds(pl.multiple_of(start + first, 128), size)
             p = p_refs[j][first : first + size, :].astype(f32) * inverse
             ds = (p * (dot(kv_ref[span, :], ups[j][...]) - inner)).astype(bf16)
-            acc_ref[span, :] += dot(ds, boths[j][:CAP, :]) + dot(p.astype(bf16), boths[j][CAP:, :])
+            acc_ref[span, :] += dot(jnp.concatenate([ds, p.astype(bf16)], 1), boths[j][...])
             part = dot(kt_ref[:, span], ds)
             dq = part if dq is None else dq + part
         dqs[j][...] = dq

time: 159 us -> 159 us (level)
  no operation moved by 1% of the time
where the time goes in v6:
time: 159 us; the launch traced here: 158 us
  Pallas kernels  62.1 us (39%)
  blocking collectives  43.5 us (27%)
  starting transfers between devices  27.7 us (17%)
  waiting for transfers between devices  23.9 us (15%)
    pallas_call x10, Pallas kernels, call(): pl.pallas_call(kernel, out_shape=tuple((jax.ShapeDtypeStruct(s, d) for s,...  62.1 us
    all_to_all x2, blocking collectives, exchange(): return lax.all_to_all(x, axis, split_axis=0, concat_axis=0, tiled=True)  43.5 us
    all_to_all x4, waiting for transfers between devices, exchange(): return lax.all_to_all(x, axis, split_axis=0, concat_axis=0, tiled=True)  21.5 us
    all_to_all x4, starting transfers between devices, exchange(): return lax.all_to_all(x, axis, split_axis=0, concat_axis=0, tiled=True)  19.8 us
    ppermute x7, starting transfers between devices, body(): lax.ppermute(share, 'member', [(j, (j + k) % MEMBERS) for j in range(MEMB...  7.98 us
  transfers between devices with their start and end apart: 11, of which 5 were waited for; matrix products, arithmetic and copies ran while one was open for 0% of the time, Pallas kernels for 19%

profile of v6, /device:TPU:0, one launch (start us, length us, event | category | flops | bytes accessed | tf_op | source)
XLA Modules:
  0.0 158.3 jit_solution(15455618149208280840)
XLA Ops:
  0.6 4.6 %shard_map.130 = bf16[16,384,128]{2,1,0:T(8,128)(2,1)S(1)} custom-call(f32[1,1024]{1,0:T(1,128)} %bitcast.10, bf16[256,1024]{1,0:T(8,128)(2,1)} %bitcast.13, bf16[1024,1024]{1,0:T(8,128)(2,1)} %refs_2_, bf16[1024,1024]{1,0:T(8,128)(2,1)} %refs_3_, bf16[1024,1024]{1,0:T(8,128)(2,1)} %refs_4_), custom_call_target="tpu_custom_call" | custom-call | tf_op jit(solution)/shard_map/pallas_call | solution.py:532
  5.2 0.0 copy-start.8
  5.3 29.5 %all_to_all.30.x_ref = bf16[16,384,128]{2,1,0:T(8,128)(2,1)S(1)} all-to-all(bf16[16,384,128]{2,1,0:T(8,128)(2,1)S(1)} %shard_map.130), channel_id=1, replica_groups=mesh['member'=8,'band'=16] {'band'}, dimensions={0} | all-to-all | bytes 3145728 | tf_op jit(solution)/shard_map/all_to_all | solution.py:547
  34.8 13.5 %shard_map.131 = (bf16[16,128,128]{2,1,0:T(8,128)(2,1)S(1)}, f32[16,256]{1,0:T(8,128)S(1)}, bf16[16,1408,256]{2,1,0:T(8,128)(2,1)}, bf16[5248,128]{1,0:T(8,128)(...) custom-call(s32[16]{0:T(128)S(1)} %copy-done.8, ...), custom_call_target="tpu_custom_call" | custom-call | tf_op jit(solution)/shard_map/pallas_call | solution.py:532
  48.3 14.0 %all_to_all.31.mixed_ref = bf16[16,128,128]{2,1,0:T(8,128)(2,1)S(1)} all-to-all(bf16[16,128,128]{2,1,0:T(8,128)(2,1)S(1)} %get-tuple-element.36), channel_id=1, replica_groups=mesh['member'=8,'band'=16] {'band'}, dimensions={0} | all-to-all | bytes 1048576 | tf_op jit(solution)/shard_map/all_to_all | solution.py:547
  62.3 3.2 %shard_map.132 = (f32[256,1024]{1,0:T(8,128)}, bf16[8,256,128]{2,1,0:T(8,128)(2,1)}) custom-call(bf16[16,128,128]{2,1,0:T(8,128)(2,1)S(1)} %all_to_all.31.mixed_ref, bf16[1024,1024]{1,0:T(8,128)(2,1)S(1)} %copy-done, f32[1,1024]{1,0:T(1,128)S(1)} %bitcast.7, bf16[1024,128]{1,0:T(8,128)(2,1)S(1)} %copy-done.2, bf16[256,1024]{1,0:T(8,128)(2,1)} %bitcast.14), custom_call_target="tpu_custom_call" | custom-call | tf_op jit(solution)/shard_map/pallas_call | solution.py:532
  65.6 5.3 %all-to-all-start.2 = ((bf16[8,256,128]{2,1,0:T(8,128)(2,1)}), bf16[8,256,128]{2,1,0:T(8,128)(2,1)S(1)}, u32[]{:S(2)}, u32[]{:S(2)}) async-start(bf16[8,256,128]{2,1,0:T(8,128)(2,1)} %get-tuple-element.37), calls=%async_computation.2 | async-start | bytes 1048576 | tf_op jit(solution)/shard_map/all_to_all | solution.py:547
  70.9 0.0 copy-start.9
  70.9 8.5 %shard_map.133 = (bf16[128,1024]{1,0:T(8,128)(2,1)S(1)}, bf16[1024,1024]{1,0:T(8,128)(2,1)S(1)}, bf16[1024,1024]{1,0:T(8,128)(2,1)}, bf16[1024,1024]{1,0:T(8,128)(2,1)}, bf16[1024,1024]{1,0:T(8,128)(2,1)}) custom-call(bf16[1024,128]{1,0:T(8,128)(2,1)} %refs_0_, bf16[1024,1024]{1,0:T(8,128)(2,1)} %refs_1_, bf16[1024,1024]{1,0:T(8,128)(2,1)} %refs_2_, ...), custom_call_target="tpu_custom_call" | custom-call | tf_op jit(solution)/shard_map/pallas_call | solution.py:532
  79.4 1.8 %all-to-all-done.2.pred_ref = bf16[8,256,128]{2,1,0:T(8,128)(2,1)S(1)} async-done(((bf16[8,256,128]{2,1,0:T(8,128)(2,1)}), bf16[8,256,128]{2,1,0:T(8,128)(2,1)S(1)}, u32[]{:S(2)}, u32[]{:S(2)}) %all-to-all-start.2) | async-done | bytes 524320 | tf_op jit(solution)/shard_map/all_to_all | solution.py:547
  81.2 4.1 %shard_map.134 = (bf16[256,128]{1,0:T(8,128)(2,1)S(1)}, f32[8,128]{1,0:T(8,128)S(1)}, f32[256,1024]{1,0:T(8,128)}, bf16[16,128,128]{2,1,0:T(8,128)(2,1)}) custom-call(s32[16]{0:T(128)S(1)} %copy-done.8, bf16[8,256,128]{2,1,0:T(8,128)(2,1)S(1)} %all-to-all-done.2.pred_ref, f32[2,128]{1,0:T(2,128)S(1)} %bitcast.12, bf16[256,128]{1,0:T(8,128)(2,1)S(1)} %copy-done.5, ...), custom_call_target="tpu_custom_call" | custom-call | tf_op jit(solution)/shard_map/pallas_call | solution.py:532
  85.4 0.0 copy-start.4
  85.4 3.7 %all-to-all-start.3 = ((bf16[16,128,128]{2,1,0:T(8,128)(2,1)}), bf16[16,128,128]{2,1,0:T(8,128)(2,1)S(1)}, u32[]{:S(2)}, u32[]{:S(2)}) async-start(bf16[16,128,128]{2,1,0:T(8,128)(2,1)} %get-tuple-element.46), calls=%async_computation.3 | async-start | bytes 1048576 | tf_op jit(solution)/shard_map/all_to_all | solution.py:547
  89.1 2.4 %shard_map.135 = bf16[16,80,128]{2,1,0:T(8,128)(2,1)} custom-call(bf16[256,128]{1,0:T(8,128)(2,1)S(1)} %get-tuple-element.47.grad_pred_ref, f32[8,128]{1,0:T(8,128)S(1)} %get-tuple-element.48.loss_ref, f32[1,1024]{1,0:T(1,128)S(1)} %bitcast.9, f32[256,1024]{1,0:T(8,128)} %get-tuple-element.45.hidden_hbm), custom_call_target="tpu_custom_call" | custom-call | tf_op jit(solution)/shard_map/pallas_call | solution.py:532
  91.5 9.0 %all-to-all-done.3.g_ref = bf16[16,128,128]{2,1,0:T(8,128)(2,1)S(1)} async-done(((bf16[16,128,128]{2,1,0:T(8,128)(2,1)}), bf16[16,128,128]{2,1,0:T(8,128)(2,1)S(1)}, u32[]{:S(2)}, u32[]{:S(2)}) %all-to-all-start.3) | async-done | bytes 524320 | tf_op jit(solution)/shard_map/all_to_all | solution.py:547
  100.5 3.7 %all-to-all-start.4 = ((bf16[16,80,128]{2,1,0:T(8,128)(2,1)}), bf16[16,80,128]{2,1,0:T(8,128)(2,1)S(1)}, u32[]{:S(2)}, u32[]{:S(2)}) async-start(bf16[16,80,128]{2,1,0:T(8,128)(2,1)} %shard_map.135), calls=%async_computation.4 | async-start | bytes 655360 | tf_op jit(solution)/shard_map/all_to_all | solution.py:547
  104.3 19.1 %shard_map.136 = bf16[16,384,128]{2,1,0:T(8,128)(2,1)} custom-call(s32[16]{0:T(128)S(1)} %copy-done.8, f32[16,256]{1,0:T(8,128)S(1)} %get-tuple-element.34.inverse_ref, bf16[16,128,128]{2,1,0:T(8,128)(2,1)S(1)} %copy-done.4, bf16[16,128,128]{2,1,0:T(8,128)(2,1)S(1)} %all-to-all-done.3.g_ref, bf16[5248,128]{1,0:T(8,128)(2,1)S(1)} %copy-done.1, ...), custom_call_target="tpu_custom_call" | custom-call | tf_op jit(solution)/shard_map/pallas_call | solution.py:532
  123.4 0.0 copy-start.7
  123.4 7.0 %all-to-all-start.5 = ((bf16[16,384,128]{2,1,0:T(8,128)(2,1)}), bf16[16,384,128]{2,1,0:T(8,128)(2,1)S(1)}, u32[]{:S(2)}, u32[]{:S(2)}) async-start(bf16[16,384,128]{2,1,0:T(8,128)(2,1)} %shard_map.136), calls=%async_computation.5 | async-start | bytes 3145728 | tf_op jit(solution)/shard_map/all_to_all | solution.py:547
  130.4 0.1 shard_map.138.refs_0_
  130.5 0.0 collective-permute-start
  130.5 0.9 collective-permute-start.1
  131.3 2.0 %collective-permute-start.2 = (bf16[80,128]{1,0:T(8,128)(2,1)S(1)}, bf16[80,128]{1,0:T(8,128)(2,1)S(1)}, u32[]{:S(2)}, u32[]{:S(2)}) collective-permute-start(bf16[80,128]{1,0:T(8,128)(2,1)S(1)} %shard_map.138.refs_0_), channel_id=1, source_target_pairs={{0,48},{16,64},{32,80},{48,96},{64,112},{80,0},{96,16},{112,32},{1... | collective-permute-start | bytes 61448 | tf_op jit(solution)/shard_map/ppermute | solution.py:658
  133.3 2.1 %collective-permute-start.3 = (bf16[80,128]{1,0:T(8,128)(2,1)S(1)}, bf16[80,128]{1,0:T(8,128)(2,1)S(1)}, u32[]{:S(2)}, u32[]{:S(2)}) collective-permute-start(bf16[80,128]{1,0:T(8,128)(2,1)S(1)} %shard_map.138.refs_0_), channel_id=1, source_target_pairs={{0,64},{16,80},{32,96},{48,112},{64,0},{80,16},{96,32},{112,48},{1... | collective-permute-start | bytes 61448 | tf_op jit(solution)/shard_map/ppermute | solution.py:658
  135.4 1.6 %collective-permute-start.4 = (bf16[80,128]{1,0:T(8,128)(2,1)S(1)}, bf16[80,128]{1,0:T(8,128)(2,1)S(1)}, u32[]{:S(2)}, u32[]{:S(2)}) collective-permute-start(bf16[80,128]{1,0:T(8,128)(2,1)S(1)} %shard_map.138.refs_0_), channel_id=1, source_target_pairs={{0,80},{16,96},{32,112},{48,0},{64,16},{80,32},{96,48},{112,64},{1... | collective-permute-start | bytes 61448 | tf_op jit(solution)/shard_map/ppermute | solution.py:658
  137.0 0.0 collective-permute-done.refs_1_
  137.0 1.5 collective-permute-start.5
  138.5 0.2 collective-permute-done.3.refs_4_
  138.7 2.1 %collective-permute-done.5.refs_6_ = bf16[80,128]{1,0:T(8,128)(2,1)S(1)} collective-permute-done((bf16[80,128]{1,0:T(8,128)(2,1)S(1)}, bf16[80,128]{1,0:T(8,128)(2,1)S(1)}, u32[]{:S(2)}, u32[]{:S(2)}) %collective-permute-start.5) | collective-permute-done | bytes 20512 | tf_op jit(solution)/shard_map/ppermute | solution.py:658
  140.8 0.7 shard_map.139
  141.5 10.7 %all-to-all-done.5.d_ref = bf16[16,384,128]{2,1,0:T(8,128)(2,1)S(1)} async-done(((bf16[16,384,128]{2,1,0:T(8,128)(2,1)}), bf16[16,384,128]{2,1,0:T(8,128)(2,1)S(1)}, u32[]{:S(2)}, u32[]{:S(2)}) %all-to-all-start.5) | async-done | bytes 1572896 | tf_op jit(solution)/shard_map/all_to_all | solution.py:547
  152.2 5.9 %shard_map.137 = bf16[256,1024]{1,0:T(8,128)(2,1)} custom-call(bf16[16,384,128]{2,1,0:T(8,128)(2,1)S(1)} %all-to-all-done.5.d_ref, f32[1,1024]{1,0:T(1,128)S(1)} %bitcast.11, bf16[1024,1024]{1,0:T(8,128)(2,1)} %get-tuple-element.56.wq_hbm, bf16[1024,1024]{1,0:T(8,128)(2,1)} %get-tuple-element.57.wk_hbm, bf16[1024,1024]{1,0:T(8,128)(2,1)} %get-tuple-element.58.wv_hbm, ...), custom_call_target="tpu_custom_call" | custom-call | tf_op jit(solution)/shard_map/pallas_call | solution.py:532
  (22 shorter events, 0.0 us)
Async XLA Ops:
  5.2 29.5 %copy-start.8 = (s32[16]{0:T(128)S(1)}, s32[16]{0:T(128)}, u32[]{:S(2)}) copy-start(s32[16]{0:T(128)} %counts_ref.5) | copy-start | bytes 196
  34.8 27.6 %copy-start = (bf16[1024,1024]{1,0:T(8,128)(2,1)S(1)}, bf16[1024,1024]{1,0:T(8,128)(2,1)}, u32[]{:S(2)}) copy-start(bf16[1024,1024]{1,0:T(8,128)(2,1)} %refs_1_) | copy-start | bytes 6291460
  34.8 27.6 %copy-start.2 = (bf16[1024,128]{1,0:T(8,128)(2,1)S(1)}, bf16[1024,128]{1,0:T(8,128)(2,1)}, u32[]{:S(2)}) copy-start(bf16[1024,128]{1,0:T(8,128)(2,1)} %refs_0_) | copy-start | bytes 786436
  34.8 27.6 %copy-start.6 = (f32[1024]{0:T(1024)S(1)}, f32[1024]{0:T(1024)}, u32[]{:S(2)}) copy-start(f32[1024]{0:T(1024)} %param.20) | copy-start | bytes 12292
  65.6 15.6 %all-to-all-start.2 = ((bf16[8,256,128]{2,1,0:T(8,128)(2,1)}), bf16[8,256,128]{2,1,0:T(8,128)(2,1)S(1)}, u32[]{:S(2)}, u32[]{:S(2)}) async-start(bf16[8,256,128]{2,1,0:T(8,128)(2,1)} %get-tuple-element.37), calls=%async_computation.2 | async-start | bytes 1048576 | tf_op jit(solution)/shard_map/all_to_all | solution.py:547
  70.9 10.3 %copy-start.5 = (bf16[256,128]{1,0:T(8,128)(2,1)S(1)}, bf16[256,128]{1,0:T(8,128)(2,1)}, u32[]{:S(2)}) copy-start(bf16[256,128]{1,0:T(8,128)(2,1)} %obs_ref.1) | copy-start | bytes 196612
  70.9 10.3 %copy-start.9 = (f32[256]{0:T(256)S(1)}, f32[256]{0:T(256)}, u32[]{:S(2)}) copy-start(f32[256]{0:T(256)} %param.13) | copy-start | bytes 3076
  85.3 18.9 %copy-start.1 = (bf16[5248,128]{1,0:T(8,128)(2,1)S(1)}, bf16[5248,128]{1,0:T(8,128)(2,1)}, u32[]{:S(2)}) copy-start(bf16[5248,128]{1,0:T(8,128)(2,1)} %get-tuple-element.50.kv_ref) | copy-start | bytes 4030468
  85.3 18.9 %copy-start.3 = (bf16[64,5248]{1,0:T(8,128)(2,1)S(1)}, bf16[64,5248]{1,0:T(8,128)(2,1)}, u32[]{:S(2)}) copy-start(bf16[64,5248]{1,0:T(8,128)(2,1)} %get-tuple-element.51.kt_ref) | copy-start | bytes 2015236
  85.4 18.9 %copy-start.4 = (bf16[16,128,128]{2,1,0:T(8,128)(2,1)S(1)}, bf16[16,128,128]{2,1,0:T(8,128)(2,1)}, u32[]{:S(2)}) copy-start(bf16[16,128,128]{2,1,0:T(8,128)(2,1)} %get-tuple-element.35.q_ref) | copy-start | bytes 1572868
  85.4 15.2 %all-to-all-start.3 = ((bf16[16,128,128]{2,1,0:T(8,128)(2,1)}), bf16[16,128,128]{2,1,0:T(8,128)(2,1)S(1)}, u32[]{:S(2)}, u32[]{:S(2)}) async-start(bf16[16,128,128]{2,1,0:T(8,128)(2,1)} %get-tuple-element.46), calls=%async_computation.3 | async-start | bytes 1048576 | tf_op jit(solution)/shard_map/all_to_all | solution.py:547
  100.5 22.9 %all-to-all-start.4 = ((bf16[16,80,128]{2,1,0:T(8,128)(2,1)}), bf16[16,80,128]{2,1,0:T(8,128)(2,1)S(1)}, u32[]{:S(2)}, u32[]{:S(2)}) async-start(bf16[16,80,128]{2,1,0:T(8,128)(2,1)} %shard_map.135), calls=%async_computation.4 | async-start | bytes 655360 | tf_op jit(solution)/shard_map/all_to_all | solution.py:547
  123.4 28.8 %copy-start.7 = (f32[1024]{0:T(1024)S(1)}, f32[1024]{0:T(1024)}, u32[]{:S(2)}) copy-start(f32[1024]{0:T(1024)} %param.15) | copy-start | bytes 12292
  123.4 28.8 %all-to-all-start.5 = ((bf16[16,384,128]{2,1,0:T(8,128)(2,1)}), bf16[16,384,128]{2,1,0:T(8,128)(2,1)S(1)}, u32[]{:S(2)}, u32[]{:S(2)}) async-start(bf16[16,384,128]{2,1,0:T(8,128)(2,1)} %shard_map.136), calls=%async_computation.5 | async-start | bytes 3145728 | tf_op jit(solution)/shard_map/all_to_all | solution.py:547
  130.5 6.5 %collective-permute-start = (bf16[80,128]{1,0:T(8,128)(2,1)S(1)}, bf16[80,128]{1,0:T(8,128)(2,1)S(1)}, u32[]{:S(2)}, u32[]{:S(2)}) collective-permute-start(bf16[80,128]{1,0:T(8,128)(2,1)S(1)} %shard_map.138.refs_0_), channel_id=1, source_target_pairs={{0,16},{16,32},{32,48},{48,64},{64,80},{80,96},{96,112},{112,0},{1... | collective-permute-start | bytes 61448 | tf_op jit(solution)/shard_map/ppermute | solution.py:658
  130.5 8.0 %collective-permute-start.1 = (bf16[80,128]{1,0:T(8,128)(2,1)S(1)}, bf16[80,128]{1,0:T(8,128)(2,1)S(1)}, u32[]{:S(2)}, u32[]{:S(2)}) collective-permute-start(bf16[80,128]{1,0:T(8,128)(2,1)S(1)} %shard_map.138.refs_0_), channel_id=1, source_target_pairs={{0,32},{16,48},{32,64},{48,80},{64,96},{80,112},{96,0},{112,16},{1... | collective-permute-start | bytes 61448 | tf_op jit(solution)/shard_map/ppermute | solution.py:658
  131.3 7.1 %collective-permute-start.2 = (bf16[80,128]{1,0:T(8,128)(2,1)S(1)}, bf16[80,128]{1,0:T(8,128)(2,1)S(1)}, u32[]{:S(2)}, u32[]{:S(2)}) collective-permute-start(bf16[80,128]{1,0:T(8,128)(2,1)S(1)} %shard_map.138.refs_0_), channel_id=1, source_target_pairs={{0,48},{16,64},{32,80},{48,96},{64,112},{80,0},{96,16},{112,32},{1... | collective-permute-start | bytes 61448 | tf_op jit(solution)/shard_map/ppermute | solution.py:658
  133.3 5.3 %collective-permute-start.3 = (bf16[80,128]{1,0:T(8,128)(2,1)S(1)}, bf16[80,128]{1,0:T(8,128)(2,1)S(1)}, u32[]{:S(2)}, u32[]{:S(2)}) collective-permute-start(bf16[80,128]{1,0:T(8,128)(2,1)S(1)} %shard_map.138.refs_0_), channel_id=1, source_target_pairs={{0,64},{16,80},{32,96},{48,112},{64,0},{80,16},{96,32},{112,48},{1... | collective-permute-start | bytes 61448 | tf_op jit(solution)/shard_map/ppermute | solution.py:658
  135.4 3.3 %collective-permute-start.4 = (bf16[80,128]{1,0:T(8,128)(2,1)S(1)}, bf16[80,128]{1,0:T(8,128)(2,1)S(1)}, u32[]{:S(2)}, u32[]{:S(2)}) collective-permute-start(bf16[80,128]{1,0:T(8,128)(2,1)S(1)} %shard_map.138.refs_0_), channel_id=1, source_target_pairs={{0,80},{16,96},{32,112},{48,0},{64,16},{80,32},{96,48},{112,64},{1... | collective-permute-start | bytes 61448 | tf_op jit(solution)/shard_map/ppermute | solution.py:658
  137.0 3.8 %collective-permute-start.5 = (bf16[80,128]{1,0:T(8,128)(2,1)S(1)}, bf16[80,128]{1,0:T(8,128)(2,1)S(1)}, u32[]{:S(2)}, u32[]{:S(2)}) collective-permute-start(bf16[80,128]{1,0:T(8,128)(2,1)S(1)} %shard_map.138.refs_0_), channel_id=1, source_target_pairs={{0,96},{16,112},{32,0},{48,16},{64,32},{80,48},{96,64},{112,80},{1... | collective-permute-start | bytes 61448 | tf_op jit(solution)/shard_map/ppermute | solution.py:658
  138.5 2.3 %collective-permute-start.6 = (bf16[80,128]{1,0:T(8,128)(2,1)S(1)}, bf16[80,128]{1,0:T(8,128)(2,1)S(1)}, u32[]{:S(2)}, u32[]{:S(2)}) collective-permute-start(bf16[80,128]{1,0:T(8,128)(2,1)S(1)} %shard_map.138.refs_0_), channel_id=1, source_target_pairs={{0,112},{16,0},{32,16},{48,32},{64,48},{80,64},{96,80},{112,96},{1... | collective-permute-start | bytes 61448 | tf_op jit(solution)/shard_map/ppermute | solution.py:658
